TPU v7x, 256 devices: a whole 4x4x8 slice. The times are simulated.
256 devices in a mesh: tm: 8 (over y_hi, x), stream: 32 (over y_lo, z, core).
Axes of the slice: x: 4, y: 4 (y_hi: 2, y_lo: 2; y = y_hi * 2 + y_lo), z: 8, core: 2. Of those that a mesh axis runs over, the one named last changes fastest.
Arguments:
- tokens: bfloat16 [32, 1024, 768], P('stream', 'tm'), may hold values from -6 to 6
- cotangent: bfloat16 [32, 1024, 768], P('stream', 'tm'), may hold values from -6 to 6
- decay: float32 [32, 1024, 24], P('stream', 'tm'), may hold values from 0.4 to 1, as said below
- in_w: bfloat16 [768, 3328], P('stream'), may hold values from -0.21875 to 0.21875
- out_w: bfloat16 [1536, 768], P('stream'), may hold values from -0.15625 to 0.15625
- conv_w: float32 [4, 1792], replicated, may hold values from -3 to 3
- dskip: float32 [24], replicated, may hold values from 0.5 to 2
- norm_w: float32 [1536], replicated, may hold values from 0.1 to 1.9
Outputs:
- out: bfloat16 [32, 1024, 768], P('stream', 'tm')
- grad_tokens: bfloat16 [32, 1024, 768], P('stream', 'tm')
- grad_out_t: float32 [768, 1536], P(('tm', 'stream'))
Inputs may be any that keep to these rules, and one draw needn't show every extreme that they name: decay lies strictly between 0 and 1.
All inputs are finite; a program needn't handle non-finite values.
Results may differ from a plain program's by a relative error of at most 0.015.
Values may be sent and summed in bfloat16 or wider, within the bound.
No kernel may reach another device: no remote copies, remote signals or barrier semaphores. Data moves between devices by JAX's collectives and lax.ppermute only.
A program may use at most 128 MiB of HBM per device.

v0:
```python
import functools

import jax
import jax.numpy as jnp
from jax import lax
from jax.experimental import pallas as pl
from jax.experimental.pallas import tpu as pltpu
from jax.sharding import PartitionSpec as P


bf16, f32 = jnp.bfloat16, jnp.float32
CHUNK = 128
LANES = 128
LIMIT = None
XS = 4
NN = (((1,), (0,)), ((), ()))
NT = (((1,), (1,)), ((), ()))
TN = (((0,), (0,)), ((), ()))


def dot(a, b, dims=NN):
    return lax.dot_general(a.astype(bf16), b.astype(bf16), dims, preferred_element_type=f32)


def exact(a, b, dims=NN):
    return lax.dot_general(
        a, b, dims, precision=lax.Precision.HIGHEST, preferred_element_type=f32
    )


def sig(v):
    return 0.5 + 0.5 * jnp.tanh(0.5 * v)


def kernel_call(body, outs, *args, scalars=None, scratch=(), flops=10**8, limit=None):
    spec = pl.BlockSpec(memory_space=pltpu.VMEM)
    size = sum(a.size * a.dtype.itemsize for a in args) + sum(
        o.size * o.dtype.itemsize for o in outs
    )
    first = [] if scalars is None else [scalars]
    return pl.pallas_call(
        body,
        out_shape=outs,
        in_specs=[pl.BlockSpec(memory_space=pltpu.SMEM)] * len(first) + [spec] * len(args),
        out_specs=[spec] * len(outs),
        scratch_shapes=list(scratch),
        compiler_params=pltpu.CompilerParams(vmem_limit_bytes=limit or LIMIT),
        cost_estimate=pl.CostEstimate(flops=flops, bytes_accessed=size, transcendentals=0),
    )(*first, *args)


def out(shape, dtype):
    return jax.ShapeDtypeStruct(shape, dtype)


def rows_of(c):
    return slice(c * CHUNK, (c + 1) * CHUNK)


def lanes_of(p):
    return slice(p * LANES, (p + 1) * LANES)


def halves():
    return lax.broadcasted_iota(jnp.int32, (CHUNK, LANES), 1) < LANES // 2


def causal():
    later = lax.broadcasted_iota(jnp.int32, (CHUNK, CHUNK), 0)
    return later >= lax.broadcasted_iota(jnp.int32, (CHUNK, CHUNK), 1)


def fades(cum_ref, cum_t_ref, c, head):
    column = cum_ref[rows_of(c), head * 64 : head * 64 + 1]
    row = cum_t_ref[c, head : head + 1, :]
    return jnp.where(causal(), jnp.exp(jnp.minimum(column - row, 0.0)), 0.0)


def prepare(at, logs, in_w, tokens, cotangent, wide, gate_w, aux, send1, send2, send3, decays):
    width = gate_w.shape[1]
    inner = XS * width
    start = pl.multiple_of(at[0] * width, width)
    for i in range(wide.shape[0]):
        wide[i, :, :width] = in_w[:, pl.ds(inner + start, width)]
        wide[i, :, width:] = in_w[:, 2 * inner :]
    gate_w[...] = in_w[:, pl.ds(start, width)]
    block = logs.shape[1]
    step = lax.broadcasted_iota(jnp.int32, (block, block), 0)
    upto = (step <= lax.broadcasted_iota(jnp.int32, (block, block), 1)).astype(f32)
    cum = exact(jnp.log(logs[...]), upto)
    high = cum.astype(bf16).astype(f32)
    rest = cum - high
    middle = rest.astype(bf16).astype(f32)
    low = rest - middle
    per = logs.shape[0] // XS
    rest_rows = jnp.zeros((5, block), f32)
    for j in range(XS):
        for i in range(per):
            h = j * per + i
            rows = [high[h : h + 1], middle[h : h + 1], low[h : h + 1], rest_rows]
            decays[j, :, i * block : (i + 1) * block] = jnp.concatenate(rows, axis=0)
    aux[...] = decays[at[0]].astype(bf16)
    for r, send in enumerate((send1, send2, send3)):
        send[:block, :] = tokens[...]
        send[block : 2 * block, :] = cotangent[...]
        send[2 * block :, :] = decays[lax.rem(at[0] + r + 1, XS)].astype(bf16)


def assemble(at, same, other, target, lanes):
    own_first = at[1] == 0
    for i in range(same.shape[0]):
        a, b = same[i, :, lanes], other[i, :, lanes]
        target[48 * i : 48 * i + 24, :] = jnp.where(own_first, a, b).astype(target.dtype)
        target[48 * i + 24 : 48 * i + 48, :] = jnp.where(own_first, b, a).astype(target.dtype)


def project(at, tokens, cotangent, aux, recv1, recv2, recv3, halo, same, other, conv_w,
            tok, cot, w_mix, cum, cum_t, pre, conv, states, last, mix):
    width = last.shape[1]
    chunks = XS
    block = CHUNK
    assemble(at, same, other, w_mix, slice(None))
    for r, source in enumerate((None, recv1, recv2, recv3)):
        c = lax.rem(at[0] + (XS - r), XS)
        here = pl.ds(pl.multiple_of(c * block, block), block)
        if source is None:
            t, k, extra = tokens[...], cotangent[...], aux[...].astype(f32)
        else:
            t, k = source[:block, :], source[block : 2 * block, :]
            extra = source[2 * block :, :].astype(f32)
        tok[here, :] = t
        cot[here, :] = k
        mix[pl.ds(pl.multiple_of(8 + c * block, 8), block), :] = (
            dot(t, w_mix[...]).astype(bf16).astype(f32)
        )
        total = extra[0:1] + extra[1:2] + extra[2:3]
        heads = [total[:, i * block : (i + 1) * block] for i in range(width // 64)]
        cum_t[c] = jnp.concatenate(heads + [jnp.zeros((8 - len(heads), block), f32)], axis=0)
    mix[:8, :] = dot(halo[...], w_mix[...]).astype(bf16).astype(f32)
    left = halves()
    state = jnp.zeros(last.shape, f32)
    for c in range(chunks):
        r = rows_of(c)
        square = jnp.concatenate([cum_t[c], jnp.zeros((block - 8, block), f32)], axis=0).T
        for p in range(width // LANES):
            cum[r, lanes_of(p)] = jnp.where(
                left, square[:, 2 * p : 2 * p + 1], square[:, 2 * p + 1 : 2 * p + 2]
            )
        for p in range(mix.shape[1] // LANES):
            s = lanes_of(p)
            value = jnp.zeros((CHUNK, LANES), f32)
            for k in range(4):
                start = 5 + k + c * CHUNK
                value = value + conv_w[k : k + 1, s] * mix[start : start + CHUNK, s]
            pre[r, s] = value
            conv[r, s] = (value * sig(value)).astype(bf16)
        states[c] = state
        end = cum[(c + 1) * CHUNK - 1 : (c + 1) * CHUNK, :]
        faded = jnp.exp(end - cum[r, :]) * conv[r, :width].astype(f32)
        state = jnp.exp(end) * state + dot(conv[r, width : width + 128], faded, TN)
    last[...] = state.astype(bf16)


def inside(conv, cum, cum_t, dskip, y):
    width = y.shape[1]
    left = halves()
    for c in range(y.shape[0] // CHUNK):
        r = rows_of(c)
        b, cv = conv[r, width : width + 128], conv[r, width + 128 : width + 256]
        scores = dot(cv, b, NT)
        for p in range(width // LANES):
            s = lanes_of(p)
            x = conv[r, s].astype(f32)
            weight = jnp.concatenate(
                [fades(cum, cum_t, c, 2 * p) * scores, fades(cum, cum_t, c, 2 * p + 1) * scores],
                axis=1,
            )
            both = jnp.concatenate([jnp.where(left, x, 0.0), jnp.where(left, 0.0, x)], axis=0)
            y[r, s] = dot(weight, both) + dskip[:, s] * x


def gated(at, conv, cum, states, entering, y_in, tok, cot, same, other, norm_w,
          y, full, gate, dn, part, stats, w_gate, raw, w_out):
    width = y.shape[1]
    chunks = y.shape[0] // CHUNK
    assemble(at, same, other, w_gate, slice(0, width))
    for p in range(width // LANES):
        assemble(at, same, other, raw.at[p], slice(width + p * LANES, width + (p + 1) * LANES))
        for k in range(2):
            lanes = slice(k * width + p * LANES, k * width + (p + 1) * LANES)
            w_out[:, lanes] = raw[p, pl.ds(k, width, stride=2), :].astype(bf16)
    carried = entering[...].astype(f32)
    ones = jnp.ones((8, LANES), f32)
    for c in range(chunks):
        r = rows_of(c)
        gate[r, :] = dot(tok[r, :], w_gate[...]).astype(bf16)
        dn[r, :] = dot(cot[r, :], w_out[...], NT) * norm_w[...]
        state = states[c] + carried
        full[c] = state.astype(bf16)
        carried = jnp.exp(cum[(c + 1) * CHUNK - 1 : (c + 1) * CHUNK, :]) * carried
        value = y_in[r, :] + jnp.exp(cum[r, :]) * dot(conv[r, width + 128 : width + 256], state)
        y[r, :] = value
        z = gate[r, :].astype(f32)
        g = value * z * sig(z)
        part[c] = dot(g * norm_w[...], w_out[...]).astype(bf16)
        squares, cross = g * g, g * dn[r, :]
        squares = sum(squares[:, lanes_of(p)] for p in range(width // LANES))
        cross = sum(cross[:, lanes_of(p)] for p in range(width // LANES))
        stats[0:1, r] = exact(ones, squares, NT)[0:1]
        stats[1:2, r] = exact(ones, cross, NT)[0:1]


def normed_part(inner, y, gate, dn, stats0, stats1, stats2, stats3, conv, cum, norm_w, cot, perm,
                factors, dgate, dy, ends, first, dw, low):
    width = y.shape[1]
    chunks = y.shape[0] // CHUNK
    adjoint = jnp.zeros(first.shape, f32)
    for c in reversed(range(chunks)):
        r = rows_of(c)
        sums = stats0[:, r] + stats1[:, r] + stats2[:, r] + stats3[:, r]
        sums = jnp.concatenate([sums, jnp.zeros((CHUNK - 2, CHUNK), f32)], axis=0).T
        factor = lax.rsqrt(sums[:, 0:1] * (1.0 / inner) + 1e-05)
        lean = factor * factor * sums[:, 1:2] * (1.0 / inner)
        factors[c] = jnp.broadcast_to(factor, (CHUNK, LANES))
        z = gate[r, :].astype(f32)
        q = sig(z)
        value = y[r, :]
        g = value * z * q
        low[r, :] = (g * factor * norm_w[...]).astype(bf16)
        dg = factor * (dn[r, :] - g * lean)
        dvalue = dg * z * q
        dy[r, :] = dvalue
        dgate[r, :] = (dg * value * q * (1.0 + z * (1.0 - q))).astype(bf16)
        ends[c] = adjoint
        end = cum[(c + 1) * CHUNK - 1 : (c + 1) * CHUNK, :]
        adjoint = jnp.exp(end) * adjoint + dot(
            conv[r, width + 128 : width + 256], jnp.exp(cum[r, :]) * dvalue, TN
        )
    first[...] = adjoint.astype(bf16)
    summed = dot(cot[...], low[...], TN)
    dw[...] = dot(perm[...], summed).astype(bf16)


def inside_back(conv, cum, cum_t, dskip, dy, full, ends, pre, dx, dbc, head):
    width = dy.shape[1]
    left = halves()
    for c in range(dy.shape[0] // CHUNK):
        r = rows_of(c)
        b, cv = conv[r, width : width + 128], conv[r, width + 128 : width + 256]
        scores = dot(cv, b, NT)
        dscores = jnp.zeros((CHUNK, CHUNK), f32)
        for p in range(width // LANES):
            s = lanes_of(p)
            x = conv[r, s]
            d = dy[r, s]
            da, db = jnp.where(left, d, 0.0), jnp.where(left, 0.0, d)
            fa, fb = fades(cum, cum_t, c, 2 * p), fades(cum, cum_t, c, 2 * p + 1)
            weight = jnp.concatenate([fa * scores, fb * scores], axis=0)
            dx[r, s] = dot(weight, jnp.concatenate([da, db], axis=0), TN) + dskip[:, s] * d
            dscores = dscores + fa * dot(da, x, NT) + fb * dot(db, x, NT)
        dbc[r, :128] = dot(dscores, cv, TN)
        dbc[r, 128:] = dot(dscores, b)
    first = conv_rows(conv, cum, full[0], ends[0], dy, dx, dbc, pre, 0, 16)
    for lanes, value in first:
        head[:, lanes] = value[:8]


def conv_rows(conv, cum, state, adjoint, dy, dx, dbc, pre, start, count):
    width = dy.shape[1]
    r = slice(start, start + count)
    chunk_end = start // CHUNK * CHUNK + CHUNK
    fade = jnp.exp(cum[chunk_end - 1 : chunk_end, :] - cum[r, :])
    grad_x = dx[r, :] + fade * dot(conv[r, width : width + 128], adjoint)
    grad_b = dbc[r, :128] + dot(fade * conv[r, :width].astype(f32), adjoint, NT)
    grad_c = dbc[r, 128:] + dot(jnp.exp(cum[r, :]) * dy[r, :], state, NT)
    result = []
    for lanes, grad in (
        (slice(0, width), grad_x),
        (slice(width, width + 128), grad_b),
        (slice(width + 128, width + 256), grad_c),
    ):
        v = pre[r, lanes]
        q = sig(v)
        result.append((lanes, grad * q * (1.0 + v * (1.0 - q))))
    return result


def conv_grad(at, conv, cum, full, ends, leaving, dy, dx, dbc, pre, parts, factors, gp, result):
    chunks = dy.shape[0] // CHUNK
    carried = leaving[...].astype(f32)
    for c in reversed(range(chunks)):
        adjoint = ends[c] + carried
        end = cum[(c + 1) * CHUNK - 1 : (c + 1) * CHUNK, :]
        carried = jnp.exp(end) * carried
        rows = conv_rows(conv, cum, full[c], adjoint, dy, dx, dbc, pre, c * CHUNK, CHUNK)
        for lanes, value in rows:
            gp[rows_of(c), lanes] = value
    factor = factors[at[0]]
    for p in range(result.shape[1] // LANES):
        s = lanes_of(p)
        total = sum(parts[k, :, s].astype(f32) for k in range(XS))
        result[:, s] = (total * factor).astype(bf16)


def token_grad(at, gp, after, conv_w, dgate, w_gate, w_mix, own, to1, to2, to3, long, low):
    rows = gp.shape[0]
    long[:rows, :] = gp[...]
    long[rows:, :] = after[...]
    for c in range(rows // CHUNK):
        for p in range(gp.shape[1] // LANES):
            s = lanes_of(p)
            value = jnp.zeros((CHUNK, LANES), f32)
            for k in range(4):
                start = c * CHUNK + 3 - k
                value = value + conv_w[k : k + 1, s] * long[start : start + CHUNK, s]
            low[rows_of(c), s] = value.astype(bf16)
    for r, target in enumerate((own, to1, to2, to3)):
        c = lax.rem(at[0] + r, XS)
        here = pl.ds(pl.multiple_of(c * CHUNK, CHUNK), CHUNK)
        target[...] = (
            dot(dgate[here, :], w_gate[...], NT) + dot(low[here, :], w_mix[...], NT)
        ).astype(bf16)


def shards(tokens, cotangent, decay, in_w, out_w, conv_w, dskip, norm_w):
    tm, stream = lax.axis_size("tm"), lax.axis_size("stream")
    me_t, me_s = lax.axis_index("tm"), lax.axis_index("stream")
    mine = lax.rem(me_t, XS)
    core = lax.rem(me_s, 2)
    heads = dskip.shape[0]
    inner = norm_w.shape[0]
    model = tokens.shape[2]
    state = (in_w.shape[1] - 2 * inner) // 2
    part_heads, width = heads // XS, inner // XS
    rows = XS * tokens.shape[1]
    x_groups = [[h * XS + i for i in range(XS)] for h in range(tm // XS)]
    up = [(i, i + XS) for i in range(XS)]
    down = [(i + XS, i) for i in range(XS)]

    def own(array, axis, size):
        return lax.dynamic_slice_in_dim(array, mine * size, size, axis)

    def along_x(array, steps):
        pairs = [(h * XS + i, h * XS + (i + steps) % XS) for h in range(tm // XS) for i in range(XS)]
        return lax.ppermute(array, "tm", pairs)

    def swap_x(array):
        return lax.all_to_all(array, "tm", 0, 0, axis_index_groups=x_groups)

    cores = [[i for i in range(stream) if i % 2 == c] for c in range(2)]
    half = stream // 2

    def gather_weights(wide):
        same = lax.all_to_all(wide, "stream", 0, 0, axis_index_groups=cores)
        return same, lax.ppermute(same, "stream", [(i, i ^ 1) for i in range(stream)])

    piece = 2 * out_w.shape[0] // XS
    routes = []
    for t in range(tm):
        for s in range(stream):
            group, place = divmod(s, stream // XS)
            target = (t // XS * XS + group, XS * place + t % XS)
            routes.append((t * stream + s, target[0] * stream + target[1]))
    out_piece = lax.ppermute(own(out_w.reshape(-1, width), 0, piece), ("tm", "stream"), routes)
    at = jnp.stack([mine, core]).astype(jnp.int32)
    block = tokens.shape[1]
    short = in_w.shape[0]
    mixed = width + 2 * state
    wide1, gate_w, aux_own, *sends = kernel_call(
        prepare,
        [out((half, short, mixed), bf16), out((short, width), bf16), out((8, model), bf16)]
        + [out((2 * block + 8, model), bf16)] * (XS - 1),
        decay[0].T, in_w, tokens[0], cotangent[0],
        scalars=at, scratch=[pltpu.VMEM((XS, 8, model), f32)],
    )
    recv = []
    for r in range(1, XS):
        recv.append(along_x(sends[r - 1], r))
    same1, other1 = gather_weights(wide1)
    tails = [piece[block - 8 : block] for piece in [tokens[0]] + recv]
    tail = lax.dynamic_index_in_dim(jnp.stack(tails), lax.rem(mine + 1, XS), 0, False)
    halo = lax.ppermute(tail, "tm", up)
    wide2 = jnp.concatenate([gate_w, out_piece], axis=1)
    wide2 = jnp.broadcast_to(wide2[None], (half,) + wide2.shape)
    wide2, same1 = lax.optimization_barrier((wide2, same1))
    same2, other2 = gather_weights(wide2)

    taps = jnp.concatenate([own(conv_w[:, :inner], 1, width), conv_w[:, inner:]], axis=1)
    gain = own(norm_w, 0, width)[None]
    skip = jnp.repeat(own(dskip, 0, part_heads), width // part_heads)[None]
    index = jnp.arange(model)
    source = index // 3 % tm * (3 * stream) + index // (3 * tm) * 3 + index % 3
    perm = (source[:, None] == index[None, :]).astype(bf16)

    chunks = rows // CHUNK
    tok, cot, w_mix, cum, cum_t, pre, conv, states, last = kernel_call(
        project,
        [out((rows, model), bf16), out((rows, model), bf16), out((model, mixed), bf16),
         out((rows, width), f32), out((chunks, 8, CHUNK), f32), out((rows, mixed), f32),
         out((rows, mixed), bf16), out((chunks, state, width), f32), out((state, width), bf16)],
        tokens[0], cotangent[0], aux_own, *recv, halo, same1, other1, taps,
        scalars=at,
        scratch=[pltpu.VMEM((rows + 8, mixed), f32)],
    )
    entering = lax.ppermute(last, "tm", up)
    (y_in,) = kernel_call(inside, [out((rows, width), f32)], conv, cum, cum_t, skip)
    y, full, gate, dn, part, stats, w_gate = kernel_call(
        gated,
        [out((rows, width), f32), out(states.shape, bf16), out((rows, width), bf16),
         out((rows, width), f32), out((XS, block, model), bf16), out((2, rows), f32),
         out((model, width), bf16)],
        conv, cum, states, entering, y_in, tok, cot, same2, other2, gain,
        scalars=at,
        scratch=[pltpu.VMEM((width // LANES, model, LANES), f32), pltpu.VMEM((width, model), bf16)],
    )
    others = []
    for r in range(1, XS):
        others.append(along_x(stats, r))
    parts = swap_x(part)
    factors, dgate, dy, ends, first, dw = kernel_call(
        functools.partial(normed_part, inner),
        [out((chunks, CHUNK, LANES), f32), out((rows, width), bf16), out((rows, width), f32),
         out(states.shape, f32), out((state, width), bf16), out((model, width), bf16)],
        y, gate, dn, stats, *others, conv, cum, gain, cot, perm,
        scratch=[pltpu.VMEM((rows, width), bf16)],
    )
    leaving = lax.ppermute(first, "tm", down)
    dx, dbc, head = kernel_call(
        inside_back,
        [out((rows, width), f32), out((rows, 2 * state), f32), out((8, mixed), f32)],
        conv, cum, cum_t, skip, dy, full, ends, pre,
    )
    after = lax.ppermute(head, "tm", down)
    pieces = lax.all_to_all(dw.reshape(stream, -1, width), "stream", 0, 0)
    gp, result = kernel_call(
        conv_grad,
        [out((rows, mixed), f32), out((block, model), bf16)],
        conv, cum, full, ends, leaving, dy, dx, dbc, pre, parts, factors,
        scalars=at,
    )
    token_parts = kernel_call(
        token_grad,
        [out((block, model), bf16)] * XS,
        gp, after, taps, dgate, w_gate, w_mix,
        scalars=at,
        scratch=[pltpu.VMEM((rows + 8, mixed), f32), pltpu.VMEM((rows, mixed), bf16)],
    )
    moved = []
    for r in range(1, XS):
        moved.append(along_x(token_parts[r], r))
    grad_tokens = sum((p.astype(f32) for p in moved), token_parts[0].astype(f32)).astype(bf16)
    summed = pieces.astype(f32).sum(axis=0).reshape(tm, 3, width)
    swapped = lax.all_to_all(summed, "tm", 0, 0)
    swapped = swapped.reshape(tm // XS, XS, 3, width).sum(axis=0)
    scale = (stream * tm * block) ** (-0.5)
    grad_out_t = jnp.transpose(swapped, (1, 0, 2)).reshape(3, inner) * scale
    return (result[None], grad_tokens[None], grad_out_t)


def solution(mesh):
    data = P("stream", "tm", None)
    in_specs = (data, data, data, P("stream", None), P("stream", None), P(), P(), P())
    out_specs = (data, data, P(("tm", "stream"), None))

    return jax.shard_map(shards, mesh=mesh, in_specs=in_specs, out_specs=out_specs, check_vma=False)
```

profile of v0, /device:TPU:32, one launch (start us, length us, event | category | flops | bytes accessed | tf_op | source)
XLA Modules:
  0.0 162.7 jit_solution(7173532887984318956)
XLA Ops:
  1.3 2.4 %shard_map.103 = (bf16[16,24,640]{2,1,0:T(8,128)(2,1)}, bf16[24,384]{1,0:T(8,128)(2,1)}, bf16[8,768]{1,0:T(8,128)(2,1)}, bf16[264,768]{1,0:T(8,128)(2,1)}, bf16[...) custom-call(s32[2]{0:T(128)} %pad_add_fusion.at, f32[24,128]{1,0:T(8,128)} %bitcast.30, bf16[24,3328]{1,0:T(8,128)(2,1)} %in_w.1, ...), custom_call_target="tpu_custom_call" | custom-call | flops 100000000 | bytes 2304000 | tf_op jit(solution)/shard_map/pallas_call | solution.py:41
  3.7 9.7 %all-to-all-start = ((bf16[16,24,640]{2,1,0:T(8,128)(2,1)}), bf16[16,24,640]{2,1,0:T(8,128)(2,1)S(1)}, u32[]{:S(2)}, u32[]{:S(2)}) async-start(bf16[16,24,640]{2,1,0:T(8,128)(2,1)} %get-tuple-element.47), calls=%async_computation | async-start | bytes 983040 | tf_op jit(solution)/shard_map/all_to_all | solution.py:354
  13.5 6.4 %collective-permute-start.4 = (bf16[24,384]{1,0:T(8,128)(2,1)S(1)}, bf16[24,384]{1,0:T(8,128)(2,1)S(1)}, u32[]{:S(2)}, u32[]{:S(2)}) collective-permute-start(bf16[24,384]{1,0:T(8,128)(2,1)S(1)} %constant_dynamic-slice_fusion.1), channel_id=1, source_target_pairs={{0,0},{1,4},{2,8},{3,12},{4,16},{5,20},{6,24},{7,28},{8,32},{9,36}... | collective-permute-start | bytes 55304 | tf_op jit(solution)/shard_map/ppermute | solution.py:364
  19.9 6.0 %collective-permute-done.4 = bf16[24,384]{1,0:T(8,128)(2,1)S(1)} collective-permute-done((bf16[24,384]{1,0:T(8,128)(2,1)S(1)}, bf16[24,384]{1,0:T(8,128)(2,1)S(1)}, u32[]{:S(2)}, u32[]{:S(2)}) %collective-permute-start.4) | collective-permute-done | bytes 18464 | tf_op jit(solution)/shard_map/ppermute | solution.py:364
  26.6 2.0 %all-to-all-done.same = bf16[16,24,640]{2,1,0:T(8,128)(2,1)S(1)} async-done(((bf16[16,24,640]{2,1,0:T(8,128)(2,1)}), bf16[16,24,640]{2,1,0:T(8,128)(2,1)S(1)}, u32[]{:S(2)}, u32[]{:S(2)}) %all-to-all-start) | async-done | bytes 491552 | tf_op jit(solution)/shard_map/all_to_all | solution.py:354
  29.5 7.3 %all-to-all-start.1 = ((bf16[16,24,768]{2,1,0:T(8,128)(2,1)}), bf16[16,24,768]{2,1,0:T(8,128)(2,1)S(1)}, u32[]{:S(2)}, u32[]{:S(2)}) async-start(bf16[16,24,768]{2,1,0:T(8,128)(2,1)} %broadcast_in_dim.20), calls=%async_computation.1 | async-start | bytes 1179648 | tf_op jit(solution)/shard_map/all_to_all | solution.py:354
  36.8 2.3 %collective-permute-start.2 = (bf16[264,768]{1,0:T(8,128)(2,1)S(1)}, bf16[264,768]{1,0:T(8,128)(2,1)S(1)}, u32[]{:S(2)}, u32[]{:S(2)}) collective-permute-start(bf16[264,768]{1,0:T(8,128)(2,1)S(1)} %copy-done.17), channel_id=1, source_target_pairs={{0,96},{32,0},{64,32},{96,64},{128,224},{160,128},{192,160},{224,1... | collective-permute-start | bytes 1216520 | tf_op jit(solution)/shard_map/ppermute | solution.py:345
  40.8 16.3 %collective-permute-done.2.recv3 = bf16[264,768]{1,0:T(8,128)(2,1)S(1)} collective-permute-done((bf16[264,768]{1,0:T(8,128)(2,1)S(1)}, bf16[264,768]{1,0:T(8,128)(2,1)S(1)}, u32[]{:S(2)}, u32[]{:S(2)}) %collective-permute-start.2) | collective-permute-done | bytes 405536 | tf_op jit(solution)/shard_map/ppermute | solution.py:345
  57.6 3.1 %collective-permute-done.recv1 = bf16[264,768]{1,0:T(8,128)(2,1)S(1)} collective-permute-done((bf16[264,768]{1,0:T(8,128)(2,1)}, bf16[264,768]{1,0:T(8,128)(2,1)S(1)}, u32[]{:S(2)}, u32[]{:S(2)}) %collective-permute-start) | collective-permute-done | bytes 405536 | tf_op jit(solution)/shard_map/ppermute | solution.py:345
  60.7 4.8 %collective-permute-start.3 = (bf16[8,768]{1,0:T(8,128)(2,1)S(1)}, bf16[8,768]{1,0:T(8,128)(2,1)S(1)}, u32[]{:S(2)}, u32[]{:S(2)}) collective-permute-start(bf16[8,768]{1,0:T(8,128)(2,1)S(1)} %fusion.5), channel_id=1, source_target_pairs={{0,128},{32,160},{64,192},{96,224},{1,129},{33,161},{65,193},{97,2... | collective-permute-start | bytes 36872 | tf_op jit(solution)/shard_map/ppermute | solution.py:382
  67.7 6.8 %shard_map.104 = (bf16[512,768]{1,0:T(8,128)(2,1)}, bf16[512,768]{1,0:T(8,128)(2,1)}, bf16[768,640]{1,0:T(8,128)(2,1)}, f32[512,384]{1,0:T(8,128)}, f32[4,8,128]...) custom-call(s32[2]{0:T(128)} %pad_add_fusion.at, ...), custom_call_target="tpu_custom_call" | custom-call | flops 100000000 | bytes 8837120 | tf_op jit(solution)/shard_map/pallas_call | solution.py:41
  74.6 5.7 %collective-permute-start.6 = (bf16[128,384]{1,0:T(8,128)(2,1)}, bf16[128,384]{1,0:T(8,128)(2,1)S(1)}, u32[]{:S(2)}, u32[]{:S(2)}) collective-permute-start(bf16[128,384]{1,0:T(8,128)(2,1)} %get-tuple-element.52), channel_id=1, source_target_pairs={{0,128},{32,160},{64,192},{96,224},{1,129},{33,161},{65,193},{97,2... | collective-permute-start | bytes 294920 | tf_op jit(solution)/shard_map/ppermute | solution.py:405
  82.5 3.2 %shard_map.105.y_in = f32[512,384]{1,0:T(8,128)} custom-call(bf16[512,640]{1,0:T(8,128)(2,1)} %get-tuple-element.49.conv, f32[512,384]{1,0:T(8,128)} %get-tuple-element.50.cum, f32[4,8,128]{2,1,0:T(8,128)} %get-tuple-element.53.cum_t, f32[1,384]{1,0:T(1,128)} %broadcast_in_dim_reshape.3.dskip), custom_call_target="tpu_custom_call" | custom-call | flops 100000000 | bytes 2246144 | tf_op jit(solution)/shard_map/pallas_call | solution.py:41
  86.5 6.9 %shard_map.106 = (f32[512,384]{1,0:T(8,128)}, bf16[4,128,384]{2,1,0:T(8,128)(2,1)}, bf16[512,384]{1,0:T(8,128)(2,1)}, f32[512,384]{1,0:T(8,128)}, bf16[4,128,768...) custom-call(s32[2]{0:T(128)} %pad_add_fusion.at, bf16[512,640]{1,0:T(8,128)(2,1)} %get-tuple-element.49.conv, ...), custom_call_target="tpu_custom_call" | custom-call | flops 100000000 | bytes 9606656 | tf_op jit(solution)/shard_map/pallas_call | solution.py:41
  93.4 3.6 %all-to-all-start.2 = ((bf16[4,128,768]{2,1,0:T(8,128)(2,1)}), bf16[4,128,768]{2,1,0:T(8,128)(2,1)S(1)}, u32[]{:S(2)}, u32[]{:S(2)}) async-start(bf16[4,128,768]{2,1,0:T(8,128)(2,1)} %get-tuple-element.68), calls=%async_computation.2 | async-start | bytes 1572864 | tf_op jit(solution)/shard_map/all_to_all | solution.py:348
  97.1 3.3 %collective-permute-start.10 = (f32[2,512]{1,0:T(2,128)S(1)}, f32[2,512]{1,0:T(2,128)S(1)}, u32[]{:S(2)}, u32[]{:S(2)}) collective-permute-start(f32[2,512]{1,0:T(2,128)S(1)} %copy-done.13), channel_id=1, source_target_pairs={{0,96},{32,0},{64,32},{96,64},{128,224},{160,128},{192,160},{224,1... | collective-permute-start | bytes 12296 | tf_op jit(solution)/shard_map/ppermute | solution.py:345
  100.4 2.3 %collective-permute-start.9 = (f32[2,512]{1,0:T(2,128)S(1)}, f32[2,512]{1,0:T(2,128)S(1)}, u32[]{:S(2)}, u32[]{:S(2)}) collective-permute-start(f32[2,512]{1,0:T(2,128)S(1)} %copy-done.13), channel_id=1, source_target_pairs={{0,64},{32,96},{64,0},{96,32},{128,192},{160,224},{192,128},{224,1... | collective-permute-start | bytes 12296 | tf_op jit(solution)/shard_map/ppermute | solution.py:345
  102.7 1.3 fusion.perm
  104.0 2.7 %collective-permute-done.10.stats3 = f32[2,512]{1,0:T(2,128)S(1)} collective-permute-done((f32[2,512]{1,0:T(2,128)S(1)}, f32[2,512]{1,0:T(2,128)S(1)}, u32[]{:S(2)}, u32[]{:S(2)}) %collective-permute-start.10) | collective-permute-done | bytes 4128 | tf_op jit(solution)/shard_map/ppermute | solution.py:345
  106.7 1.5 collective-permute-done.8.stats1
  108.8 6.1 %shard_map.107 = (f32[4,128,128]{2,1,0:T(8,128)}, bf16[512,384]{1,0:T(8,128)(2,1)}, f32[512,384]{1,0:T(8,128)}, f32[4,128,384]{2,1,0:T(8,128)}, bf16[128,384]{1,0:T(8,128)(2,1)}, /*index=5*/bf16[768,384]{1,0:T(8,128)(2,1)}) custom-call(f32[512,384]{1,0:T(8,128)} %get-tuple-element.58.y, bf16[512,384]{1,0:T(8,128)(2,1)} %get-tuple-element.59.gate, ...), custom_call_target="tpu_custom_call" | custom-call | flops 100000000 | bytes 8308224 | tf_op jit(solution)/shard_map/pallas_call | solution.py:41
  114.9 7.7 %all-to-all-start.3 = ((bf16[32,24,384]{2,1,0:T(8,128)(2,1)}), bf16[32,24,384]{2,1,0:T(8,128)(2,1)S(1)}, u32[]{:S(2)}, u32[]{:S(2)}) async-start(bf16[32,24,384]{2,1,0:T(8,128)(2,1)} %bitcast.27), calls=%async_computation.3 | async-start | bytes 1179648 | tf_op jit(solution)/shard_map/all_to_all | solution.py:434
  122.6 1.3 collective-permute-start.11
  123.9 5.6 %shard_map.108 = (f32[512,384]{1,0:T(8,128)}, f32[512,256]{1,0:T(8,128)}, f32[8,640]{1,0:T(8,128)}) custom-call(bf16[512,640]{1,0:T(8,128)(2,1)} %get-tuple-element.49.conv, f32[512,384]{1,0:T(8,128)} %get-tuple-element.50.cum, f32[4,8,128]{2,1,0:T(8,128)} %get-tuple-element.53.cum_t, f32[1,384]{1,0:T(1,128)} %broadcast_in_dim_reshape.3.dskip, ...), custom_call_target="tpu_custom_call" | custom-call | flops 100000000 | bytes 6067712 | tf_op jit(solution)/shard_map/pallas_call | solution.py:41
  129.6 1.3 collective-permute-start.12
  130.8 1.3 collective-permute-done.11.leaving
  132.8 5.0 %shard_map.109 = (f32[512,640]{1,0:T(8,128)}, bf16[128,768]{1,0:T(8,128)(2,1)}) custom-call(s32[2]{0:T(128)} %pad_add_fusion.at, bf16[512,640]{1,0:T(8,128)(2,1)} %get-tuple-element.49.conv, f32[512,384]{1,0:T(8,128)} %get-tuple-element.50.cum, bf16[4,128,384]{2,1,0:T(8,128)(2,1)} %get-tuple-element.57.full, f32[4,128,384]{2,1,0:T(8,128)} %get-tuple-element.62.ends, ...), custom_call_target="tpu_custom_call" | custom-call | flops 100000000 | bytes 8683520 | tf_op jit(solution)/shard_map/pallas_call | solution.py:41
  138.4 5.5 %shard_map.110 = (bf16[128,768]{1,0:T(8,128)(2,1)}, bf16[128,768]{1,0:T(8,128)(2,1)}, bf16[128,768]{1,0:T(8,128)(2,1)}, bf16[128,768]{1,0:T(8,128)(2,1)}) custom-call(s32[2]{0:T(128)} %pad_add_fusion.at, f32[512,640]{1,0:T(8,128)} %get-tuple-element.71.gp, f32[8,640]{1,0:T(8,128)} %copy-done.11, f32[4,640]{1,0:T(4,128)} %pad_maximum_fusion.1.conv_w, ...), custom_call_target="tpu_custom_call" | custom-call | flops 100000000 | bytes 4093952 | tf_op jit(solution)/shard_map/pallas_call | solution.py:41
  144.4 2.1 %collective-permute-start.14 = (bf16[128,768]{1,0:T(8,128)(2,1)}, bf16[128,768]{1,0:T(8,128)(2,1)S(1)}, u32[]{:S(2)}, u32[]{:S(2)}) collective-permute-start(bf16[128,768]{1,0:T(8,128)(2,1)} %get-tuple-element.78), channel_id=1, source_target_pairs={{0,64},{32,96},{64,0},{96,32},{128,192},{160,224},{192,128},{224,1... | collective-permute-start | bytes 589832 | tf_op jit(solution)/shard_map/ppermute | solution.py:345
  148.3 5.9 %all-to-all-start.4 = ((f32[8,3,384]{2,1,0:T(4,128)}), f32[8,3,384]{2,1,0:T(4,128)S(1)}, u32[]{:S(2)}, u32[]{:S(2)}) async-start(f32[8,3,384]{2,1,0:T(4,128)} %reshape.66), calls=%async_computation.4 | async-start | bytes 98304 | tf_op jit(solution)/shard_map/all_to_all | solution.py:453
  155.7 1.7 %fusion.1 = bf16[1,128,768]{2,1,0:T(8,128)(2,1)} fusion(bf16[128,768]{1,0:T(8,128)(2,1)S(1)} %collective-permute-done.15, bf16[128,768]{1,0:T(8,128)(2,1)S(1)} %collective-permute-done.14, bf16[128,768]{1,0:T(8,128)(2,1)S(1)} %collective-permute-done.13, bf16[128,768]{1,0:T(8,128)(2,1)} %get-tuple-element.76), kind=kLoop, calls=%fused_computation.4 | loop fusion | flops 786432 | bytes 983040 | tf_op jit(solution)/shard_map/broadcast_in_dim | solution.py:457
  157.4 4.7 %all-to-all-done.4 = f32[8,3,384]{2,1,0:T(4,128)S(1)} async-done(((f32[8,3,384]{2,1,0:T(4,128)}), f32[8,3,384]{2,1,0:T(4,128)S(1)}, u32[]{:S(2)}, u32[]{:S(2)}) %all-to-all-start.4) | async-done | bytes 36896 | tf_op jit(solution)/shard_map/all_to_all | solution.py:453
  (84 shorter events, 16.1 us)
Async XLA Ops:
  0.6 12.8 %copy-start.10 = (bf16[48,768]{1,0:T(8,128)(2,1)S(1)}, bf16[48,768]{1,0:T(8,128)(2,1)}, u32[]{:S(2)}) copy-start(bf16[48,768]{1,0:T(8,128)(2,1)} %param.12) | copy-start | bytes 221188
  3.7 33.1 %copy-start.17 = (bf16[264,768]{1,0:T(8,128)(2,1)S(1)}, bf16[264,768]{1,0:T(8,128)(2,1)}, u32[]{:S(2)}) copy-start(bf16[264,768]{1,0:T(8,128)(2,1)} %get-tuple-element.45) | copy-start | bytes 1216516
  3.7 24.9 %all-to-all-start = ((bf16[16,24,640]{2,1,0:T(8,128)(2,1)}), bf16[16,24,640]{2,1,0:T(8,128)(2,1)S(1)}, u32[]{:S(2)}, u32[]{:S(2)}) async-start(bf16[16,24,640]{2,1,0:T(8,128)(2,1)} %get-tuple-element.47), calls=%async_computation | async-start | bytes 983040 | tf_op jit(solution)/shard_map/all_to_all | solution.py:354
  13.4 27.3 %slice-start = ((f32[4,1792]{1,0:T(4,128)}), f32[4,1536]{1,0:T(4,128)S(1)}, s32[]{:S(2)}) async-start(f32[4,1792]{1,0:T(4,128)} %param.13), calls=%async_computation.5 | async-start | bytes 49152 | tf_op jit(solution)/shard_map/slice | solution.py:388
  13.5 52.1 %slice-start.1 = ((f32[4,1792]{1,0:T(4,128)}), f32[4,256]{1,0:T(4,128)S(1)}, s32[]{:S(2)}) async-start(f32[4,1792]{1,0:T(4,128)} %param.13), calls=%async_computation.6 | async-start | bytes 8192 | tf_op jit(solution)/shard_map/slice | solution.py:388
  13.5 12.3 %collective-permute-start.4 = (bf16[24,384]{1,0:T(8,128)(2,1)S(1)}, bf16[24,384]{1,0:T(8,128)(2,1)S(1)}, u32[]{:S(2)}, u32[]{:S(2)}) collective-permute-start(bf16[24,384]{1,0:T(8,128)(2,1)S(1)} %constant_dynamic-slice_fusion.1), channel_id=1, source_target_pairs={{0,0},{1,4},{2,8},{3,12},{4,16},{5,20},{6,24},{7,28},{8,32},{9,36}... | collective-permute-start | bytes 55304 | tf_op jit(solution)/shard_map/ppermute | solution.py:364
  28.6 38.4 %copy-start.2 = (bf16[16,24,640]{2,1,0:T(8,128)(2,1)}, bf16[16,24,640]{2,1,0:T(8,128)(2,1)S(1)}, u32[]{:S(2)}) copy-start(bf16[16,24,640]{2,1,0:T(8,128)(2,1)S(1)} %all-to-all-done.same) | copy-start | bytes 1474564
  29.5 27.6 %all-to-all-start.1 = ((bf16[16,24,768]{2,1,0:T(8,128)(2,1)}), bf16[16,24,768]{2,1,0:T(8,128)(2,1)S(1)}, u32[]{:S(2)}, u32[]{:S(2)}) async-start(bf16[16,24,768]{2,1,0:T(8,128)(2,1)} %broadcast_in_dim.20), calls=%async_computation.1 | async-start | bytes 1179648 | tf_op jit(solution)/shard_map/all_to_all | solution.py:354
  36.8 20.3 %collective-permute-start.2 = (bf16[264,768]{1,0:T(8,128)(2,1)S(1)}, bf16[264,768]{1,0:T(8,128)(2,1)S(1)}, u32[]{:S(2)}, u32[]{:S(2)}) collective-permute-start(bf16[264,768]{1,0:T(8,128)(2,1)S(1)} %copy-done.17), channel_id=1, source_target_pairs={{0,96},{32,0},{64,32},{96,64},{128,224},{160,128},{192,160},{224,1... | collective-permute-start | bytes 1216520 | tf_op jit(solution)/shard_map/ppermute | solution.py:345
  39.1 18.5 %collective-permute-start.1 = (bf16[264,768]{1,0:T(8,128)(2,1)}, bf16[264,768]{1,0:T(8,128)(2,1)S(1)}, u32[]{:S(2)}, u32[]{:S(2)}) collective-permute-start(bf16[264,768]{1,0:T(8,128)(2,1)} %get-tuple-element.44), channel_id=1, source_target_pairs={{0,64},{32,96},{64,0},{96,32},{128,192},{160,224},{192,128},{224,1... | collective-permute-start | bytes 1216520 | tf_op jit(solution)/shard_map/ppermute | solution.py:345
  39.3 21.4 %collective-permute-start = (bf16[264,768]{1,0:T(8,128)(2,1)}, bf16[264,768]{1,0:T(8,128)(2,1)S(1)}, u32[]{:S(2)}, u32[]{:S(2)}) collective-permute-start(bf16[264,768]{1,0:T(8,128)(2,1)} %get-tuple-element.43), channel_id=1, source_target_pairs={{0,32},{32,64},{64,96},{96,0},{128,160},{160,192},{192,224},{224,1... | collective-permute-start | bytes 1216520 | tf_op jit(solution)/shard_map/ppermute | solution.py:345
  57.1 9.9 %copy-start.5 = (bf16[264,768]{1,0:T(8,128)(2,1)}, bf16[264,768]{1,0:T(8,128)(2,1)S(1)}, u32[]{:S(2)}) copy-start(bf16[264,768]{1,0:T(8,128)(2,1)S(1)} %collective-permute-done.2.recv3) | copy-start | bytes 1216516
  57.1 9.9 %collective-permute-start.5 = (bf16[16,24,640]{2,1,0:T(8,128)(2,1)S(1)}, bf16[16,24,640]{2,1,0:T(8,128)(2,1)S(1)}, u32[]{:S(2)}, u32[]{:S(2)}) collective-permute-start(bf16[16,24,640]{2,1,0:T(8,128)(2,1)S(1)} %all-to-all-done.same), channel_id=1, source_target_pairs={{0,1},{1,0},{2,3},{3,2},{4,5},{5,4},{6,7},{7,6},{8,9},{9,8},{10,11... | collective-permute-start | bytes 1474568 | tf_op jit(solution)/shard_map/ppermute | solution.py:355
  57.1 17.5 %copy-start.1 = (bf16[16,24,768]{2,1,0:T(8,128)(2,1)}, bf16[16,24,768]{2,1,0:T(8,128)(2,1)S(1)}, u32[]{:S(2)}) copy-start(bf16[16,24,768]{2,1,0:T(8,128)(2,1)S(1)} %all-to-all-done.1.same) | copy-start | bytes 1769476
  57.1 28.6 %collective-permute-start.7 = (bf16[16,24,768]{2,1,0:T(8,128)(2,1)S(1)}, bf16[16,24,768]{2,1,0:T(8,128)(2,1)S(1)}, u32[]{:S(2)}, u32[]{:S(2)}) collective-permute-start(bf16[16,24,768]{2,1,0:T(8,128)(2,1)S(1)} %all-to-all-done.1.same), channel_id=1, source_target_pairs={{0,1},{1,0},{2,3},{3,2},{4,5},{5,4},{6,7},{7,6},{8,9},{9,8},{10,11... | collective-permute-start | bytes 1769480 | tf_op jit(solution)/shard_map/ppermute | solution.py:355
  57.6 9.4 %copy-start.6 = (bf16[264,768]{1,0:T(8,128)(2,1)}, bf16[264,768]{1,0:T(8,128)(2,1)S(1)}, u32[]{:S(2)}) copy-start(bf16[264,768]{1,0:T(8,128)(2,1)S(1)} %collective-permute-done.1.recv2) | copy-start | bytes 1216516
  60.7 6.3 %copy-start.7 = (bf16[264,768]{1,0:T(8,128)(2,1)}, bf16[264,768]{1,0:T(8,128)(2,1)S(1)}, u32[]{:S(2)}) copy-start(bf16[264,768]{1,0:T(8,128)(2,1)S(1)} %collective-permute-done.recv1) | copy-start | bytes 1216516
  60.7 6.2 %collective-permute-start.3 = (bf16[8,768]{1,0:T(8,128)(2,1)S(1)}, bf16[8,768]{1,0:T(8,128)(2,1)S(1)}, u32[]{:S(2)}, u32[]{:S(2)}) collective-permute-start(bf16[8,768]{1,0:T(8,128)(2,1)S(1)} %fusion.5), channel_id=1, source_target_pairs={{0,128},{32,160},{64,192},{96,224},{1,129},{33,161},{65,193},{97,2... | collective-permute-start | bytes 36872 | tf_op jit(solution)/shard_map/ppermute | solution.py:382
  67.7 12.6 %copy-start.18 = (f32[24]{0:T(128)S(1)}, f32[24]{0:T(128)}, u32[]{:S(2)}) copy-start(f32[24]{0:T(128)} %param.14) | copy-start | bytes 292
  74.6 11.1 %collective-permute-start.6 = (bf16[128,384]{1,0:T(8,128)(2,1)}, bf16[128,384]{1,0:T(8,128)(2,1)S(1)}, u32[]{:S(2)}, u32[]{:S(2)}) collective-permute-start(bf16[128,384]{1,0:T(8,128)(2,1)} %get-tuple-element.52), channel_id=1, source_target_pairs={{0,128},{32,160},{64,192},{96,224},{1,129},{33,161},{65,193},{97,2... | collective-permute-start | bytes 294920 | tf_op jit(solution)/shard_map/ppermute | solution.py:405
  93.4 21.4 %all-to-all-start.2 = ((bf16[4,128,768]{2,1,0:T(8,128)(2,1)}), bf16[4,128,768]{2,1,0:T(8,128)(2,1)S(1)}, u32[]{:S(2)}, u32[]{:S(2)}) async-start(bf16[4,128,768]{2,1,0:T(8,128)(2,1)} %get-tuple-element.68), calls=%async_computation.2 | async-start | bytes 1572864 | tf_op jit(solution)/shard_map/all_to_all | solution.py:348
  97.1 9.6 %collective-permute-start.10 = (f32[2,512]{1,0:T(2,128)S(1)}, f32[2,512]{1,0:T(2,128)S(1)}, u32[]{:S(2)}, u32[]{:S(2)}) collective-permute-start(f32[2,512]{1,0:T(2,128)S(1)} %copy-done.13), channel_id=1, source_target_pairs={{0,96},{32,0},{64,32},{96,64},{128,224},{160,128},{192,160},{224,1... | collective-permute-start | bytes 12296 | tf_op jit(solution)/shard_map/ppermute | solution.py:345
  100.4 7.8 %collective-permute-start.8 = (f32[2,512]{1,0:T(2,128)S(1)}, f32[2,512]{1,0:T(2,128)S(1)}, u32[]{:S(2)}, u32[]{:S(2)}) collective-permute-start(f32[2,512]{1,0:T(2,128)S(1)} %copy-done.13), channel_id=1, source_target_pairs={{0,32},{32,64},{64,96},{96,0},{128,160},{160,192},{192,224},{224,1... | collective-permute-start | bytes 12296 | tf_op jit(solution)/shard_map/ppermute | solution.py:345
  100.4 7.9 %collective-permute-start.9 = (f32[2,512]{1,0:T(2,128)S(1)}, f32[2,512]{1,0:T(2,128)S(1)}, u32[]{:S(2)}, u32[]{:S(2)}) collective-permute-start(f32[2,512]{1,0:T(2,128)S(1)} %copy-done.13), channel_id=1, source_target_pairs={{0,64},{32,96},{64,0},{96,32},{128,192},{160,224},{192,128},{224,1... | collective-permute-start | bytes 12296 | tf_op jit(solution)/shard_map/ppermute | solution.py:345
  114.9 14.7 %copy-start = (bf16[4,128,768]{2,1,0:T(8,128)(2,1)}, bf16[4,128,768]{2,1,0:T(8,128)(2,1)S(1)}, u32[]{:S(2)}) copy-start(bf16[4,128,768]{2,1,0:T(8,128)(2,1)S(1)} %all-to-all-done.2.parts) | copy-start | bytes 2359300
  114.9 32.7 %all-to-all-start.3 = ((bf16[32,24,384]{2,1,0:T(8,128)(2,1)}), bf16[32,24,384]{2,1,0:T(8,128)(2,1)S(1)}, u32[]{:S(2)}, u32[]{:S(2)}) async-start(bf16[32,24,384]{2,1,0:T(8,128)(2,1)} %bitcast.27), calls=%async_computation.3 | async-start | bytes 1179648 | tf_op jit(solution)/shard_map/all_to_all | solution.py:434
  122.6 9.5 %collective-permute-start.11 = (bf16[128,384]{1,0:T(8,128)(2,1)}, bf16[128,384]{1,0:T(8,128)(2,1)S(1)}, u32[]{:S(2)}, u32[]{:S(2)}) collective-permute-start(bf16[128,384]{1,0:T(8,128)(2,1)} %get-tuple-element.63), channel_id=1, source_target_pairs={{128,0},{160,32},{192,64},{224,96},{129,1},{161,33},{193,65},{225,... | collective-permute-start | bytes 294920 | tf_op jit(solution)/shard_map/ppermute | solution.py:427
  129.6 8.2 %collective-permute-start.12 = (f32[8,640]{1,0:T(8,128)}, f32[8,640]{1,0:T(8,128)S(1)}, u32[]{:S(2)}, u32[]{:S(2)}) collective-permute-start(f32[8,640]{1,0:T(8,128)} %get-tuple-element.72), channel_id=1, source_target_pairs={{128,0},{160,32},{192,64},{224,96},{129,1},{161,33},{193,65},{225,... | collective-permute-start | bytes 61448 | tf_op jit(solution)/shard_map/ppermute | solution.py:433
  143.8 11.3 %collective-permute-start.13 = (bf16[128,768]{1,0:T(8,128)(2,1)}, bf16[128,768]{1,0:T(8,128)(2,1)S(1)}, u32[]{:S(2)}, u32[]{:S(2)}) collective-permute-start(bf16[128,768]{1,0:T(8,128)(2,1)} %get-tuple-element.77), channel_id=1, source_target_pairs={{0,32},{32,64},{64,96},{96,0},{128,160},{160,192},{192,224},{224,1... | collective-permute-start | bytes 589832 | tf_op jit(solution)/shard_map/ppermute | solution.py:345
  144.4 10.7 %collective-permute-start.14 = (bf16[128,768]{1,0:T(8,128)(2,1)}, bf16[128,768]{1,0:T(8,128)(2,1)S(1)}, u32[]{:S(2)}, u32[]{:S(2)}) collective-permute-start(bf16[128,768]{1,0:T(8,128)(2,1)} %get-tuple-element.78), channel_id=1, source_target_pairs={{0,64},{32,96},{64,0},{96,32},{128,192},{160,224},{192,128},{224,1... | collective-permute-start | bytes 589832 | tf_op jit(solution)/shard_map/ppermute | solution.py:345
  146.5 9.2 %collective-permute-start.15 = (bf16[128,768]{1,0:T(8,128)(2,1)}, bf16[128,768]{1,0:T(8,128)(2,1)S(1)}, u32[]{:S(2)}, u32[]{:S(2)}) collective-permute-start(bf16[128,768]{1,0:T(8,128)(2,1)} %get-tuple-element.79), channel_id=1, source_target_pairs={{0,96},{32,0},{64,32},{96,64},{128,224},{160,128},{192,160},{224,1... | collective-permute-start | bytes 589832 | tf_op jit(solution)/shard_map/ppermute | solution.py:345
  148.3 13.8 %all-to-all-start.4 = ((f32[8,3,384]{2,1,0:T(4,128)}), f32[8,3,384]{2,1,0:T(4,128)S(1)}, u32[]{:S(2)}, u32[]{:S(2)}) async-start(f32[8,3,384]{2,1,0:T(4,128)} %reshape.66), calls=%async_computation.4 | async-start | bytes 98304 | tf_op jit(solution)/shard_map/all_to_all | solution.py:453
  (10 other events, 10.5 us)
where the time goes:
time: 164 us; the launch traced here: 163 us
  starting transfers between devices  66.9 us (41%)
  Pallas kernels  41.4 us (25%)
  waiting for transfers between devices  39.8 us (24%)
  local copies, waits for them, and re-layouts  7.95 us (5%)
  other arithmetic  5.75 us (4%)
    pallas_call x8, Pallas kernels, kernel_call(): pl.pallas_call(body, out_shape=outs, in_specs=[pl.BlockSpec(memory_space=...  41.4 us
    ppermute x9, waiting for transfers between devices, along_x(): return lax.ppermute(array, 'tm', pairs)  25 us
    all_to_all x2, starting transfers between devices, gather_weights(): same = lax.all_to_all(wide, 'stream', 0, 0, axis_index_groups=cores)  17 us
    ppermute x9, starting transfers between devices, along_x(): return lax.ppermute(array, 'tm', pairs)  12.6 us
    all_to_all x1, starting transfers between devices, shards(): pieces = lax.all_to_all(dw.reshape(stream, -1, width), 'stream', 0, 0)  7.73 us
    ppermute x1, starting transfers between devices, shards(): lax.ppermute(own(out_w.reshape(-1, width), 0, piece), ('tm', 'stream'), r...  6.38 us
    ppermute x1, waiting for transfers between devices, shards(): lax.ppermute(own(out_w.reshape(-1, width), 0, piece), ('tm', 'stream'), r...  5.96 us
    all_to_all x1, starting transfers between devices, shards(): swapped = lax.all_to_all(summed, 'tm', 0, 0)  5.94 us
  transfers between devices with their start and end apart: 21, of which 11 were waited for; matrix products, arithmetic and copies ran while one was open for 5% of the time, Pallas kernels for 20%

commit v1 on v0

--- a/solution.py
+++ b/solution.py
@@ -76,7 +76,12 @@
     return jnp.where(causal(), jnp.exp(jnp.minimum(column - row, 0.0)), 0.0)
 
 
-def prepare(at, logs, in_w, tokens, cotangent, wide, gate_w, aux, send1, send2, send3, decays):
+def place(at, r):
+    chunk = lax.rem(at[0] + (XS - r), XS)
+    return chunk, pl.ds(pl.multiple_of(chunk * CHUNK, CHUNK), CHUNK)
+
+
+def prepare(at, in_w, wide, gate_w):
     width = gate_w.shape[1]
     inner = XS * width
     start = pl.multiple_of(at[0] * width, width)
@@ -84,6 +89,9 @@
         wide[i, :, :width] = in_w[:, pl.ds(inner + start, width)]
         wide[i, :, width:] = in_w[:, 2 * inner :]
     gate_w[...] = in_w[:, pl.ds(start, width)]
+
+
+def pack(at, logs, tokens, halo, aux, send1, send2, send3, decays):
     block = logs.shape[1]
     step = lax.broadcasted_iota(jnp.int32, (block, block), 0)
     upto = (step <= lax.broadcasted_iota(jnp.int32, (block, block), 1)).astype(f32)
@@ -93,17 +101,17 @@
     middle = rest.astype(bf16).astype(f32)
     low = rest - middle
     per = logs.shape[0] // XS
-    rest_rows = jnp.zeros((5, block), f32)
     for j in range(XS):
         for i in range(per):
             h = j * per + i
-            rows = [high[h : h + 1], middle[h : h + 1], low[h : h + 1], rest_rows]
+            rows = [high[h : h + 1], middle[h : h + 1], low[h : h + 1], jnp.zeros((5, block), f32)]
             decays[j, :, i * block : (i + 1) * block] = jnp.concatenate(rows, axis=0)
-    aux[...] = decays[at[0]].astype(bf16)
+    tail = halo[...].astype(f32)
+    tail = jnp.where(lax.broadcasted_iota(jnp.int32, tail.shape, 0) < 3, 0.0, tail)
+    aux[...] = (decays[at[0]] + tail).astype(bf16)
     for r, send in enumerate((send1, send2, send3)):
         send[:block, :] = tokens[...]
-        send[block : 2 * block, :] = cotangent[...]
-        send[2 * block :, :] = decays[lax.rem(at[0] + r + 1, XS)].astype(bf16)
+        send[block:, :] = (decays[lax.rem(at[0] + r + 1, XS)] + tail).astype(bf16)
 
 
 def assemble(at, same, other, target, lanes):
@@ -114,29 +122,25 @@
         target[48 * i + 24 : 48 * i + 48, :] = jnp.where(own_first, b, a).astype(target.dtype)
 
 
-def project(at, tokens, cotangent, aux, recv1, recv2, recv3, halo, same, other, conv_w,
-            tok, cot, w_mix, cum, cum_t, pre, conv, states, last, mix):
+def project(at, tokens, aux, recv1, recv2, recv3, same, other, conv_w,
+            w_mix, cum, cum_t, pre, conv, states, last, mix):
     width = last.shape[1]
     chunks = XS
     block = CHUNK
     assemble(at, same, other, w_mix, slice(None))
+    halo = jnp.zeros(aux.shape, f32)
     for r, source in enumerate((None, recv1, recv2, recv3)):
-        c = lax.rem(at[0] + (XS - r), XS)
-        here = pl.ds(pl.multiple_of(c * block, block), block)
-        if source is None:
-            t, k, extra = tokens[...], cotangent[...], aux[...].astype(f32)
-        else:
-            t, k = source[:block, :], source[block : 2 * block, :]
-            extra = source[2 * block :, :].astype(f32)
-        tok[here, :] = t
-        cot[here, :] = k
+        c, _ = place(at, r)
+        t = tokens[...] if r == 0 else source[:block, :]
+        extra = (aux[...] if r == 0 else source[block:, :]).astype(f32)
+        halo = halo + extra
         mix[pl.ds(pl.multiple_of(8 + c * block, 8), block), :] = (
             dot(t, w_mix[...]).astype(bf16).astype(f32)
         )
         total = extra[0:1] + extra[1:2] + extra[2:3]
         heads = [total[:, i * block : (i + 1) * block] for i in range(width // 64)]
         cum_t[c] = jnp.concatenate(heads + [jnp.zeros((8 - len(heads), block), f32)], axis=0)
-    mix[:8, :] = dot(halo[...], w_mix[...]).astype(bf16).astype(f32)
+    mix[:8, :] = dot(halo, w_mix[...]).astype(bf16).astype(f32)
     left = halves()
     state = jnp.zeros(last.shape, f32)
     for c in range(chunks):
@@ -154,7 +158,7 @@
                 value = value + conv_w[k : k + 1, s] * mix[start : start + CHUNK, s]
             pre[r, s] = value
             conv[r, s] = (value * sig(value)).astype(bf16)
-        states[c] = state
+        states[c] = state.astype(bf16)
         end = cum[(c + 1) * CHUNK - 1 : (c + 1) * CHUNK, :]
         faded = jnp.exp(end - cum[r, :]) * conv[r, :width].astype(f32)
         state = jnp.exp(end) * state + dot(conv[r, width : width + 128], faded, TN)
@@ -179,7 +183,8 @@
             y[r, s] = dot(weight, both) + dskip[:, s] * x
 
 
-def gated(at, conv, cum, states, entering, y_in, tok, cot, same, other, norm_w,
+def gated(at, conv, cum, states, entering, y_in, tok0, tok1, tok2, tok3, cot0, cot1, cot2, cot3,
+          same, other, norm_w,
           y, full, gate, dn, part, stats, w_gate, raw, w_out):
     width = y.shape[1]
     chunks = y.shape[0] // CHUNK
@@ -189,13 +194,15 @@
         for k in range(2):
             lanes = slice(k * width + p * LANES, k * width + (p + 1) * LANES)
             w_out[:, lanes] = raw[p, pl.ds(k, width, stride=2), :].astype(bf16)
+    for r, (tok, cot) in enumerate(((tok0, cot0), (tok1, cot1), (tok2, cot2), (tok3, cot3))):
+        here = place(at, r)[1]
+        gate[here, :] = dot(tok[:CHUNK, :], w_gate[...]).astype(bf16)
+        dn[here, :] = dot(cot[...], w_out[...], NT) * norm_w[...]
     carried = entering[...].astype(f32)
     ones = jnp.ones((8, LANES), f32)
     for c in range(chunks):
         r = rows_of(c)
-        gate[r, :] = dot(tok[r, :], w_gate[...]).astype(bf16)
-        dn[r, :] = dot(cot[r, :], w_out[...], NT) * norm_w[...]
-        state = states[c] + carried
+        state = states[c].astype(f32) + carried
         full[c] = state.astype(bf16)
         carried = jnp.exp(cum[(c + 1) * CHUNK - 1 : (c + 1) * CHUNK, :]) * carried
         value = y_in[r, :] + jnp.exp(cum[r, :]) * dot(conv[r, width + 128 : width + 256], state)
@@ -210,8 +217,9 @@
         stats[1:2, r] = exact(ones, cross, NT)[0:1]
 
 
-def normed_part(inner, y, gate, dn, stats0, stats1, stats2, stats3, conv, cum, norm_w, cot, perm,
-                factors, dgate, dy, ends, first, dw, low):
+def normed_part(inner, at, y, gate, dn, stats0, stats1, stats2, stats3, conv, cum, norm_w,
+                cot0, cot1, cot2, cot3, perm,
+                factors, dgate, dy, ends, first, keep, give, low, cot):
     width = y.shape[1]
     chunks = y.shape[0] // CHUNK
     adjoint = jnp.zeros(first.shape, f32)
@@ -237,11 +245,15 @@
             conv[r, width + 128 : width + 256], jnp.exp(cum[r, :]) * dvalue, TN
         )
     first[...] = adjoint.astype(bf16)
+    for r, source in enumerate((cot0, cot1, cot2, cot3)):
+        cot[place(at, r)[1], :] = source[...]
     summed = dot(cot[...], low[...], TN)
-    dw[...] = dot(perm[...], summed).astype(bf16)
-
-
-def inside_back(conv, cum, cum_t, dskip, dy, full, ends, pre, dx, dbc, head):
+    keep[...] = dot(perm[: keep.shape[0], :], summed).astype(bf16)
+    give[...] = dot(perm[keep.shape[0] :, :], summed).astype(bf16)
+
+
+def inside_back(conv, cum, cum_t, dskip, dy, full, ends, pre, keep, got, dx, dbc, head, pair):
+    pair[...] = (keep[...].astype(f32) + got[...].astype(f32)).astype(bf16)
     width = dy.shape[1]
     left = halves()
     for c in range(dy.shape[0] // CHUNK):
@@ -354,51 +366,55 @@
         same = lax.all_to_all(wide, "stream", 0, 0, axis_index_groups=cores)
         return same, lax.ppermute(same, "stream", [(i, i ^ 1) for i in range(stream)])
 
+    halo = lax.ppermute(tokens[0, -8:], "tm", [(XS - 1, XS)])
+    at = jnp.stack([mine, core]).astype(jnp.int32)
+    block = tokens.shape[1]
+    short = in_w.shape[0]
+    mixed = width + 2 * state
+    wide1, gate_w = kernel_call(
+        prepare,
+        [out((half, short, mixed), bf16), out((short, width), bf16)],
+        in_w, scalars=at,
+    )
+    same1, other1 = gather_weights(wide1)
+    aux, *sends = kernel_call(
+        pack,
+        [out((8, model), bf16)] + [out((block + 8, model), bf16)] * (XS - 1),
+        decay[0].T, tokens[0], halo,
+        scalars=at, scratch=[pltpu.VMEM((XS, 8, model), f32)],
+    )
+    toks, cots = [tokens[0]], [cotangent[0]]
+    for r in range(1, XS):
+        toks.append(along_x(sends[r - 1], r))
+        cots.append(along_x(cotangent[0], r))
     piece = 2 * out_w.shape[0] // XS
     routes = []
     for t in range(tm):
         for s in range(stream):
-            group, place = divmod(s, stream // XS)
-            target = (t // XS * XS + group, XS * place + t % XS)
+            group, place_ = divmod(s, stream // XS)
+            target = (t // XS * XS + group, XS * place_ + t % XS)
             routes.append((t * stream + s, target[0] * stream + target[1]))
     out_piece = lax.ppermute(own(out_w.reshape(-1, width), 0, piece), ("tm", "stream"), routes)
-    at = jnp.stack([mine, core]).astype(jnp.int32)
-    block = tokens.shape[1]
-    short = in_w.shape[0]
-    mixed = width + 2 * state
-    wide1, gate_w, aux_own, *sends = kernel_call(
-        prepare,
-        [out((half, short, mixed), bf16), out((short, width), bf16), out((8, model), bf16)]
-        + [out((2 * block + 8, model), bf16)] * (XS - 1),
-        decay[0].T, in_w, tokens[0], cotangent[0],
-        scalars=at, scratch=[pltpu.VMEM((XS, 8, model), f32)],
-    )
-    recv = []
-    for r in range(1, XS):
-        recv.append(along_x(sends[r - 1], r))
-    same1, other1 = gather_weights(wide1)
-    tails = [piece[block - 8 : block] for piece in [tokens[0]] + recv]
-    tail = lax.dynamic_index_in_dim(jnp.stack(tails), lax.rem(mine + 1, XS), 0, False)
-    halo = lax.ppermute(tail, "tm", up)
     wide2 = jnp.concatenate([gate_w, out_piece], axis=1)
     wide2 = jnp.broadcast_to(wide2[None], (half,) + wide2.shape)
-    wide2, same1 = lax.optimization_barrier((wide2, same1))
     same2, other2 = gather_weights(wide2)
 
     taps = jnp.concatenate([own(conv_w[:, :inner], 1, width), conv_w[:, inner:]], axis=1)
     gain = own(norm_w, 0, width)[None]
     skip = jnp.repeat(own(dskip, 0, part_heads), width // part_heads)[None]
     index = jnp.arange(model)
-    source = index // 3 % tm * (3 * stream) + index // (3 * tm) * 3 + index % 3
+    late, spot = index // (model // 2), index % (model // 2)
+    target = 2 * (spot // (3 * tm)) + jnp.where(late == 0, core, 1 - core)
+    source = index // 3 % tm * (3 * stream) + target * 3 + index % 3
     perm = (source[:, None] == index[None, :]).astype(bf16)
 
     chunks = rows // CHUNK
-    tok, cot, w_mix, cum, cum_t, pre, conv, states, last = kernel_call(
+    w_mix, cum, cum_t, pre, conv, states, last = kernel_call(
         project,
-        [out((rows, model), bf16), out((rows, model), bf16), out((model, mixed), bf16),
-         out((rows, width), f32), out((chunks, 8, CHUNK), f32), out((rows, mixed), f32),
-         out((rows, mixed), bf16), out((chunks, state, width), f32), out((state, width), bf16)],
-        tokens[0], cotangent[0], aux_own, *recv, halo, same1, other1, taps,
+        [out((model, mixed), bf16), out((rows, width), f32), out((chunks, 8, CHUNK), f32),
+         out((rows, mixed), f32), out((rows, mixed), bf16), out((chunks, state, width), bf16),
+         out((state, width), bf16)],
+        tokens[0], aux, *toks[1:], same1, other1, taps,
         scalars=at,
         scratch=[pltpu.VMEM((rows + 8, mixed), f32)],
     )
@@ -409,7 +425,7 @@
         [out((rows, width), f32), out(states.shape, bf16), out((rows, width), bf16),
          out((rows, width), f32), out((XS, block, model), bf16), out((2, rows), f32),
          out((model, width), bf16)],
-        conv, cum, states, entering, y_in, tok, cot, same2, other2, gain,
+        conv, cum, states, entering, y_in, *toks, *cots, same2, other2, gain,
         scalars=at,
         scratch=[pltpu.VMEM((width // LANES, model, LANES), f32), pltpu.VMEM((width, model), bf16)],
     )
@@ -417,21 +433,25 @@
     for r in range(1, XS):
         others.append(along_x(stats, r))
     parts = swap_x(part)
-    factors, dgate, dy, ends, first, dw = kernel_call(
+    factors, dgate, dy, ends, first, keep, give = kernel_call(
         functools.partial(normed_part, inner),
         [out((chunks, CHUNK, LANES), f32), out((rows, width), bf16), out((rows, width), f32),
-         out(states.shape, f32), out((state, width), bf16), out((model, width), bf16)],
-        y, gate, dn, stats, *others, conv, cum, gain, cot, perm,
-        scratch=[pltpu.VMEM((rows, width), bf16)],
+         out(states.shape, f32), out((state, width), bf16), out((model // 2, width), bf16),
+         out((model // 2, width), bf16)],
+        y, gate, dn, stats, *others, conv, cum, gain, *cots, perm,
+        scalars=at,
+        scratch=[pltpu.VMEM((rows, width), bf16), pltpu.VMEM((rows, model), bf16)],
     )
     leaving = lax.ppermute(first, "tm", down)
-    dx, dbc, head = kernel_call(
+    got = lax.ppermute(give, "stream", [(i, i ^ 1) for i in range(stream)])
+    dx, dbc, head, pair = kernel_call(
         inside_back,
-        [out((rows, width), f32), out((rows, 2 * state), f32), out((8, mixed), f32)],
-        conv, cum, cum_t, skip, dy, full, ends, pre,
+        [out((rows, width), f32), out((rows, 2 * state), f32), out((8, mixed), f32),
+         out(keep.shape, bf16)],
+        conv, cum, cum_t, skip, dy, full, ends, pre, keep, got,
     )
     after = lax.ppermute(head, "tm", down)
-    pieces = lax.all_to_all(dw.reshape(stream, -1, width), "stream", 0, 0)
+    pieces = lax.all_to_all(pair.reshape(half, -1, width), "stream", 0, 0, axis_index_groups=cores)
     gp, result = kernel_call(
         conv_grad,
         [out((rows, mixed), f32), out((block, model), bf16)],

time: 164 us -> 178 us (1.085)
  waiting for transfers between devices: 39.8 us -> 52.4 us
    all_to_all x2, waiting for transfers between devices: 1.98 us -> 18.2 us  [gather_weights(): same = lax.all_to_all(wide, 'stream', 0, 0, axis_index_groups=cores)]
    ppermute x9 -> x12, starting transfers between devices: 12.6 us -> 21.7 us  [along_x(): return lax.ppermute(array, 'tm', pairs)]
    ppermute x9 -> x12, waiting for transfers between devices: 25 us -> 17.9 us  [along_x(): return lax.ppermute(array, 'tm', pairs)]
    ppermute x1, waiting for transfers between devices: 1.31 us -> 6.06 us  [shards(): leaving = lax.ppermute(first, 'tm', down)]
    ppermute x1 -> x2, starting transfers between devices: 4.8 us -> 0.66 us  [the longest x1 0.65 us: shards(): halo = lax.ppermute(tokens[0, -8:], 'tm', [(XS - 1, XS)])]
    all_to_all x1, starting transfers between devices: 7.73 us -> 4.71 us  [shards(): lax.all_to_all(pair.reshape(half, -1, width), 'stream', 0, 0, axis_index_...]
    all_to_all x1, starting transfers between devices: 5.94 us -> 3.66 us  [shards(): swapped = lax.all_to_all(summed, 'tm', 0, 0)]
    all_to_all x1, waiting for transfers between devices: 4.68 us -> 2.53 us  [shards(): swapped = lax.all_to_all(summed, 'tm', 0, 0)]
  transfers between devices with their start and end apart: 21 -> 25, of which waited for: 11 -> 12; matrix products, arithmetic and copies ran while one was open for 5% -> 4% of each run, Pallas kernels for 20% -> 19%
where the time goes in v1:
time: 178 us; the launch traced here: 177 us
  starting transfers between devices  67.9 us (38%)
  waiting for transfers between devices  52.4 us (29%)
  Pallas kernels  41.2 us (23%)
  local copies, waits for them, and re-layouts  8.61 us (5%)
  other arithmetic  5.65 us (3%)
    pallas_call x9, Pallas kernels, kernel_call(): pl.pallas_call(body, out_shape=outs, in_specs=[pl.BlockSpec(memory_space=...  41.2 us
    ppermute x12, starting transfers between devices, along_x(): return lax.ppermute(array, 'tm', pairs)  21.7 us
    all_to_all x2, waiting for transfers between devices, gather_weights(): same = lax.all_to_all(wide, 'stream', 0, 0, axis_index_groups=cores)  18.2 us
    ppermute x12, waiting for transfers between devices, along_x(): return lax.ppermute(array, 'tm', pairs)  17.9 us
    all_to_all x2, starting transfers between devices, gather_weights(): same = lax.all_to_all(wide, 'stream', 0, 0, axis_index_groups=cores)  16.9 us
    ppermute x1, starting transfers between devices, shards(): entering = lax.ppermute(last, 'tm', up)  6.77 us
    ppermute x1, starting transfers between devices, shards(): lax.ppermute(own(out_w.reshape(-1, width), 0, piece), ('tm', 'stream'), r...  6.51 us
    ppermute x1, waiting for transfers between devices, shards(): leaving = lax.ppermute(first, 'tm', down)  6.06 us
  transfers between devices with their start and end apart: 25, of which 12 were waited for; matrix products, arithmetic and copies ran while one was open for 4% of the time, Pallas kernels for 19%

profile of v1, /device:TPU:32, one launch (start us, length us, event | category | flops | bytes accessed | tf_op | source)
XLA Modules:
  0.0 176.7 jit_solution(2881421464770074122)
XLA Ops:
  1.3 1.8 shard_map.104
  3.0 9.6 %all-to-all-start = ((bf16[16,24,640]{2,1,0:T(8,128)(2,1)}), bf16[16,24,640]{2,1,0:T(8,128)(2,1)S(1)}, u32[]{:S(2)}, u32[]{:S(2)}) async-start(bf16[16,24,640]{2,1,0:T(8,128)(2,1)} %get-tuple-element.44), calls=%async_computation | async-start | bytes 983040 | tf_op jit(solution)/shard_map/all_to_all | solution.py:366
  12.8 6.5 %collective-permute-start.9 = (bf16[24,384]{1,0:T(8,128)(2,1)S(1)}, bf16[24,384]{1,0:T(8,128)(2,1)S(1)}, u32[]{:S(2)}, u32[]{:S(2)}) collective-permute-start(bf16[24,384]{1,0:T(8,128)(2,1)S(1)} %constant_dynamic-slice_fusion), channel_id=1, source_target_pairs={{0,0},{1,4},{2,8},{3,12},{4,16},{5,20},{6,24},{7,28},{8,32},{9,36}... | collective-permute-start | bytes 55304 | tf_op jit(solution)/shard_map/ppermute | solution.py:397
  19.3 5.8 %collective-permute-done.9 = bf16[24,384]{1,0:T(8,128)(2,1)S(1)} collective-permute-done((bf16[24,384]{1,0:T(8,128)(2,1)S(1)}, bf16[24,384]{1,0:T(8,128)(2,1)S(1)}, u32[]{:S(2)}, u32[]{:S(2)}) %collective-permute-start.9) | collective-permute-done | bytes 18464 | tf_op jit(solution)/shard_map/ppermute | solution.py:397
  25.8 2.0 %all-to-all-done.same = bf16[16,24,640]{2,1,0:T(8,128)(2,1)S(1)} async-done(((bf16[16,24,640]{2,1,0:T(8,128)(2,1)}), bf16[16,24,640]{2,1,0:T(8,128)(2,1)S(1)}, u32[]{:S(2)}, u32[]{:S(2)}) %all-to-all-start) | async-done | bytes 491552 | tf_op jit(solution)/shard_map/all_to_all | solution.py:366
  28.7 7.3 %all-to-all-start.1 = ((bf16[16,24,768]{2,1,0:T(8,128)(2,1)}), bf16[16,24,768]{2,1,0:T(8,128)(2,1)S(1)}, u32[]{:S(2)}, u32[]{:S(2)}) async-start(bf16[16,24,768]{2,1,0:T(8,128)(2,1)} %broadcast_in_dim.29), calls=%async_computation.1 | async-start | bytes 1179648 | tf_op jit(solution)/shard_map/all_to_all | solution.py:366
  36.1 16.3 %all-to-all-done.1.same = bf16[16,24,768]{2,1,0:T(8,128)(2,1)S(1)} async-done(((bf16[16,24,768]{2,1,0:T(8,128)(2,1)}), bf16[16,24,768]{2,1,0:T(8,128)(2,1)S(1)}, u32[]{:S(2)}, u32[]{:S(2)}) %all-to-all-start.1) | async-done | bytes 589856 | tf_op jit(solution)/shard_map/all_to_all | solution.py:366
  54.4 2.0 %shard_map.103 = (bf16[8,768]{1,0:T(8,128)(2,1)}, bf16[136,768]{1,0:T(8,128)(2,1)}, bf16[136,768]{1,0:T(8,128)(2,1)}, bf16[136,768]{1,0:T(8,128)(2,1)}) custom-call(s32[2]{0:T(128)} %pad_add_fusion.at, f32[24,128]{1,0:T(8,128)} %bitcast.29, bf16[128,768]{1,0:T(8,128)(2,1)} %bitcast.17, bf16[8,768]{1,0:T(8,128)(2,1)} %copy-done.21), custom_call_target="tpu_custom_call" | custom-call | flops 100000000 | bytes 860160 | tf_op jit(solution)/shard_map/pallas_call | solution.py:41
  57.7 8.3 %collective-permute-start.2 = (bf16[136,768]{1,0:T(8,128)(2,1)}, bf16[136,768]{1,0:T(8,128)(2,1)S(1)}, u32[]{:S(2)}, u32[]{:S(2)}) collective-permute-start(bf16[136,768]{1,0:T(8,128)(2,1)} %get-tuple-element.42), channel_id=1, source_target_pairs={{0,64},{32,96},{64,0},{96,32},{128,192},{160,224},{192,128},{224,1... | collective-permute-start | bytes 626696 | tf_op jit(solution)/shard_map/ppermute | solution.py:357
  66.0 3.9 %collective-permute-done.1.recv1.tok1 = bf16[136,768]{1,0:T(8,128)(2,1)S(1)} collective-permute-done((bf16[136,768]{1,0:T(8,128)(2,1)}, bf16[136,768]{1,0:T(8,128)(2,1)S(1)}, u32[]{:S(2)}, u32[]{:S(2)}) %collective-permute-start.1) | collective-permute-done | bytes 208928 | tf_op jit(solution)/shard_map/ppermute | solution.py:357
  69.9 6.8 %collective-permute-done.2.recv2.tok2 = bf16[136,768]{1,0:T(8,128)(2,1)S(1)} collective-permute-done((bf16[136,768]{1,0:T(8,128)(2,1)}, bf16[136,768]{1,0:T(8,128)(2,1)S(1)}, u32[]{:S(2)}, u32[]{:S(2)}) %collective-permute-start.2) | collective-permute-done | bytes 208928 | tf_op jit(solution)/shard_map/ppermute | solution.py:357
  76.7 2.0 %collective-permute-start.8 = (bf16[128,768]{1,0:T(8,128)(2,1)S(1)}, bf16[128,768]{1,0:T(8,128)(2,1)S(1)}, u32[]{:S(2)}, u32[]{:S(2)}) collective-permute-start(bf16[128,768]{1,0:T(8,128)(2,1)S(1)} %bitcast.24), channel_id=1, source_target_pairs={{0,96},{32,0},{64,32},{96,64},{128,224},{160,128},{192,160},{224,1... | collective-permute-start | bytes 589832 | tf_op jit(solution)/shard_map/ppermute | solution.py:357
  79.4 5.6 %shard_map.105 = (bf16[768,640]{1,0:T(8,128)(2,1)}, f32[512,384]{1,0:T(8,128)}, f32[4,8,128]{2,1,0:T(8,128)}, f32[512,640]{1,0:T(8,128)}, bf16[512,640]{1,0:T(8,...) custom-call(s32[2]{0:T(128)} %pad_add_fusion.at, bf16[128,768]{1,0:T(8,128)(2,1)} %bitcast.18, ...), custom_call_target="tpu_custom_call" | custom-call | flops 100000000 | bytes 6072320 | tf_op jit(solution)/shard_map/pallas_call | solution.py:41
  85.1 6.8 %collective-permute-start.5 = (bf16[128,384]{1,0:T(8,128)(2,1)}, bf16[128,384]{1,0:T(8,128)(2,1)S(1)}, u32[]{:S(2)}, u32[]{:S(2)}) collective-permute-start(bf16[128,384]{1,0:T(8,128)(2,1)} %get-tuple-element.48), channel_id=1, source_target_pairs={{0,128},{32,160},{64,192},{96,224},{1,129},{33,161},{65,193},{97,2... | collective-permute-start | bytes 294920 | tf_op jit(solution)/shard_map/ppermute | solution.py:421
  94.0 3.1 %shard_map.106.y_in = f32[512,384]{1,0:T(8,128)} custom-call(bf16[512,640]{1,0:T(8,128)(2,1)} %get-tuple-element.45.conv, f32[512,384]{1,0:T(8,128)} %get-tuple-element.46.cum, f32[4,8,128]{2,1,0:T(8,128)} %get-tuple-element.49.cum_t, f32[1,384]{1,0:T(1,128)} %broadcast_in_dim_reshape.3.dskip), custom_call_target="tpu_custom_call" | custom-call | flops 100000000 | bytes 2246144 | tf_op jit(solution)/shard_map/pallas_call | solution.py:41
  98.2 6.6 %shard_map.107 = (f32[512,384]{1,0:T(8,128)}, bf16[4,128,384]{2,1,0:T(8,128)(2,1)}, bf16[512,384]{1,0:T(8,128)(2,1)}, f32[512,384]{1,0:T(8,128)}, bf16[4,128,768...) custom-call(s32[2]{0:T(128)} %pad_add_fusion.at, bf16[512,640]{1,0:T(8,128)(2,1)} %get-tuple-element.45.conv, ...), custom_call_target="tpu_custom_call" | custom-call | flops 100000000 | bytes 9250304 | tf_op jit(solution)/shard_map/pallas_call | solution.py:41
  104.8 4.1 %all-to-all-start.2 = ((bf16[4,128,768]{2,1,0:T(8,128)(2,1)}), bf16[4,128,768]{2,1,0:T(8,128)(2,1)S(1)}, u32[]{:S(2)}, u32[]{:S(2)}) async-start(bf16[4,128,768]{2,1,0:T(8,128)(2,1)} %get-tuple-element.64), calls=%async_computation.2 | async-start | bytes 1572864 | tf_op jit(solution)/shard_map/all_to_all | solution.py:360
  108.9 2.1 %collective-permute-start.11 = (f32[2,512]{1,0:T(2,128)S(1)}, f32[2,512]{1,0:T(2,128)S(1)}, u32[]{:S(2)}, u32[]{:S(2)}) collective-permute-start(f32[2,512]{1,0:T(2,128)S(1)} %copy-done.16), channel_id=1, source_target_pairs={{0,32},{32,64},{64,96},{96,0},{128,160},{160,192},{192,224},{224,1... | collective-permute-start | bytes 12296 | tf_op jit(solution)/shard_map/ppermute | solution.py:357
  111.0 2.7 %collective-permute-start.12 = (f32[2,512]{1,0:T(2,128)S(1)}, f32[2,512]{1,0:T(2,128)S(1)}, u32[]{:S(2)}, u32[]{:S(2)}) collective-permute-start(f32[2,512]{1,0:T(2,128)S(1)} %copy-done.16), channel_id=1, source_target_pairs={{0,64},{32,96},{64,0},{96,32},{128,192},{160,224},{192,128},{224,1... | collective-permute-start | bytes 12296 | tf_op jit(solution)/shard_map/ppermute | solution.py:357
  117.9 2.2 %collective-permute-done.12.stats2 = f32[2,512]{1,0:T(2,128)S(1)} collective-permute-done((f32[2,512]{1,0:T(2,128)S(1)}, f32[2,512]{1,0:T(2,128)S(1)}, u32[]{:S(2)}, u32[]{:S(2)}) %collective-permute-start.12) | collective-permute-done | bytes 4128 | tf_op jit(solution)/shard_map/ppermute | solution.py:357
  120.7 5.8 %shard_map.108 = (f32[4,128,128]{2,1,0:T(8,128)}, bf16[512,384]{1,0:T(8,128)(2,1)}, f32[512,384]{1,0:T(8,128)}, f32[4,128,384]{2,1,0:T(8,128)}, bf16[128,384]{1,...) custom-call(s32[2]{0:T(128)} %pad_add_fusion.at, f32[512,384]{1,0:T(8,128)} %get-tuple-element.52.y, ...), custom_call_target="tpu_custom_call" | custom-call | flops 100000000 | bytes 8308224 | tf_op jit(solution)/shard_map/pallas_call | solution.py:41
  126.5 1.8 %collective-permute-done.15.got = bf16[384,384]{1,0:T(8,128)(2,1)S(1)} collective-permute-done((bf16[384,384]{1,0:T(8,128)(2,1)}, bf16[384,384]{1,0:T(8,128)(2,1)S(1)}, u32[]{:S(2)}, u32[]{:S(2)}) %collective-permute-start.15) | collective-permute-done | bytes 294944 | tf_op jit(solution)/shard_map/ppermute | solution.py:446
  129.0 5.9 %shard_map.109 = (f32[512,384]{1,0:T(8,128)}, f32[512,256]{1,0:T(8,128)}, f32[8,640]{1,0:T(8,128)}, bf16[384,384]{1,0:T(8,128)(2,1)}) custom-call(bf16[512,640]{1,0:T(8,128)(2,1)} %get-tuple-element.45.conv, f32[512,384]{1,0:T(8,128)} %get-tuple-element.46.cum, f32[4,8,128]{2,1,0:T(8,128)} %get-tuple-element.49.cum_t, ...), custom_call_target="tpu_custom_call" | custom-call | flops 100000000 | bytes 6952448 | tf_op jit(solution)/shard_map/pallas_call | solution.py:41
  134.9 4.7 %all-to-all-start.3 = ((bf16[16,24,384]{2,1,0:T(8,128)(2,1)}), bf16[16,24,384]{2,1,0:T(8,128)(2,1)S(1)}, u32[]{:S(2)}, u32[]{:S(2)}) async-start(bf16[16,24,384]{2,1,0:T(8,128)(2,1)} %bitcast.25), calls=%async_computation.3 | async-start | bytes 589824 | tf_op jit(solution)/shard_map/all_to_all | solution.py:454
  142.4 6.1 %collective-permute-done.14.leaving = bf16[128,384]{1,0:T(8,128)(2,1)S(1)} collective-permute-done((bf16[128,384]{1,0:T(8,128)(2,1)S(1)}, bf16[128,384]{1,0:T(8,128)(2,1)S(1)}, u32[]{:S(2)}, u32[]{:S(2)}) %collective-permute-start.14) | collective-permute-done | bytes 98336 | tf_op jit(solution)/shard_map/ppermute | solution.py:445
  149.1 5.0 %shard_map.110 = (f32[512,640]{1,0:T(8,128)}, bf16[128,768]{1,0:T(8,128)(2,1)}) custom-call(s32[2]{0:T(128)} %pad_add_fusion.at, bf16[512,640]{1,0:T(8,128)(2,1)} %get-tuple-element.45.conv, f32[512,384]{1,0:T(8,128)} %get-tuple-element.46.cum, bf16[4,128,384]{2,1,0:T(8,128)(2,1)} %get-tuple-element.51.full, f32[4,128,384]{2,1,0:T(8,128)} %get-tuple-element.56.ends, ...), custom_call_target="tpu_custom_call" | custom-call | flops 100000000 | bytes 8683520 | tf_op jit(solution)/shard_map/pallas_call | solution.py:41
  154.7 5.4 %shard_map.111 = (bf16[128,768]{1,0:T(8,128)(2,1)}, bf16[128,768]{1,0:T(8,128)(2,1)}, bf16[128,768]{1,0:T(8,128)(2,1)}, bf16[128,768]{1,0:T(8,128)(2,1)}) custom-call(s32[2]{0:T(128)} %pad_add_fusion.at, f32[512,640]{1,0:T(8,128)} %get-tuple-element.67.gp, f32[8,640]{1,0:T(8,128)} %copy-done.15, f32[4,640]{1,0:T(4,128)} %pad_maximum_fusion.1.conv_w, ...), custom_call_target="tpu_custom_call" | custom-call | flops 100000000 | bytes 4093952 | tf_op jit(solution)/shard_map/pallas_call | solution.py:41
  160.6 2.2 %collective-permute-start.18 = (bf16[128,768]{1,0:T(8,128)(2,1)}, bf16[128,768]{1,0:T(8,128)(2,1)S(1)}, u32[]{:S(2)}, u32[]{:S(2)}) collective-permute-start(bf16[128,768]{1,0:T(8,128)(2,1)} %get-tuple-element.74), channel_id=1, source_target_pairs={{0,64},{32,96},{64,0},{96,32},{128,192},{160,224},{192,128},{224,1... | collective-permute-start | bytes 589832 | tf_op jit(solution)/shard_map/ppermute | solution.py:357
  164.6 3.7 %all-to-all-start.4 = ((f32[8,3,384]{2,1,0:T(4,128)}), f32[8,3,384]{2,1,0:T(4,128)S(1)}, u32[]{:S(2)}, u32[]{:S(2)}) async-start(f32[8,3,384]{2,1,0:T(4,128)} %reshape.80), calls=%async_computation.4 | async-start | bytes 98304 | tf_op jit(solution)/shard_map/all_to_all | solution.py:473
  168.3 2.9 %collective-permute-done.17 = bf16[128,768]{1,0:T(8,128)(2,1)S(1)} collective-permute-done((bf16[128,768]{1,0:T(8,128)(2,1)}, bf16[128,768]{1,0:T(8,128)(2,1)S(1)}, u32[]{:S(2)}, u32[]{:S(2)}) %collective-permute-start.17) | collective-permute-done | bytes 196640 | tf_op jit(solution)/shard_map/ppermute | solution.py:357
  171.9 1.7 fusion.1
  173.6 2.5 %all-to-all-done.4 = f32[8,3,384]{2,1,0:T(4,128)S(1)} async-done(((f32[8,3,384]{2,1,0:T(4,128)}), f32[8,3,384]{2,1,0:T(4,128)S(1)}, u32[]{:S(2)}, u32[]{:S(2)}) %all-to-all-start.4) | async-done | bytes 36896 | tf_op jit(solution)/shard_map/all_to_all | solution.py:473
  (97 shorter events, 22.7 us)
Async XLA Ops:
  3.0 24.7 %all-to-all-start = ((bf16[16,24,640]{2,1,0:T(8,128)(2,1)}), bf16[16,24,640]{2,1,0:T(8,128)(2,1)S(1)}, u32[]{:S(2)}, u32[]{:S(2)}) async-start(bf16[16,24,640]{2,1,0:T(8,128)(2,1)} %get-tuple-element.44), calls=%async_computation | async-start | bytes 983040 | tf_op jit(solution)/shard_map/all_to_all | solution.py:366
  12.6 53.4 %slice-start = ((f32[4,1792]{1,0:T(4,128)}), f32[4,1536]{1,0:T(4,128)S(1)}, s32[]{:S(2)}) async-start(f32[4,1792]{1,0:T(4,128)} %param.13), calls=%async_computation.5 | async-start | bytes 49152 | tf_op jit(solution)/shard_map/slice | solution.py:402
  12.7 57.2 %copy-start.6 = (bf16[1,128,768]{2,1,0:T(8,128)(2,1)S(1)}, bf16[1,128,768]{2,1,0:T(8,128)(2,1)}, u32[]{:S(2)}) copy-start(bf16[1,128,768]{2,1,0:T(8,128)(2,1)} %param.9) | copy-start | bytes 589828
  12.7 66.1 %slice-start.1 = ((f32[4,1792]{1,0:T(4,128)}), f32[4,256]{1,0:T(4,128)S(1)}, s32[]{:S(2)}) async-start(f32[4,1792]{1,0:T(4,128)} %param.13), calls=%async_computation.6 | async-start | bytes 8192 | tf_op jit(solution)/shard_map/slice | solution.py:402
  12.8 12.3 %collective-permute-start.9 = (bf16[24,384]{1,0:T(8,128)(2,1)S(1)}, bf16[24,384]{1,0:T(8,128)(2,1)S(1)}, u32[]{:S(2)}, u32[]{:S(2)}) collective-permute-start(bf16[24,384]{1,0:T(8,128)(2,1)S(1)} %constant_dynamic-slice_fusion), channel_id=1, source_target_pairs={{0,0},{1,4},{2,8},{3,12},{4,16},{5,20},{6,24},{7,28},{8,32},{9,36}... | collective-permute-start | bytes 55304 | tf_op jit(solution)/shard_map/ppermute | solution.py:397
  27.8 51.6 %copy-start.2 = (bf16[16,24,640]{2,1,0:T(8,128)(2,1)}, bf16[16,24,640]{2,1,0:T(8,128)(2,1)S(1)}, u32[]{:S(2)}) copy-start(bf16[16,24,640]{2,1,0:T(8,128)(2,1)S(1)} %all-to-all-done.same) | copy-start | bytes 1474564
  28.7 23.7 %all-to-all-start.1 = ((bf16[16,24,768]{2,1,0:T(8,128)(2,1)}), bf16[16,24,768]{2,1,0:T(8,128)(2,1)S(1)}, u32[]{:S(2)}, u32[]{:S(2)}) async-start(bf16[16,24,768]{2,1,0:T(8,128)(2,1)} %broadcast_in_dim.29), calls=%async_computation.1 | async-start | bytes 1179648 | tf_op jit(solution)/shard_map/all_to_all | solution.py:366
  36.0 55.8 %copy-start.22 = (f32[24]{0:T(128)S(1)}, f32[24]{0:T(128)}, u32[]{:S(2)}) copy-start(f32[24]{0:T(128)} %param.14) | copy-start | bytes 292
  36.0 43.4 %collective-permute-start.4 = (bf16[16,24,640]{2,1,0:T(8,128)(2,1)S(1)}, bf16[16,24,640]{2,1,0:T(8,128)(2,1)}, u32[]{:S(2)}, u32[]{:S(2)}) collective-permute-start(bf16[16,24,640]{2,1,0:T(8,128)(2,1)S(1)} %all-to-all-done.same), channel_id=1, source_target_pairs={{0,1},{1,0},{2,3},{3,2},{4,5},{5,4},{6,7},{7,6},{8,9},{9,8},{10,11... | collective-permute-start | bytes 1474568 | tf_op jit(solution)/shard_map/ppermute | solution.py:367
  52.4 44.7 %copy-start.1 = (bf16[16,24,768]{2,1,0:T(8,128)(2,1)}, bf16[16,24,768]{2,1,0:T(8,128)(2,1)S(1)}, u32[]{:S(2)}) copy-start(bf16[16,24,768]{2,1,0:T(8,128)(2,1)S(1)} %all-to-all-done.1.same) | copy-start | bytes 1769476
  52.4 44.8 %collective-permute-start.10 = (bf16[16,24,768]{2,1,0:T(8,128)(2,1)S(1)}, bf16[16,24,768]{2,1,0:T(8,128)(2,1)S(1)}, u32[]{:S(2)}, u32[]{:S(2)}) collective-permute-start(bf16[16,24,768]{2,1,0:T(8,128)(2,1)S(1)} %all-to-all-done.1.same), channel_id=1, source_target_pairs={{0,1},{1,0},{2,3},{3,2},{4,5},{5,4},{6,7},{7,6},{8,9},{9,8},{10,11... | collective-permute-start | bytes 1769480 | tf_op jit(solution)/shard_map/ppermute | solution.py:367
  53.1 0.7 collective-permute-start
  56.4 13.5 %collective-permute-start.1 = (bf16[136,768]{1,0:T(8,128)(2,1)}, bf16[136,768]{1,0:T(8,128)(2,1)S(1)}, u32[]{:S(2)}, u32[]{:S(2)}) collective-permute-start(bf16[136,768]{1,0:T(8,128)(2,1)} %get-tuple-element.41), channel_id=1, source_target_pairs={{0,32},{32,64},{64,96},{96,0},{128,160},{160,192},{192,224},{224,1... | collective-permute-start | bytes 626696 | tf_op jit(solution)/shard_map/ppermute | solution.py:357
  57.7 19.0 %collective-permute-start.2 = (bf16[136,768]{1,0:T(8,128)(2,1)}, bf16[136,768]{1,0:T(8,128)(2,1)S(1)}, u32[]{:S(2)}, u32[]{:S(2)}) collective-permute-start(bf16[136,768]{1,0:T(8,128)(2,1)} %get-tuple-element.42), channel_id=1, source_target_pairs={{0,64},{32,96},{64,0},{96,32},{128,192},{160,224},{192,128},{224,1... | collective-permute-start | bytes 626696 | tf_op jit(solution)/shard_map/ppermute | solution.py:357
  66.0 10.7 %collective-permute-start.3 = (bf16[136,768]{1,0:T(8,128)(2,1)}, bf16[136,768]{1,0:T(8,128)(2,1)S(1)}, u32[]{:S(2)}, u32[]{:S(2)}) collective-permute-start(bf16[136,768]{1,0:T(8,128)(2,1)} %get-tuple-element.43), channel_id=1, source_target_pairs={{0,96},{32,0},{64,32},{96,64},{128,224},{160,128},{192,160},{224,1... | collective-permute-start | bytes 626696 | tf_op jit(solution)/shard_map/ppermute | solution.py:357
  69.9 27.2 %collective-permute-start.6 = (bf16[128,768]{1,0:T(8,128)(2,1)S(1)}, bf16[128,768]{1,0:T(8,128)(2,1)S(1)}, u32[]{:S(2)}, u32[]{:S(2)}) collective-permute-start(bf16[128,768]{1,0:T(8,128)(2,1)S(1)} %bitcast.22), channel_id=1, source_target_pairs={{0,32},{32,64},{64,96},{96,0},{128,160},{160,192},{192,224},{224,1... | collective-permute-start | bytes 589832 | tf_op jit(solution)/shard_map/ppermute | solution.py:357
  76.7 20.4 %collective-permute-start.7 = (bf16[128,768]{1,0:T(8,128)(2,1)S(1)}, bf16[128,768]{1,0:T(8,128)(2,1)S(1)}, u32[]{:S(2)}, u32[]{:S(2)}) collective-permute-start(bf16[128,768]{1,0:T(8,128)(2,1)S(1)} %bitcast.23), channel_id=1, source_target_pairs={{0,64},{32,96},{64,0},{96,32},{128,192},{160,224},{192,128},{224,1... | collective-permute-start | bytes 589832 | tf_op jit(solution)/shard_map/ppermute | solution.py:357
  76.7 20.4 %collective-permute-start.8 = (bf16[128,768]{1,0:T(8,128)(2,1)S(1)}, bf16[128,768]{1,0:T(8,128)(2,1)S(1)}, u32[]{:S(2)}, u32[]{:S(2)}) collective-permute-start(bf16[128,768]{1,0:T(8,128)(2,1)S(1)} %bitcast.24), channel_id=1, source_target_pairs={{0,96},{32,0},{64,32},{96,64},{128,224},{160,128},{192,160},{224,1... | collective-permute-start | bytes 589832 | tf_op jit(solution)/shard_map/ppermute | solution.py:357
  85.1 12.1 %collective-permute-start.5 = (bf16[128,384]{1,0:T(8,128)(2,1)}, bf16[128,384]{1,0:T(8,128)(2,1)S(1)}, u32[]{:S(2)}, u32[]{:S(2)}) collective-permute-start(bf16[128,384]{1,0:T(8,128)(2,1)} %get-tuple-element.48), channel_id=1, source_target_pairs={{0,128},{32,160},{64,192},{96,224},{1,129},{33,161},{65,193},{97,2... | collective-permute-start | bytes 294920 | tf_op jit(solution)/shard_map/ppermute | solution.py:421
  104.8 30.1 %all-to-all-start.2 = ((bf16[4,128,768]{2,1,0:T(8,128)(2,1)}), bf16[4,128,768]{2,1,0:T(8,128)(2,1)S(1)}, u32[]{:S(2)}, u32[]{:S(2)}) async-start(bf16[4,128,768]{2,1,0:T(8,128)(2,1)} %get-tuple-element.64), calls=%async_computation.2 | async-start | bytes 1572864 | tf_op jit(solution)/shard_map/all_to_all | solution.py:360
  108.9 9.0 %collective-permute-start.11 = (f32[2,512]{1,0:T(2,128)S(1)}, f32[2,512]{1,0:T(2,128)S(1)}, u32[]{:S(2)}, u32[]{:S(2)}) collective-permute-start(f32[2,512]{1,0:T(2,128)S(1)} %copy-done.16), channel_id=1, source_target_pairs={{0,32},{32,64},{64,96},{96,0},{128,160},{160,192},{192,224},{224,1... | collective-permute-start | bytes 12296 | tf_op jit(solution)/shard_map/ppermute | solution.py:357
  111.0 9.1 %collective-permute-start.12 = (f32[2,512]{1,0:T(2,128)S(1)}, f32[2,512]{1,0:T(2,128)S(1)}, u32[]{:S(2)}, u32[]{:S(2)}) collective-permute-start(f32[2,512]{1,0:T(2,128)S(1)} %copy-done.16), channel_id=1, source_target_pairs={{0,64},{32,96},{64,0},{96,32},{128,192},{160,224},{192,128},{224,1... | collective-permute-start | bytes 12296 | tf_op jit(solution)/shard_map/ppermute | solution.py:357
  113.7 6.4 %collective-permute-start.13 = (f32[2,512]{1,0:T(2,128)S(1)}, f32[2,512]{1,0:T(2,128)S(1)}, u32[]{:S(2)}, u32[]{:S(2)}) collective-permute-start(f32[2,512]{1,0:T(2,128)S(1)} %copy-done.16), channel_id=1, source_target_pairs={{0,96},{32,0},{64,32},{96,64},{128,224},{160,128},{192,160},{224,1... | collective-permute-start | bytes 12296 | tf_op jit(solution)/shard_map/ppermute | solution.py:357
  126.5 1.8 %collective-permute-start.15 = (bf16[384,384]{1,0:T(8,128)(2,1)}, bf16[384,384]{1,0:T(8,128)(2,1)S(1)}, u32[]{:S(2)}, u32[]{:S(2)}) collective-permute-start(bf16[384,384]{1,0:T(8,128)(2,1)} %get-tuple-element.61), channel_id=1, source_target_pairs={{0,1},{1,0},{2,3},{3,2},{4,5},{5,4},{6,7},{7,6},{8,9},{9,8},{10,11... | collective-permute-start | bytes 884744 | tf_op jit(solution)/shard_map/ppermute | solution.py:446
  134.9 13.6 %copy-start = (bf16[4,128,768]{2,1,0:T(8,128)(2,1)}, bf16[4,128,768]{2,1,0:T(8,128)(2,1)S(1)}, u32[]{:S(2)}) copy-start(bf16[4,128,768]{2,1,0:T(8,128)(2,1)S(1)} %all-to-all-done.2.parts) | copy-start | bytes 2359300
  134.9 29.1 %all-to-all-start.3 = ((bf16[16,24,384]{2,1,0:T(8,128)(2,1)}), bf16[16,24,384]{2,1,0:T(8,128)(2,1)S(1)}, u32[]{:S(2)}, u32[]{:S(2)}) async-start(bf16[16,24,384]{2,1,0:T(8,128)(2,1)} %bitcast.25), calls=%async_computation.3 | async-start | bytes 589824 | tf_op jit(solution)/shard_map/all_to_all | solution.py:454
  139.6 8.9 %collective-permute-start.14 = (bf16[128,384]{1,0:T(8,128)(2,1)S(1)}, bf16[128,384]{1,0:T(8,128)(2,1)S(1)}, u32[]{:S(2)}, u32[]{:S(2)}) collective-permute-start(bf16[128,384]{1,0:T(8,128)(2,1)S(1)} %copy-done.20), channel_id=1, source_target_pairs={{128,0},{160,32},{192,64},{224,96},{129,1},{161,33},{193,65},{225,... | collective-permute-start | bytes 294920 | tf_op jit(solution)/shard_map/ppermute | solution.py:445
  140.9 13.2 %collective-permute-start.16 = (f32[8,640]{1,0:T(8,128)}, f32[8,640]{1,0:T(8,128)S(1)}, u32[]{:S(2)}, u32[]{:S(2)}) collective-permute-start(f32[8,640]{1,0:T(8,128)} %get-tuple-element.68), channel_id=1, source_target_pairs={{128,0},{160,32},{192,64},{224,96},{129,1},{161,33},{193,65},{225,... | collective-permute-start | bytes 61448 | tf_op jit(solution)/shard_map/ppermute | solution.py:453
  160.2 11.1 %collective-permute-start.17 = (bf16[128,768]{1,0:T(8,128)(2,1)}, bf16[128,768]{1,0:T(8,128)(2,1)S(1)}, u32[]{:S(2)}, u32[]{:S(2)}) collective-permute-start(bf16[128,768]{1,0:T(8,128)(2,1)} %get-tuple-element.73), channel_id=1, source_target_pairs={{0,32},{32,64},{64,96},{96,0},{128,160},{160,192},{192,224},{224,1... | collective-permute-start | bytes 589832 | tf_op jit(solution)/shard_map/ppermute | solution.py:357
  160.6 10.6 %collective-permute-start.18 = (bf16[128,768]{1,0:T(8,128)(2,1)}, bf16[128,768]{1,0:T(8,128)(2,1)S(1)}, u32[]{:S(2)}, u32[]{:S(2)}) collective-permute-start(bf16[128,768]{1,0:T(8,128)(2,1)} %get-tuple-element.74), channel_id=1, source_target_pairs={{0,64},{32,96},{64,0},{96,32},{128,192},{160,224},{192,128},{224,1... | collective-permute-start | bytes 589832 | tf_op jit(solution)/shard_map/ppermute | solution.py:357
  162.8 9.0 %collective-permute-start.19 = (bf16[128,768]{1,0:T(8,128)(2,1)}, bf16[128,768]{1,0:T(8,128)(2,1)S(1)}, u32[]{:S(2)}, u32[]{:S(2)}) collective-permute-start(bf16[128,768]{1,0:T(8,128)(2,1)} %get-tuple-element.75), channel_id=1, source_target_pairs={{0,96},{32,0},{64,32},{96,64},{128,224},{160,128},{192,160},{224,1... | collective-permute-start | bytes 589832 | tf_op jit(solution)/shard_map/ppermute | solution.py:357
  164.6 11.5 %all-to-all-start.4 = ((f32[8,3,384]{2,1,0:T(4,128)}), f32[8,3,384]{2,1,0:T(4,128)S(1)}, u32[]{:S(2)}, u32[]{:S(2)}) async-start(f32[8,3,384]{2,1,0:T(4,128)} %reshape.80), calls=%async_computation.4 | async-start | bytes 98304 | tf_op jit(solution)/shard_map/all_to_all | solution.py:473
  (18 other events, 51.5 us)

commit v2 on v1

--- a/solution.py
+++ b/solution.py
@@ -32,11 +32,9 @@
     return 0.5 + 0.5 * jnp.tanh(0.5 * v)
 
 
-def kernel_call(body, outs, *args, scalars=None, scratch=(), flops=10**8, limit=None):
+def kernel_call(body, outs, *args, scalars=None, scratch=(), flops=10**8):
     spec = pl.BlockSpec(memory_space=pltpu.VMEM)
-    size = sum(a.size * a.dtype.itemsize for a in args) + sum(
-        o.size * o.dtype.itemsize for o in outs
-    )
+    size = sum(a.size * a.dtype.itemsize for a in list(args) + list(outs))
     first = [] if scalars is None else [scalars]
     return pl.pallas_call(
         body,
@@ -44,7 +42,7 @@
         in_specs=[pl.BlockSpec(memory_space=pltpu.SMEM)] * len(first) + [spec] * len(args),
         out_specs=[spec] * len(outs),
         scratch_shapes=list(scratch),
-        compiler_params=pltpu.CompilerParams(vmem_limit_bytes=limit or LIMIT),
+        compiler_params=pltpu.CompilerParams(vmem_limit_bytes=LIMIT),
         cost_estimate=pl.CostEstimate(flops=flops, bytes_accessed=size, transcendentals=0),
     )(*first, *args)
 
@@ -91,7 +89,7 @@
     gate_w[...] = in_w[:, pl.ds(start, width)]
 
 
-def pack(at, logs, tokens, halo, aux, send1, send2, send3, decays):
+def pack(at, logs, tokens, cotangent, halo, aux, send1, send2, send3, decays):
     block = logs.shape[1]
     step = lax.broadcasted_iota(jnp.int32, (block, block), 0)
     upto = (step <= lax.broadcasted_iota(jnp.int32, (block, block), 1)).astype(f32)
@@ -111,7 +109,8 @@
     aux[...] = (decays[at[0]] + tail).astype(bf16)
     for r, send in enumerate((send1, send2, send3)):
         send[:block, :] = tokens[...]
-        send[block:, :] = (decays[lax.rem(at[0] + r + 1, XS)] + tail).astype(bf16)
+        send[block : 2 * block, :] = cotangent[...]
+        send[2 * block :, :] = (decays[lax.rem(at[0] + r + 1, XS)] + tail).astype(bf16)
 
 
 def assemble(at, same, other, target, lanes):
@@ -132,7 +131,7 @@
     for r, source in enumerate((None, recv1, recv2, recv3)):
         c, _ = place(at, r)
         t = tokens[...] if r == 0 else source[:block, :]
-        extra = (aux[...] if r == 0 else source[block:, :]).astype(f32)
+        extra = (aux[...] if r == 0 else source[2 * block :, :]).astype(f32)
         halo = halo + extra
         mix[pl.ds(pl.multiple_of(8 + c * block, 8), block), :] = (
             dot(t, w_mix[...]).astype(bf16).astype(f32)
@@ -156,7 +155,7 @@
             for k in range(4):
                 start = 5 + k + c * CHUNK
                 value = value + conv_w[k : k + 1, s] * mix[start : start + CHUNK, s]
-            pre[r, s] = value
+            pre[r, s] = value.astype(bf16)
             conv[r, s] = (value * sig(value)).astype(bf16)
         states[c] = state.astype(bf16)
         end = cum[(c + 1) * CHUNK - 1 : (c + 1) * CHUNK, :]
@@ -180,11 +179,10 @@
                 axis=1,
             )
             both = jnp.concatenate([jnp.where(left, x, 0.0), jnp.where(left, 0.0, x)], axis=0)
-            y[r, s] = dot(weight, both) + dskip[:, s] * x
-
-
-def gated(at, conv, cum, states, entering, y_in, tok0, tok1, tok2, tok3, cot0, cot1, cot2, cot3,
-          same, other, norm_w,
+            y[r, s] = (dot(weight, both) + dskip[:, s] * x).astype(y.dtype)
+
+
+def gated(at, conv, cum, states, entering, y_in, tok0, cot0, tok1, tok2, tok3, same, other, norm_w,
           y, full, gate, dn, part, stats, w_gate, raw, w_out):
     width = y.shape[1]
     chunks = y.shape[0] // CHUNK
@@ -194,10 +192,11 @@
         for k in range(2):
             lanes = slice(k * width + p * LANES, k * width + (p + 1) * LANES)
             w_out[:, lanes] = raw[p, pl.ds(k, width, stride=2), :].astype(bf16)
-    for r, (tok, cot) in enumerate(((tok0, cot0), (tok1, cot1), (tok2, cot2), (tok3, cot3))):
+    for r, tok in enumerate((tok0, tok1, tok2, tok3)):
         here = place(at, r)[1]
         gate[here, :] = dot(tok[:CHUNK, :], w_gate[...]).astype(bf16)
-        dn[here, :] = dot(cot[...], w_out[...], NT) * norm_w[...]
+        cot = cot0[...] if r == 0 else tok[CHUNK : 2 * CHUNK, :]
+        dn[here, :] = (dot(cot, w_out[...], NT) * norm_w[...]).astype(dn.dtype)
     carried = entering[...].astype(f32)
     ones = jnp.ones((8, LANES), f32)
     for c in range(chunks):
@@ -205,12 +204,12 @@
         state = states[c].astype(f32) + carried
         full[c] = state.astype(bf16)
         carried = jnp.exp(cum[(c + 1) * CHUNK - 1 : (c + 1) * CHUNK, :]) * carried
-        value = y_in[r, :] + jnp.exp(cum[r, :]) * dot(conv[r, width + 128 : width + 256], state)
+        value = y_in[r, :].astype(f32) + jnp.exp(cum[r, :]) * dot(conv[r, width + 128 : width + 256], state)
         y[r, :] = value
         z = gate[r, :].astype(f32)
         g = value * z * sig(z)
         part[c] = dot(g * norm_w[...], w_out[...]).astype(bf16)
-        squares, cross = g * g, g * dn[r, :]
+        squares, cross = g * g, g * dn[r, :].astype(f32)
         squares = sum(squares[:, lanes_of(p)] for p in range(width // LANES))
         cross = sum(cross[:, lanes_of(p)] for p in range(width // LANES))
         stats[0:1, r] = exact(ones, squares, NT)[0:1]
@@ -235,25 +234,24 @@
         value = y[r, :]
         g = value * z * q
         low[r, :] = (g * factor * norm_w[...]).astype(bf16)
-        dg = factor * (dn[r, :] - g * lean)
+        dg = factor * (dn[r, :].astype(f32) - g * lean)
         dvalue = dg * z * q
-        dy[r, :] = dvalue
+        dy[r, :] = dvalue.astype(bf16)
         dgate[r, :] = (dg * value * q * (1.0 + z * (1.0 - q))).astype(bf16)
-        ends[c] = adjoint
+        ends[c] = adjoint.astype(bf16)
         end = cum[(c + 1) * CHUNK - 1 : (c + 1) * CHUNK, :]
         adjoint = jnp.exp(end) * adjoint + dot(
             conv[r, width + 128 : width + 256], jnp.exp(cum[r, :]) * dvalue, TN
         )
     first[...] = adjoint.astype(bf16)
     for r, source in enumerate((cot0, cot1, cot2, cot3)):
-        cot[place(at, r)[1], :] = source[...]
+        cot[place(at, r)[1], :] = source[...] if r == 0 else source[CHUNK : 2 * CHUNK, :]
     summed = dot(cot[...], low[...], TN)
+    give[...] = dot(perm[keep.shape[0] :, :], summed).astype(bf16)
     keep[...] = dot(perm[: keep.shape[0], :], summed).astype(bf16)
-    give[...] = dot(perm[keep.shape[0] :, :], summed).astype(bf16)
-
-
-def inside_back(conv, cum, cum_t, dskip, dy, full, ends, pre, keep, got, dx, dbc, head, pair):
-    pair[...] = (keep[...].astype(f32) + got[...].astype(f32)).astype(bf16)
+
+
+def inside_back(conv, cum, cum_t, dskip, dy, full, ends, pre, dx, dbc, head):
     width = dy.shape[1]
     left = halves()
     for c in range(dy.shape[0] // CHUNK):
@@ -264,14 +262,16 @@
         for p in range(width // LANES):
             s = lanes_of(p)
             x = conv[r, s]
-            d = dy[r, s]
+            d = dy[r, s].astype(f32)
             da, db = jnp.where(left, d, 0.0), jnp.where(left, 0.0, d)
             fa, fb = fades(cum, cum_t, c, 2 * p), fades(cum, cum_t, c, 2 * p + 1)
             weight = jnp.concatenate([fa * scores, fb * scores], axis=0)
-            dx[r, s] = dot(weight, jnp.concatenate([da, db], axis=0), TN) + dskip[:, s] * d
+            dx[r, s] = (
+                dot(weight, jnp.concatenate([da, db], axis=0), TN) + dskip[:, s] * d
+            ).astype(dx.dtype)
             dscores = dscores + fa * dot(da, x, NT) + fb * dot(db, x, NT)
-        dbc[r, :128] = dot(dscores, cv, TN)
-        dbc[r, 128:] = dot(dscores, b)
+        dbc[r, :128] = dot(dscores, cv, TN).astype(dbc.dtype)
+        dbc[r, 128:] = dot(dscores, b).astype(dbc.dtype)
     first = conv_rows(conv, cum, full[0], ends[0], dy, dx, dbc, pre, 0, 16)
     for lanes, value in first:
         head[:, lanes] = value[:8]
@@ -284,14 +284,14 @@
     fade = jnp.exp(cum[chunk_end - 1 : chunk_end, :] - cum[r, :])
     grad_x = dx[r, :] + fade * dot(conv[r, width : width + 128], adjoint)
     grad_b = dbc[r, :128] + dot(fade * conv[r, :width].astype(f32), adjoint, NT)
-    grad_c = dbc[r, 128:] + dot(jnp.exp(cum[r, :]) * dy[r, :], state, NT)
+    grad_c = dbc[r, 128:] + dot(jnp.exp(cum[r, :]) * dy[r, :].astype(f32), state, NT)
     result = []
     for lanes, grad in (
         (slice(0, width), grad_x),
         (slice(width, width + 128), grad_b),
         (slice(width + 128, width + 256), grad_c),
     ):
-        v = pre[r, lanes]
+        v = pre[r, lanes].astype(f32)
         q = sig(v)
         result.append((lanes, grad * q * (1.0 + v * (1.0 - q))))
     return result
@@ -301,12 +301,12 @@
     chunks = dy.shape[0] // CHUNK
     carried = leaving[...].astype(f32)
     for c in reversed(range(chunks)):
-        adjoint = ends[c] + carried
+        adjoint = ends[c].astype(f32) + carried
         end = cum[(c + 1) * CHUNK - 1 : (c + 1) * CHUNK, :]
         carried = jnp.exp(end) * carried
         rows = conv_rows(conv, cum, full[c], adjoint, dy, dx, dbc, pre, c * CHUNK, CHUNK)
         for lanes, value in rows:
-            gp[rows_of(c), lanes] = value
+            gp[rows_of(c), lanes] = value.astype(gp.dtype)
     factor = factors[at[0]]
     for p in range(result.shape[1] // LANES):
         s = lanes_of(p)
@@ -314,11 +314,12 @@
         result[:, s] = (total * factor).astype(bf16)
 
 
-def token_grad(at, gp, after, conv_w, dgate, w_gate, w_mix, own, to1, to2, to3, long, low):
+def token_grad(at, gp, after, conv_w, dgate, w_gate, w_mix, pieces,
+               own, to1, to2, to3, own_dw, long, low, dws):
     rows = gp.shape[0]
-    long[:rows, :] = gp[...]
     long[rows:, :] = after[...]
-    for c in range(rows // CHUNK):
+    for c in reversed(range(rows // CHUNK)):
+        long[rows_of(c), :] = gp[rows_of(c), :].astype(f32)
         for p in range(gp.shape[1] // LANES):
             s = lanes_of(p)
             value = jnp.zeros((CHUNK, LANES), f32)
@@ -326,12 +327,34 @@
                 start = c * CHUNK + 3 - k
                 value = value + conv_w[k : k + 1, s] * long[start : start + CHUNK, s]
             low[rows_of(c), s] = value.astype(bf16)
-    for r, target in enumerate((own, to1, to2, to3)):
+    total = sum(pieces[i].astype(f32) for i in range(pieces.shape[0]))
+    width = total.shape[1]
+    dws[...] = jnp.zeros(dws.shape, f32)
+    for x in range(XS):
+        dws[x, 0:3, :width] = total[3 * x : 3 * x + 3]
+    own_dw[...] = dws[at[0], :, :width]
+    for r, target in ((2, to2), (1, to1), (3, to3), (0, own)):
         c = lax.rem(at[0] + r, XS)
         here = pl.ds(pl.multiple_of(c * CHUNK, CHUNK), CHUNK)
-        target[...] = (
+        target[:CHUNK, :] = (
             dot(dgate[here, :], w_gate[...], NT) + dot(low[here, :], w_mix[...], NT)
         ).astype(bf16)
+        if r:
+            target[CHUNK:, :] = dws[c].astype(bf16)
+
+
+def finish(scale, at, own, own_dw, got1, got2, got3, tokens, dw):
+    width = own_dw.shape[1]
+    for r, got in enumerate((own_dw, got1, got2, got3)):
+        lanes = pl.ds(pl.multiple_of(place(at, r)[0] * width, width), width)
+        rows = got[...] if r == 0 else got[CHUNK:, :width].astype(f32)
+        dw[:, lanes] = rows[0:3] * scale
+    for p in range(tokens.shape[1] // LANES):
+        s = lanes_of(p)
+        value = own[:, s].astype(f32)
+        for got in (got1, got2, got3):
+            value = value + got[:CHUNK, s].astype(f32)
+        tokens[:, s] = value.astype(bf16)
 
 
 def shards(tokens, cotangent, decay, in_w, out_w, conv_w, dskip, norm_w):
@@ -379,14 +402,13 @@
     same1, other1 = gather_weights(wide1)
     aux, *sends = kernel_call(
         pack,
-        [out((8, model), bf16)] + [out((block + 8, model), bf16)] * (XS - 1),
-        decay[0].T, tokens[0], halo,
+        [out((8, model), bf16)] + [out((2 * block + 8, model), bf16)] * (XS - 1),
+        decay[0].T, tokens[0], cotangent[0], halo,
         scalars=at, scratch=[pltpu.VMEM((XS, 8, model), f32)],
     )
-    toks, cots = [tokens[0]], [cotangent[0]]
+    recv = []
     for r in range(1, XS):
-        toks.append(along_x(sends[r - 1], r))
-        cots.append(along_x(cotangent[0], r))
+        recv.append(along_x(sends[r - 1], r))
     piece = 2 * out_w.shape[0] // XS
     routes = []
     for t in range(tm):
@@ -403,18 +425,21 @@
     gain = own(norm_w, 0, width)[None]
     skip = jnp.repeat(own(dskip, 0, part_heads), width // part_heads)[None]
     index = jnp.arange(model)
-    late, spot = index // (model // 2), index % (model // 2)
-    target = 2 * (spot // (3 * tm)) + jnp.where(late == 0, core, 1 - core)
-    source = index // 3 % tm * (3 * stream) + target * 3 + index % 3
+    quarter = model // 4
+    late, far = index // (2 * quarter), index // quarter % 2
+    target = 2 * (index % quarter // (3 * XS)) + jnp.where(late == 0, core, 1 - core)
+    side = me_t // XS
+    target_t = index // 3 % XS + XS * jnp.where(far == 0, side, 1 - side)
+    source = target_t * (3 * stream) + target * 3 + index % 3
     perm = (source[:, None] == index[None, :]).astype(bf16)
 
     chunks = rows // CHUNK
     w_mix, cum, cum_t, pre, conv, states, last = kernel_call(
         project,
         [out((model, mixed), bf16), out((rows, width), f32), out((chunks, 8, CHUNK), f32),
-         out((rows, mixed), f32), out((rows, mixed), bf16), out((chunks, state, width), bf16),
+         out((rows, mixed), bf16), out((rows, mixed), bf16), out((chunks, state, width), bf16),
          out((state, width), bf16)],
-        tokens[0], aux, *toks[1:], same1, other1, taps,
+        tokens[0], aux, *recv, same1, other1, taps,
         scalars=at,
         scratch=[pltpu.VMEM((rows + 8, mixed), f32)],
     )
@@ -423,9 +448,9 @@
     y, full, gate, dn, part, stats, w_gate = kernel_call(
         gated,
         [out((rows, width), f32), out(states.shape, bf16), out((rows, width), bf16),
-         out((rows, width), f32), out((XS, block, model), bf16), out((2, rows), f32),
+         out((rows, width), bf16), out((XS, block, model), bf16), out((2, rows), f32),
          out((model, width), bf16)],
-        conv, cum, states, entering, y_in, *toks, *cots, same2, other2, gain,
+        conv, cum, states, entering, y_in, tokens[0], cotangent[0], *recv, same2, other2, gain,
         scalars=at,
         scratch=[pltpu.VMEM((width // LANES, model, LANES), f32), pltpu.VMEM((width, model), bf16)],
     )
@@ -435,45 +460,51 @@
     parts = swap_x(part)
     factors, dgate, dy, ends, first, keep, give = kernel_call(
         functools.partial(normed_part, inner),
-        [out((chunks, CHUNK, LANES), f32), out((rows, width), bf16), out((rows, width), f32),
-         out(states.shape, f32), out((state, width), bf16), out((model // 2, width), bf16),
+        [out((chunks, CHUNK, LANES), f32), out((rows, width), bf16), out((rows, width), bf16),
+         out(states.shape, bf16), out((state, width), bf16), out((model // 2, width), bf16),
          out((model // 2, width), bf16)],
-        y, gate, dn, stats, *others, conv, cum, gain, *cots, perm,
+        y, gate, dn, stats, *others, conv, cum, gain, cotangent[0], *recv, perm,
         scalars=at,
         scratch=[pltpu.VMEM((rows, width), bf16), pltpu.VMEM((rows, model), bf16)],
     )
     leaving = lax.ppermute(first, "tm", down)
     got = lax.ppermute(give, "stream", [(i, i ^ 1) for i in range(stream)])
-    dx, dbc, head, pair = kernel_call(
+    pair = keep.astype(f32) + got.astype(f32)
+    swap = [(i, (i + XS) % tm) for i in range(tm)]
+    crossed = lax.ppermute(pair[quarter:].astype(bf16), "tm", swap)
+    dx, dbc, head = kernel_call(
         inside_back,
-        [out((rows, width), f32), out((rows, 2 * state), f32), out((8, mixed), f32),
-         out(keep.shape, bf16)],
-        conv, cum, cum_t, skip, dy, full, ends, pre, keep, got,
+        [out((rows, width), bf16), out((rows, 2 * state), bf16), out((8, mixed), f32)],
+        conv, cum, cum_t, skip, dy, full, ends, pre,
     )
     after = lax.ppermute(head, "tm", down)
+    pair = (pair[:quarter] + crossed.astype(f32)).astype(bf16)
     pieces = lax.all_to_all(pair.reshape(half, -1, width), "stream", 0, 0, axis_index_groups=cores)
     gp, result = kernel_call(
         conv_grad,
-        [out((rows, mixed), f32), out((block, model), bf16)],
+        [out((rows, mixed), bf16), out((block, model), bf16)],
         conv, cum, full, ends, leaving, dy, dx, dbc, pre, parts, factors,
         scalars=at,
     )
-    token_parts = kernel_call(
+    *token_parts, own_dw = kernel_call(
         token_grad,
-        [out((block, model), bf16)] * XS,
-        gp, after, taps, dgate, w_gate, w_mix,
+        [out((block, model), bf16)] + [out((block + 8, model), bf16)] * (XS - 1)
+        + [out((8, width), f32)],
+        gp, after, taps, dgate, w_gate, w_mix, pieces,
         scalars=at,
-        scratch=[pltpu.VMEM((rows + 8, mixed), f32), pltpu.VMEM((rows, mixed), bf16)],
-    )
-    moved = []
-    for r in range(1, XS):
-        moved.append(along_x(token_parts[r], r))
-    grad_tokens = sum((p.astype(f32) for p in moved), token_parts[0].astype(f32)).astype(bf16)
-    summed = pieces.astype(f32).sum(axis=0).reshape(tm, 3, width)
-    swapped = lax.all_to_all(summed, "tm", 0, 0)
-    swapped = swapped.reshape(tm // XS, XS, 3, width).sum(axis=0)
+        scratch=[pltpu.VMEM((rows + 8, mixed), f32), pltpu.VMEM((rows, mixed), bf16),
+                 pltpu.VMEM((XS, 8, model), f32)],
+    )
+    moved = {}
+    for r in (2, 1, 3):
+        moved[r] = along_x(token_parts[r], r)
     scale = (stream * tm * block) ** (-0.5)
-    grad_out_t = jnp.transpose(swapped, (1, 0, 2)).reshape(3, inner) * scale
+    grad_tokens, grad_out_t = kernel_call(
+        functools.partial(finish, scale),
+        [out((block, model), bf16), out((3, inner), f32)],
+        token_parts[0], own_dw, moved[1], moved[2], moved[3],
+        scalars=at,
+    )
     return (result[None], grad_tokens[None], grad_out_t)
 
 

time: 178 us -> 181 us (1.017)
  waiting for transfers between devices: 52.4 us -> 60.4 us
  starting transfers between devices: 67.9 us -> 62.5 us
  other arithmetic: 5.65 us -> 2.62 us
    ppermute x12 -> x9, waiting for transfers between devices: 17.9 us -> 25.4 us  [along_x(): return lax.ppermute(array, 'tm', pairs)]
    ppermute x1, waiting for transfers between devices: 6.06 us -> 0.81 us  [shards(): leaving = lax.ppermute(first, 'tm', down)]
    ppermute x12 -> x9, starting transfers between devices: 21.7 us -> 17.1 us  [along_x(): return lax.ppermute(array, 'tm', pairs)]
    all_to_all x1, waiting for transfers between devices: 0.01 us -> 4.52 us  [swap_x(): return lax.all_to_all(array, 'tm', 0, 0, axis_index_groups=x_groups)]
    ppermute x0 -> x1, waiting for transfers between devices: none -> 4.37 us  [shards(): crossed = lax.ppermute(pair[quarter:].astype(bf16), 'tm', swap)]
    all_to_all x1 -> x0, starting transfers between devices: 3.66 us -> none  [shards(): swapped = lax.all_to_all(summed, 'tm', 0, 0)]
    ppermute x0 -> x1, starting transfers between devices: none -> 3.18 us  [shards(): crossed = lax.ppermute(pair[quarter:].astype(bf16), 'tm', swap)]
    all_to_all x1 -> x0, waiting for transfers between devices: 2.53 us -> none  [shards(): swapped = lax.all_to_all(summed, 'tm', 0, 0)]
  transfers between devices with their start and end apart: 25 -> 22, of which waited for: 12 -> 13; matrix products, arithmetic and copies ran while one was open for 4% -> 3% of each run, Pallas kernels for 19% -> 12%
where the time goes in v2:
time: 181 us; the launch traced here: 179 us
  starting transfers between devices  62.5 us (35%)
  waiting for transfers between devices  60.4 us (33%)
  Pallas kernels  42.4 us (23%)
  local copies, waits for them, and re-layouts  9.71 us (5%)
  other arithmetic  2.62 us (1%)
    pallas_call x10, Pallas kernels, kernel_call(): pl.pallas_call(body, out_shape=outs, in_specs=[pl.BlockSpec(memory_space=...  42.4 us
    ppermute x9, waiting for transfers between devices, along_x(): return lax.ppermute(array, 'tm', pairs)  25.4 us
    all_to_all x2, waiting for transfers between devices, gather_weights(): same = lax.all_to_all(wide, 'stream', 0, 0, axis_index_groups=cores)  19 us
    ppermute x9, starting transfers between devices, along_x(): return lax.ppermute(array, 'tm', pairs)  17.1 us
    all_to_all x2, starting transfers between devices, gather_weights(): same = lax.all_to_all(wide, 'stream', 0, 0, axis_index_groups=cores)  16.3 us
    ppermute x1, starting transfers between devices, shards(): entering = lax.ppermute(last, 'tm', up)  7.08 us
    ppermute x1, starting transfers between devices, shards(): lax.ppermute(own(out_w.reshape(-1, width), 0, piece), ('tm', 'stream'), r...  6.38 us
    ppermute x1, waiting for transfers between devices, shards(): lax.ppermute(own(out_w.reshape(-1, width), 0, piece), ('tm', 'stream'), r...  5.99 us
  transfers between devices with their start and end apart: 22, of which 13 were waited for; matrix products, arithmetic and copies ran while one was open for 3% of the time, Pallas kernels for 12%

profile of v2, /device:TPU:32, one launch (start us, length us, event | category | flops | bytes accessed | tf_op | source)
XLA Modules:
  0.0 178.6 jit_solution(15974885436728212263)
XLA Ops:
  1.2 1.8 shard_map.104
  3.0 9.7 %all-to-all-start = ((bf16[16,24,640]{2,1,0:T(8,128)(2,1)}), bf16[16,24,640]{2,1,0:T(8,128)(2,1)S(1)}, u32[]{:S(2)}, u32[]{:S(2)}) async-start(bf16[16,24,640]{2,1,0:T(8,128)(2,1)} %get-tuple-element.46), calls=%async_computation | async-start | bytes 983040 | tf_op jit(solution)/shard_map/all_to_all | solution.py:389
  12.8 6.4 %collective-permute-start.6 = (bf16[24,384]{1,0:T(8,128)(2,1)S(1)}, bf16[24,384]{1,0:T(8,128)(2,1)S(1)}, u32[]{:S(2)}, u32[]{:S(2)}) collective-permute-start(bf16[24,384]{1,0:T(8,128)(2,1)S(1)} %constant_dynamic-slice_fusion), channel_id=1, source_target_pairs={{0,0},{1,4},{2,8},{3,12},{4,16},{5,20},{6,24},{7,28},{8,32},{9,36}... | collective-permute-start | bytes 55304 | tf_op jit(solution)/shard_map/ppermute | solution.py:419
  19.2 6.0 %collective-permute-done.6 = bf16[24,384]{1,0:T(8,128)(2,1)S(1)} collective-permute-done((bf16[24,384]{1,0:T(8,128)(2,1)S(1)}, bf16[24,384]{1,0:T(8,128)(2,1)S(1)}, u32[]{:S(2)}, u32[]{:S(2)}) %collective-permute-start.6) | collective-permute-done | bytes 18464 | tf_op jit(solution)/shard_map/ppermute | solution.py:419
  25.2 2.7 %all-to-all-done.same = bf16[16,24,640]{2,1,0:T(8,128)(2,1)S(1)} async-done(((bf16[16,24,640]{2,1,0:T(8,128)(2,1)}), bf16[16,24,640]{2,1,0:T(8,128)(2,1)S(1)}, u32[]{:S(2)}, u32[]{:S(2)}) %all-to-all-start) | async-done | bytes 491552 | tf_op jit(solution)/shard_map/all_to_all | solution.py:389
  28.8 6.5 %all-to-all-start.1 = ((bf16[16,24,768]{2,1,0:T(8,128)(2,1)}), bf16[16,24,768]{2,1,0:T(8,128)(2,1)S(1)}, u32[]{:S(2)}, u32[]{:S(2)}) async-start(bf16[16,24,768]{2,1,0:T(8,128)(2,1)} %broadcast_in_dim.35), calls=%async_computation.1 | async-start | bytes 1179648 | tf_op jit(solution)/shard_map/all_to_all | solution.py:389
  35.3 16.4 %all-to-all-done.1.same = bf16[16,24,768]{2,1,0:T(8,128)(2,1)S(1)} async-done(((bf16[16,24,768]{2,1,0:T(8,128)(2,1)}), bf16[16,24,768]{2,1,0:T(8,128)(2,1)S(1)}, u32[]{:S(2)}, u32[]{:S(2)}) %all-to-all-start.1) | async-done | bytes 589856 | tf_op jit(solution)/shard_map/all_to_all | solution.py:389
  53.7 2.4 %shard_map.103 = (bf16[8,768]{1,0:T(8,128)(2,1)}, bf16[264,768]{1,0:T(8,128)(2,1)}, bf16[264,768]{1,0:T(8,128)(2,1)}, bf16[264,768]{1,0:T(8,128)(2,1)}) custom-call(s32[2]{0:T(128)} %pad_add_fusion.at, f32[24,128]{1,0:T(8,128)} %bitcast.17, bf16[128,768]{1,0:T(8,128)(2,1)} %bitcast.11, bf16[128,768]{1,0:T(8,128)(2,1)} %bitcast.14, bf16[8,768]{1,0:T(8,128)(2,1)} %copy-done.18), custom_call_target="tpu_custom_call" | custom-call | flops 100000000 | bytes 1646592 | tf_op jit(solution)/shard_map/pallas_call | solution.py:39
  56.0 1.3 collective-permute-start.1
  57.4 8.3 %collective-permute-start.2 = (bf16[264,768]{1,0:T(8,128)(2,1)}, bf16[264,768]{1,0:T(8,128)(2,1)S(1)}, u32[]{:S(2)}, u32[]{:S(2)}) collective-permute-start(bf16[264,768]{1,0:T(8,128)(2,1)} %get-tuple-element.44), channel_id=1, source_target_pairs={{0,64},{32,96},{64,0},{96,32},{128,192},{160,224},{192,128},{224,1... | collective-permute-start | bytes 1216520 | tf_op jit(solution)/shard_map/ppermute | solution.py:380
  68.5 5.3 %collective-permute-done.1.recv1.tok1.cot1 = bf16[264,768]{1,0:T(8,128)(2,1)S(1)} collective-permute-done((bf16[264,768]{1,0:T(8,128)(2,1)}, bf16[264,768]{1,0:T(8,128)(2,1)S(1)}, u32[]{:S(2)}, u32[]{:S(2)}) %collective-permute-start.1) | collective-permute-done | bytes 405536 | tf_op jit(solution)/shard_map/ppermute | solution.py:380
  73.8 9.7 %collective-permute-done.2.recv2.tok2.cot2 = bf16[264,768]{1,0:T(8,128)(2,1)S(1)} collective-permute-done((bf16[264,768]{1,0:T(8,128)(2,1)}, bf16[264,768]{1,0:T(8,128)(2,1)S(1)}, u32[]{:S(2)}, u32[]{:S(2)}) %collective-permute-start.2) | collective-permute-done | bytes 405536 | tf_op jit(solution)/shard_map/ppermute | solution.py:380
  84.6 6.0 %shard_map.105 = (bf16[768,640]{1,0:T(8,128)(2,1)}, f32[512,384]{1,0:T(8,128)}, f32[4,8,128]{2,1,0:T(8,128)}, bf16[512,640]{1,0:T(8,128)(2,1)}, bf16[512,640]{1,...) custom-call(s32[2]{0:T(128)} %pad_add_fusion.at, bf16[128,768]{1,0:T(8,128)(2,1)} %bitcast.12, ...), custom_call_target="tpu_custom_call" | custom-call | flops 100000000 | bytes 6006784 | tf_op jit(solution)/shard_map/pallas_call | solution.py:39
  90.6 7.1 %collective-permute-start.5 = (bf16[128,384]{1,0:T(8,128)(2,1)}, bf16[128,384]{1,0:T(8,128)(2,1)S(1)}, u32[]{:S(2)}, u32[]{:S(2)}) collective-permute-start(bf16[128,384]{1,0:T(8,128)(2,1)} %get-tuple-element.50), channel_id=1, source_target_pairs={{0,128},{32,160},{64,192},{96,224},{1,129},{33,161},{65,193},{97,2... | collective-permute-start | bytes 294920 | tf_op jit(solution)/shard_map/ppermute | solution.py:446
  97.7 3.2 %shard_map.106.y_in = f32[512,384]{1,0:T(8,128)} custom-call(bf16[512,640]{1,0:T(8,128)(2,1)} %get-tuple-element.47.conv, f32[512,384]{1,0:T(8,128)} %get-tuple-element.48.cum, f32[4,8,128]{2,1,0:T(8,128)} %get-tuple-element.51.cum_t, f32[1,384]{1,0:T(1,128)} %broadcast_in_dim_reshape.3.dskip), custom_call_target="tpu_custom_call" | custom-call | flops 100000000 | bytes 2246144 | tf_op jit(solution)/shard_map/pallas_call | solution.py:39
  101.8 6.7 %shard_map.107 = (f32[512,384]{1,0:T(8,128)}, bf16[4,128,384]{2,1,0:T(8,128)(2,1)}, bf16[512,384]{1,0:T(8,128)(2,1)}, bf16[512,384]{1,0:T(8,128)(2,1)}, bf16[4,1...) custom-call(s32[2]{0:T(128)} %pad_add_fusion.at, bf16[512,640]{1,0:T(8,128)(2,1)} %get-tuple-element.47.conv, ...), custom_call_target="tpu_custom_call" | custom-call | flops 100000000 | bytes 8857088 | tf_op jit(solution)/shard_map/pallas_call | solution.py:39
  108.4 2.3 %collective-permute-start.10 = (f32[2,512]{1,0:T(2,128)}, f32[2,512]{1,0:T(2,128)S(1)}, u32[]{:S(2)}, u32[]{:S(2)}) collective-permute-start(f32[2,512]{1,0:T(2,128)} %get-tuple-element.57.stats0), channel_id=1, source_target_pairs={{0,96},{32,0},{64,32},{96,64},{128,224},{160,128},{192,160},{224,1... | collective-permute-start | bytes 12296 | tf_op jit(solution)/shard_map/ppermute | solution.py:380
  110.8 1.7 collective-permute-start.9
  112.5 1.3 fusion.perm
  113.9 2.0 %collective-permute-done.8.stats1 = f32[2,512]{1,0:T(2,128)S(1)} collective-permute-done((f32[2,512]{1,0:T(2,128)}, f32[2,512]{1,0:T(2,128)S(1)}, u32[]{:S(2)}, u32[]{:S(2)}) %collective-permute-start.8) | collective-permute-done | bytes 4128 | tf_op jit(solution)/shard_map/ppermute | solution.py:380
  116.7 5.7 %shard_map.108 = (f32[4,128,128]{2,1,0:T(8,128)}, bf16[512,384]{1,0:T(8,128)(2,1)}, bf16[512,384]{1,0:T(8,128)(2,1)}, bf16[4,128,384]{2,1,0:T(8,128)(2,1)}, bf16...) custom-call(s32[2]{0:T(128)} %pad_add_fusion.at, f32[512,384]{1,0:T(8,128)} %get-tuple-element.54.y, ...), custom_call_target="tpu_custom_call" | custom-call | flops 100000000 | bytes 7755264 | tf_op jit(solution)/shard_map/pallas_call | solution.py:39
  122.5 4.5 %all-to-all-start.2 = ((bf16[4,128,768]{2,1,0:T(8,128)(2,1)}), bf16[4,128,768]{2,1,0:T(8,128)(2,1)S(1)}, u32[]{:S(2)}, u32[]{:S(2)}) async-start(bf16[4,128,768]{2,1,0:T(8,128)(2,1)} %get-tuple-element.64), calls=%async_computation.2 | async-start | bytes 1572864 | tf_op jit(solution)/shard_map/all_to_all | solution.py:383
  127.2 3.2 %collective-permute-start.14 = (bf16[192,384]{1,0:T(8,128)(2,1)S(1)}, bf16[192,384]{1,0:T(8,128)(2,1)S(1)}, u32[]{:S(2)}, u32[]{:S(2)}) collective-permute-start(bf16[192,384]{1,0:T(8,128)(2,1)S(1)} %slice.28), channel_id=1, source_target_pairs={{0,128},{32,160},{64,192},{96,224},{128,0},{160,32},{192,64},{224,... | collective-permute-start | bytes 442376 | tf_op jit(solution)/shard_map/ppermute | solution.py:474
  130.4 4.4 %collective-permute-done.14 = bf16[192,384]{1,0:T(8,128)(2,1)S(1)} collective-permute-done((bf16[192,384]{1,0:T(8,128)(2,1)S(1)}, bf16[192,384]{1,0:T(8,128)(2,1)S(1)}, u32[]{:S(2)}, u32[]{:S(2)}) %collective-permute-start.14) | collective-permute-done | bytes 147488 | tf_op jit(solution)/shard_map/ppermute | solution.py:474
  135.5 4.5 %all-to-all-done.2.parts = bf16[4,128,768]{2,1,0:T(8,128)(2,1)S(1)} async-done(((bf16[4,128,768]{2,1,0:T(8,128)(2,1)}), bf16[4,128,768]{2,1,0:T(8,128)(2,1)S(1)}, u32[]{:S(2)}, u32[]{:S(2)}) %all-to-all-start.2) | async-done | bytes 786464 | tf_op jit(solution)/shard_map/all_to_all | solution.py:383
  140.0 4.7 %all-to-all-start.3 = ((bf16[16,12,384]{2,1,0:T(8,128)(2,1)}), bf16[16,12,384]{2,1,0:T(8,128)(2,1)S(1)}, u32[]{:S(2)}, u32[]{:S(2)}) async-start(bf16[16,12,384]{2,1,0:T(8,128)(2,1)} %reshape.93), calls=%async_computation.3 | async-start | bytes 393216 | tf_op jit(solution)/shard_map/all_to_all | solution.py:482
  146.0 5.0 %shard_map.109 = (bf16[512,384]{1,0:T(8,128)(2,1)}, bf16[512,256]{1,0:T(8,128)(2,1)}, f32[8,640]{1,0:T(8,128)}) custom-call(bf16[512,640]{1,0:T(8,128)(2,1)} %get-tuple-element.47.conv, f32[512,384]{1,0:T(8,128)} %get-tuple-element.48.cum, f32[4,8,128]{2,1,0:T(8,128)} %get-tuple-element.51.cum_t, f32[1,384]{1,0:T(1,128)} %broadcast_in_dim_reshape.3.dskip, ...), custom_call_target="tpu_custom_call" | custom-call | flops 100000000 | bytes 3970560 | tf_op jit(solution)/shard_map/pallas_call | solution.py:39
  153.8 4.3 %shard_map.110 = (bf16[512,640]{1,0:T(8,128)(2,1)}, bf16[128,768]{1,0:T(8,128)(2,1)}) custom-call(s32[2]{0:T(128)} %pad_add_fusion.at, bf16[512,640]{1,0:T(8,128)(2,1)} %get-tuple-element.47.conv, f32[512,384]{1,0:T(8,128)} %get-tuple-element.48.cum, bf16[4,128,384]{2,1,0:T(8,128)(2,1)} %get-tuple-element.53.full, ...), custom_call_target="tpu_custom_call" | custom-call | flops 100000000 | bytes 5931008 | tf_op jit(solution)/shard_map/pallas_call | solution.py:39
  159.1 5.4 %shard_map.111 = (bf16[128,768]{1,0:T(8,128)(2,1)}, bf16[136,768]{1,0:T(8,128)(2,1)}, bf16[136,768]{1,0:T(8,128)(2,1)}, bf16[136,768]{1,0:T(8,128)(2,1)}, f32[8,384]{1,0:T(8,128)}) custom-call(s32[2]{0:T(128)} %pad_add_fusion.at, bf16[512,640]{1,0:T(8,128)(2,1)} %get-tuple-element.67.gp, f32[8,640]{1,0:T(8,128)} %copy-done.16, ...), custom_call_target="tpu_custom_call" | custom-call | flops 100000000 | bytes 3635200 | tf_op jit(solution)/shard_map/pallas_call | solution.py:39
  165.0 2.1 %collective-permute-start.16 = (bf16[136,768]{1,0:T(8,128)(2,1)}, bf16[136,768]{1,0:T(8,128)(2,1)S(1)}, u32[]{:S(2)}, u32[]{:S(2)}) collective-permute-start(bf16[136,768]{1,0:T(8,128)(2,1)} %get-tuple-element.77), channel_id=1, source_target_pairs={{0,64},{32,96},{64,0},{96,32},{128,192},{160,224},{192,128},{224,1... | collective-permute-start | bytes 626696 | tf_op jit(solution)/shard_map/ppermute | solution.py:380
  167.8 7.4 %collective-permute-done.15.got1 = bf16[136,768]{1,0:T(8,128)(2,1)S(1)} collective-permute-done((bf16[136,768]{1,0:T(8,128)(2,1)}, bf16[136,768]{1,0:T(8,128)(2,1)S(1)}, u32[]{:S(2)}, u32[]{:S(2)}) %collective-permute-start.15) | collective-permute-done | bytes 208928 | tf_op jit(solution)/shard_map/ppermute | solution.py:380
  176.5 2.0 %shard_map.112 = (bf16[128,768]{1,0:T(8,128)(2,1)}, f32[3,1536]{1,0:T(4,128)}) custom-call(s32[2]{0:T(128)} %pad_add_fusion.at, bf16[128,768]{1,0:T(8,128)(2,1)} %get-tuple-element.74.own, f32[8,384]{1,0:T(8,128)} %get-tuple-element.75.own_dw, bf16[136,768]{1,0:T(8,128)(2,1)} %copy-done.10, bf16[136,768]{1,0:T(8,128)(2,1)} %copy-done.11, ...), custom_call_target="tpu_custom_call" | custom-call | flops 100000000 | bytes 1050624 | tf_op jit(solution)/shard_map/pallas_call | solution.py:39
  (93 shorter events, 17.7 us)
Async XLA Ops:
  0.6 12.1 %copy-start.15 = (bf16[48,768]{1,0:T(8,128)(2,1)S(1)}, bf16[48,768]{1,0:T(8,128)(2,1)}, u32[]{:S(2)}) copy-start(bf16[48,768]{1,0:T(8,128)(2,1)} %param.12) | copy-start | bytes 221188
  3.0 22.2 %copy-start.17 = (bf16[24,384]{1,0:T(8,128)(2,1)S(1)}, bf16[24,384]{1,0:T(8,128)(2,1)}, u32[]{:S(2)}) copy-start(bf16[24,384]{1,0:T(8,128)(2,1)} %get-tuple-element.52) | copy-start | bytes 55300
  3.0 24.9 %all-to-all-start = ((bf16[16,24,640]{2,1,0:T(8,128)(2,1)}), bf16[16,24,640]{2,1,0:T(8,128)(2,1)S(1)}, u32[]{:S(2)}, u32[]{:S(2)}) async-start(bf16[16,24,640]{2,1,0:T(8,128)(2,1)} %get-tuple-element.46), calls=%async_computation | async-start | bytes 983040 | tf_op jit(solution)/shard_map/all_to_all | solution.py:389
  12.8 12.4 %collective-permute-start.6 = (bf16[24,384]{1,0:T(8,128)(2,1)S(1)}, bf16[24,384]{1,0:T(8,128)(2,1)S(1)}, u32[]{:S(2)}, u32[]{:S(2)}) collective-permute-start(bf16[24,384]{1,0:T(8,128)(2,1)S(1)} %constant_dynamic-slice_fusion), channel_id=1, source_target_pairs={{0,0},{1,4},{2,8},{3,12},{4,16},{5,20},{6,24},{7,28},{8,32},{9,36}... | collective-permute-start | bytes 55304 | tf_op jit(solution)/shard_map/ppermute | solution.py:419
  25.2 40.5 %copy-start.23 = (f32[24]{0:T(128)S(1)}, f32[24]{0:T(128)}, u32[]{:S(2)}) copy-start(f32[24]{0:T(128)} %param.14) | copy-start | bytes 292
  25.2 42.7 %slice-start = ((f32[4,1792]{1,0:T(4,128)}), f32[4,1536]{1,0:T(4,128)S(1)}, s32[]{:S(2)}) async-start(f32[4,1792]{1,0:T(4,128)} %param.13), calls=%async_computation.4 | async-start | bytes 49152 | tf_op jit(solution)/shard_map/slice | solution.py:424
  25.2 42.7 %slice-start.1 = ((f32[4,1792]{1,0:T(4,128)}), f32[4,256]{1,0:T(4,128)S(1)}, s32[]{:S(2)}) async-start(f32[4,1792]{1,0:T(4,128)} %param.13), calls=%async_computation.5 | async-start | bytes 8192 | tf_op jit(solution)/shard_map/slice | solution.py:424
  27.9 40.0 %copy-start.5 = (bf16[16,24,640]{2,1,0:T(8,128)(2,1)}, bf16[16,24,640]{2,1,0:T(8,128)(2,1)S(1)}, u32[]{:S(2)}) copy-start(bf16[16,24,640]{2,1,0:T(8,128)(2,1)S(1)} %all-to-all-done.same) | copy-start | bytes 1474564
  28.8 22.9 %all-to-all-start.1 = ((bf16[16,24,768]{2,1,0:T(8,128)(2,1)}), bf16[16,24,768]{2,1,0:T(8,128)(2,1)S(1)}, u32[]{:S(2)}, u32[]{:S(2)}) async-start(bf16[16,24,768]{2,1,0:T(8,128)(2,1)} %broadcast_in_dim.35), calls=%async_computation.1 | async-start | bytes 1179648 | tf_op jit(solution)/shard_map/all_to_all | solution.py:389
  35.3 48.2 %collective-permute-start.4 = (bf16[16,24,640]{2,1,0:T(8,128)(2,1)S(1)}, bf16[16,24,640]{2,1,0:T(8,128)(2,1)S(1)}, u32[]{:S(2)}, u32[]{:S(2)}) collective-permute-start(bf16[16,24,640]{2,1,0:T(8,128)(2,1)S(1)} %all-to-all-done.same), channel_id=1, source_target_pairs={{0,1},{1,0},{2,3},{3,2},{4,5},{5,4},{6,7},{7,6},{8,9},{9,8},{10,11... | collective-permute-start | bytes 1474568 | tf_op jit(solution)/shard_map/ppermute | solution.py:390
  51.7 38.9 %copy-start.4 = (bf16[16,24,768]{2,1,0:T(8,128)(2,1)}, bf16[16,24,768]{2,1,0:T(8,128)(2,1)S(1)}, u32[]{:S(2)}) copy-start(bf16[16,24,768]{2,1,0:T(8,128)(2,1)S(1)} %all-to-all-done.1.same) | copy-start | bytes 1769476
  51.7 49.2 %collective-permute-start.7 = (bf16[16,24,768]{2,1,0:T(8,128)(2,1)S(1)}, bf16[16,24,768]{2,1,0:T(8,128)(2,1)S(1)}, u32[]{:S(2)}, u32[]{:S(2)}) collective-permute-start(bf16[16,24,768]{2,1,0:T(8,128)(2,1)S(1)} %all-to-all-done.1.same), channel_id=1, source_target_pairs={{0,1},{1,0},{2,3},{3,2},{4,5},{5,4},{6,7},{7,6},{8,9},{9,8},{10,11... | collective-permute-start | bytes 1769480 | tf_op jit(solution)/shard_map/ppermute | solution.py:390
  52.4 0.7 collective-permute-start
  56.0 17.7 %collective-permute-start.1 = (bf16[264,768]{1,0:T(8,128)(2,1)}, bf16[264,768]{1,0:T(8,128)(2,1)S(1)}, u32[]{:S(2)}, u32[]{:S(2)}) collective-permute-start(bf16[264,768]{1,0:T(8,128)(2,1)} %get-tuple-element.43), channel_id=1, source_target_pairs={{0,32},{32,64},{64,96},{96,0},{128,160},{160,192},{192,224},{224,1... | collective-permute-start | bytes 1216520 | tf_op jit(solution)/shard_map/ppermute | solution.py:380
  57.4 26.1 %collective-permute-start.2 = (bf16[264,768]{1,0:T(8,128)(2,1)}, bf16[264,768]{1,0:T(8,128)(2,1)S(1)}, u32[]{:S(2)}, u32[]{:S(2)}) collective-permute-start(bf16[264,768]{1,0:T(8,128)(2,1)} %get-tuple-element.44), channel_id=1, source_target_pairs={{0,64},{32,96},{64,0},{96,32},{128,192},{160,224},{192,128},{224,1... | collective-permute-start | bytes 1216520 | tf_op jit(solution)/shard_map/ppermute | solution.py:380
  65.7 17.8 %collective-permute-start.3 = (bf16[264,768]{1,0:T(8,128)(2,1)}, bf16[264,768]{1,0:T(8,128)(2,1)S(1)}, u32[]{:S(2)}, u32[]{:S(2)}) collective-permute-start(bf16[264,768]{1,0:T(8,128)(2,1)} %get-tuple-element.45), channel_id=1, source_target_pairs={{0,96},{32,0},{64,32},{96,64},{128,224},{160,128},{192,160},{224,1... | collective-permute-start | bytes 1216520 | tf_op jit(solution)/shard_map/ppermute | solution.py:380
  73.8 9.8 %copy-start = (bf16[264,768]{1,0:T(8,128)(2,1)}, bf16[264,768]{1,0:T(8,128)(2,1)S(1)}, u32[]{:S(2)}) copy-start(bf16[264,768]{1,0:T(8,128)(2,1)S(1)} %collective-permute-done.1.recv1.tok1.cot1) | copy-start | bytes 1216516
  90.6 10.3 %collective-permute-start.5 = (bf16[128,384]{1,0:T(8,128)(2,1)}, bf16[128,384]{1,0:T(8,128)(2,1)S(1)}, u32[]{:S(2)}, u32[]{:S(2)}) collective-permute-start(bf16[128,384]{1,0:T(8,128)(2,1)} %get-tuple-element.50), channel_id=1, source_target_pairs={{0,128},{32,160},{64,192},{96,224},{1,129},{33,161},{65,193},{97,2... | collective-permute-start | bytes 294920 | tf_op jit(solution)/shard_map/ppermute | solution.py:446
  108.4 5.4 %collective-permute-start.10 = (f32[2,512]{1,0:T(2,128)}, f32[2,512]{1,0:T(2,128)S(1)}, u32[]{:S(2)}, u32[]{:S(2)}) collective-permute-start(f32[2,512]{1,0:T(2,128)} %get-tuple-element.57.stats0), channel_id=1, source_target_pairs={{0,96},{32,0},{64,32},{96,64},{128,224},{160,128},{192,160},{224,1... | collective-permute-start | bytes 12296 | tf_op jit(solution)/shard_map/ppermute | solution.py:380
  110.8 5.0 %collective-permute-start.8 = (f32[2,512]{1,0:T(2,128)}, f32[2,512]{1,0:T(2,128)S(1)}, u32[]{:S(2)}, u32[]{:S(2)}) collective-permute-start(f32[2,512]{1,0:T(2,128)} %get-tuple-element.57.stats0), channel_id=1, source_target_pairs={{0,32},{32,64},{64,96},{96,0},{128,160},{160,192},{192,224},{224,1... | collective-permute-start | bytes 12296 | tf_op jit(solution)/shard_map/ppermute | solution.py:380
  110.8 5.3 %collective-permute-start.9 = (f32[2,512]{1,0:T(2,128)}, f32[2,512]{1,0:T(2,128)S(1)}, u32[]{:S(2)}, u32[]{:S(2)}) collective-permute-start(f32[2,512]{1,0:T(2,128)} %get-tuple-element.57.stats0), channel_id=1, source_target_pairs={{0,64},{32,96},{64,0},{96,32},{128,192},{160,224},{192,128},{224,1... | collective-permute-start | bytes 12296 | tf_op jit(solution)/shard_map/ppermute | solution.py:380
  122.4 4.6 %collective-permute-start.13 = (bf16[384,384]{1,0:T(8,128)(2,1)}, bf16[384,384]{1,0:T(8,128)(2,1)S(1)}, u32[]{:S(2)}, u32[]{:S(2)}) collective-permute-start(bf16[384,384]{1,0:T(8,128)(2,1)} %get-tuple-element.73), channel_id=1, source_target_pairs={{0,1},{1,0},{2,3},{3,2},{4,5},{5,4},{6,7},{7,6},{8,9},{9,8},{10,11... | collective-permute-start | bytes 884744 | tf_op jit(solution)/shard_map/ppermute | solution.py:471
  122.5 17.4 %all-to-all-start.2 = ((bf16[4,128,768]{2,1,0:T(8,128)(2,1)}), bf16[4,128,768]{2,1,0:T(8,128)(2,1)S(1)}, u32[]{:S(2)}, u32[]{:S(2)}) async-start(bf16[4,128,768]{2,1,0:T(8,128)(2,1)} %get-tuple-element.64), calls=%async_computation.2 | async-start | bytes 1572864 | tf_op jit(solution)/shard_map/all_to_all | solution.py:383
  127.1 17.6 %copy-start.22 = (bf16[128,384]{1,0:T(8,128)(2,1)S(1)}, bf16[128,384]{1,0:T(8,128)(2,1)}, u32[]{:S(2)}) copy-start(bf16[128,384]{1,0:T(8,128)(2,1)} %get-tuple-element.59) | copy-start | bytes 294916
  127.2 7.5 %collective-permute-start.14 = (bf16[192,384]{1,0:T(8,128)(2,1)S(1)}, bf16[192,384]{1,0:T(8,128)(2,1)S(1)}, u32[]{:S(2)}, u32[]{:S(2)}) collective-permute-start(bf16[192,384]{1,0:T(8,128)(2,1)S(1)} %slice.28), channel_id=1, source_target_pairs={{0,128},{32,160},{64,192},{96,224},{128,0},{160,32},{192,64},{224,... | collective-permute-start | bytes 442376 | tf_op jit(solution)/shard_map/ppermute | solution.py:474
  140.0 11.0 %copy-start.3 = (bf16[4,128,768]{2,1,0:T(8,128)(2,1)}, bf16[4,128,768]{2,1,0:T(8,128)(2,1)S(1)}, u32[]{:S(2)}) copy-start(bf16[4,128,768]{2,1,0:T(8,128)(2,1)S(1)} %all-to-all-done.2.parts) | copy-start | bytes 2359300
  140.0 18.4 %all-to-all-start.3 = ((bf16[16,12,384]{2,1,0:T(8,128)(2,1)}), bf16[16,12,384]{2,1,0:T(8,128)(2,1)S(1)}, u32[]{:S(2)}, u32[]{:S(2)}) async-start(bf16[16,12,384]{2,1,0:T(8,128)(2,1)} %reshape.93), calls=%async_computation.3 | async-start | bytes 393216 | tf_op jit(solution)/shard_map/all_to_all | solution.py:482
  144.7 8.4 %collective-permute-start.11 = (bf16[128,384]{1,0:T(8,128)(2,1)S(1)}, bf16[128,384]{1,0:T(8,128)(2,1)S(1)}, u32[]{:S(2)}, u32[]{:S(2)}) collective-permute-start(bf16[128,384]{1,0:T(8,128)(2,1)S(1)} %copy-done.22), channel_id=1, source_target_pairs={{128,0},{160,32},{192,64},{224,96},{129,1},{161,33},{193,65},{225,... | collective-permute-start | bytes 294920 | tf_op jit(solution)/shard_map/ppermute | solution.py:470
  151.0 7.4 %collective-permute-start.12 = (f32[8,640]{1,0:T(8,128)}, f32[8,640]{1,0:T(8,128)S(1)}, u32[]{:S(2)}, u32[]{:S(2)}) collective-permute-start(f32[8,640]{1,0:T(8,128)} %get-tuple-element.68), channel_id=1, source_target_pairs={{128,0},{160,32},{192,64},{224,96},{129,1},{161,33},{193,65},{225,... | collective-permute-start | bytes 61448 | tf_op jit(solution)/shard_map/ppermute | solution.py:480
  164.4 10.7 %collective-permute-start.15 = (bf16[136,768]{1,0:T(8,128)(2,1)}, bf16[136,768]{1,0:T(8,128)(2,1)S(1)}, u32[]{:S(2)}, u32[]{:S(2)}) collective-permute-start(bf16[136,768]{1,0:T(8,128)(2,1)} %get-tuple-element.76), channel_id=1, source_target_pairs={{0,32},{32,64},{64,96},{96,0},{128,160},{160,192},{192,224},{224,1... | collective-permute-start | bytes 626696 | tf_op jit(solution)/shard_map/ppermute | solution.py:380
  165.0 10.2 %collective-permute-start.16 = (bf16[136,768]{1,0:T(8,128)(2,1)}, bf16[136,768]{1,0:T(8,128)(2,1)S(1)}, u32[]{:S(2)}, u32[]{:S(2)}) collective-permute-start(bf16[136,768]{1,0:T(8,128)(2,1)} %get-tuple-element.77), channel_id=1, source_target_pairs={{0,64},{32,96},{64,0},{96,32},{128,192},{160,224},{192,128},{224,1... | collective-permute-start | bytes 626696 | tf_op jit(solution)/shard_map/ppermute | solution.py:380
  167.1 8.8 %collective-permute-start.17 = (bf16[136,768]{1,0:T(8,128)(2,1)}, bf16[136,768]{1,0:T(8,128)(2,1)S(1)}, u32[]{:S(2)}, u32[]{:S(2)}) collective-permute-start(bf16[136,768]{1,0:T(8,128)(2,1)} %get-tuple-element.78), channel_id=1, source_target_pairs={{0,96},{32,0},{64,32},{96,64},{128,224},{160,128},{192,160},{224,1... | collective-permute-start | bytes 626696 | tf_op jit(solution)/shard_map/ppermute | solution.py:380
  (16 other events, 17.0 us)

commit v3 on v2

--- a/solution.py
+++ b/solution.py
@@ -11,7 +11,6 @@
 bf16, f32 = jnp.bfloat16, jnp.float32
 CHUNK = 128
 LANES = 128
-LIMIT = None
 XS = 4
 NN = (((1,), (0,)), ((), ()))
 NT = (((1,), (1,)), ((), ()))
@@ -32,7 +31,7 @@
     return 0.5 + 0.5 * jnp.tanh(0.5 * v)
 
 
-def kernel_call(body, outs, *args, scalars=None, scratch=(), flops=10**8):
+def kernel_call(body, outs, *args, scalars=None, scratch=(), flops=10**8, limit=None):
     spec = pl.BlockSpec(memory_space=pltpu.VMEM)
     size = sum(a.size * a.dtype.itemsize for a in list(args) + list(outs))
     first = [] if scalars is None else [scalars]
@@ -42,7 +41,7 @@
         in_specs=[pl.BlockSpec(memory_space=pltpu.SMEM)] * len(first) + [spec] * len(args),
         out_specs=[spec] * len(outs),
         scratch_shapes=list(scratch),
-        compiler_params=pltpu.CompilerParams(vmem_limit_bytes=LIMIT),
+        compiler_params=pltpu.CompilerParams(vmem_limit_bytes=limit),
         cost_estimate=pl.CostEstimate(flops=flops, bytes_accessed=size, transcendentals=0),
     )(*first, *args)
 
@@ -89,7 +88,7 @@
     gate_w[...] = in_w[:, pl.ds(start, width)]
 
 
-def pack(at, logs, tokens, cotangent, halo, aux, send1, send2, send3, decays):
+def pack(at, logs, tokens, halo, aux, send1, send2, send3, decays):
     block = logs.shape[1]
     step = lax.broadcasted_iota(jnp.int32, (block, block), 0)
     upto = (step <= lax.broadcasted_iota(jnp.int32, (block, block), 1)).astype(f32)
@@ -109,8 +108,7 @@
     aux[...] = (decays[at[0]] + tail).astype(bf16)
     for r, send in enumerate((send1, send2, send3)):
         send[:block, :] = tokens[...]
-        send[block : 2 * block, :] = cotangent[...]
-        send[2 * block :, :] = (decays[lax.rem(at[0] + r + 1, XS)] + tail).astype(bf16)
+        send[block:, :] = (decays[lax.rem(at[0] + r + 1, XS)] + tail).astype(bf16)
 
 
 def assemble(at, same, other, target, lanes):
@@ -131,7 +129,7 @@
     for r, source in enumerate((None, recv1, recv2, recv3)):
         c, _ = place(at, r)
         t = tokens[...] if r == 0 else source[:block, :]
-        extra = (aux[...] if r == 0 else source[2 * block :, :]).astype(f32)
+        extra = (aux[...] if r == 0 else source[block:, :]).astype(f32)
         halo = halo + extra
         mix[pl.ds(pl.multiple_of(8 + c * block, 8), block), :] = (
             dot(t, w_mix[...]).astype(bf16).astype(f32)
@@ -182,7 +180,8 @@
             y[r, s] = (dot(weight, both) + dskip[:, s] * x).astype(y.dtype)
 
 
-def gated(at, conv, cum, states, entering, y_in, tok0, cot0, tok1, tok2, tok3, same, other, norm_w,
+def gated(at, conv, cum, states, entering, y_in, tok0, tok1, tok2, tok3, cot0, cot1, cot2, cot3,
+          same, other, norm_w,
           y, full, gate, dn, part, stats, w_gate, raw, w_out):
     width = y.shape[1]
     chunks = y.shape[0] // CHUNK
@@ -192,11 +191,10 @@
         for k in range(2):
             lanes = slice(k * width + p * LANES, k * width + (p + 1) * LANES)
             w_out[:, lanes] = raw[p, pl.ds(k, width, stride=2), :].astype(bf16)
-    for r, tok in enumerate((tok0, tok1, tok2, tok3)):
+    for r, (tok, cot) in enumerate(((tok0, cot0), (tok1, cot1), (tok2, cot2), (tok3, cot3))):
         here = place(at, r)[1]
         gate[here, :] = dot(tok[:CHUNK, :], w_gate[...]).astype(bf16)
-        cot = cot0[...] if r == 0 else tok[CHUNK : 2 * CHUNK, :]
-        dn[here, :] = (dot(cot, w_out[...], NT) * norm_w[...]).astype(dn.dtype)
+        dn[here, :] = (dot(cot[...], w_out[...], NT) * norm_w[...]).astype(dn.dtype)
     carried = entering[...].astype(f32)
     ones = jnp.ones((8, LANES), f32)
     for c in range(chunks):
@@ -245,7 +243,7 @@
         )
     first[...] = adjoint.astype(bf16)
     for r, source in enumerate((cot0, cot1, cot2, cot3)):
-        cot[place(at, r)[1], :] = source[...] if r == 0 else source[CHUNK : 2 * CHUNK, :]
+        cot[place(at, r)[1], :] = source[...]
     summed = dot(cot[...], low[...], TN)
     give[...] = dot(perm[keep.shape[0] :, :], summed).astype(bf16)
     keep[...] = dot(perm[: keep.shape[0], :], summed).astype(bf16)
@@ -402,13 +400,14 @@
     same1, other1 = gather_weights(wide1)
     aux, *sends = kernel_call(
         pack,
-        [out((8, model), bf16)] + [out((2 * block + 8, model), bf16)] * (XS - 1),
-        decay[0].T, tokens[0], cotangent[0], halo,
+        [out((8, model), bf16)] + [out((block + 8, model), bf16)] * (XS - 1),
+        decay[0].T, tokens[0], halo,
         scalars=at, scratch=[pltpu.VMEM((XS, 8, model), f32)],
     )
-    recv = []
+    recv, cots = [], [cotangent[0]]
     for r in range(1, XS):
         recv.append(along_x(sends[r - 1], r))
+        cots.append(along_x(cotangent[0], r))
     piece = 2 * out_w.shape[0] // XS
     routes = []
     for t in range(tm):
@@ -450,7 +449,7 @@
         [out((rows, width), f32), out(states.shape, bf16), out((rows, width), bf16),
          out((rows, width), bf16), out((XS, block, model), bf16), out((2, rows), f32),
          out((model, width), bf16)],
-        conv, cum, states, entering, y_in, tokens[0], cotangent[0], *recv, same2, other2, gain,
+        conv, cum, states, entering, y_in, tokens[0], *recv, *cots, same2, other2, gain,
         scalars=at,
         scratch=[pltpu.VMEM((width // LANES, model, LANES), f32), pltpu.VMEM((width, model), bf16)],
     )
@@ -463,7 +462,7 @@
         [out((chunks, CHUNK, LANES), f32), out((rows, width), bf16), out((rows, width), bf16),
          out(states.shape, bf16), out((state, width), bf16), out((model // 2, width), bf16),
          out((model // 2, width), bf16)],
-        y, gate, dn, stats, *others, conv, cum, gain, cotangent[0], *recv, perm,
+        y, gate, dn, stats, *others, conv, cum, gain, *cots, perm,
         scalars=at,
         scratch=[pltpu.VMEM((rows, width), bf16), pltpu.VMEM((rows, model), bf16)],
     )
@@ -503,7 +502,7 @@
         functools.partial(finish, scale),
         [out((block, model), bf16), out((3, inner), f32)],
         token_parts[0], own_dw, moved[1], moved[2], moved[3],
-        scalars=at,
+        scalars=at, limit=2**23,
     )
     return (result[None], grad_tokens[None], grad_out_t)
 

time: 181 us -> 175 us (0.967)
  waiting for transfers between devices: 60.4 us -> 51.8 us
  starting transfers between devices: 62.5 us -> 66.1 us
    ppermute x9 -> x12, waiting for transfers between devices: 25.4 us -> 16.7 us  [along_x(): return lax.ppermute(array, 'tm', pairs)]
    ppermute x9 -> x12, starting transfers between devices: 17.1 us -> 20.9 us  [along_x(): return lax.ppermute(array, 'tm', pairs)]
    unnamed x48 -> x54, local copies, waits for them, and re-layouts: 5.13 us -> 5.21 us
  transfers between devices with their start and end apart: 22 -> 25, of which waited for: 13 -> 12; matrix products, arithmetic and copies ran while one was open for 3% -> 3% of each run, Pallas kernels for 12% -> 12%
where the time goes in v3:
time: 175 us; the launch traced here: 172 us
  starting transfers between devices  66.1 us (38%)
  waiting for transfers between devices  51.8 us (30%)
  Pallas kernels  40.9 us (23%)
  local copies, waits for them, and re-layouts  9.7 us (6%)
  other arithmetic  2.61 us (1%)
    pallas_call x10, Pallas kernels, kernel_call(): pl.pallas_call(body, out_shape=outs, in_specs=[pl.BlockSpec(memory_space=...  40.9 us
    ppermute x12, starting transfers between devices, along_x(): return lax.ppermute(array, 'tm', pairs)  20.9 us
    all_to_all x2, waiting for transfers between devices, gather_weights(): same = lax.all_to_all(wide, 'stream', 0, 0, axis_index_groups=cores)  19 us
    ppermute x12, waiting for transfers between devices, along_x(): return lax.ppermute(array, 'tm', pairs)  16.7 us
    all_to_all x2, starting transfers between devices, gather_weights(): same = lax.all_to_all(wide, 'stream', 0, 0, axis_index_groups=cores)  16.3 us
    ppermute x1, starting transfers between devices, shards(): entering = lax.ppermute(last, 'tm', up)  6.76 us
    ppermute x1, starting transfers between devices, shards(): lax.ppermute(own(out_w.reshape(-1, width), 0, piece), ('tm', 'stream'), r...  6.38 us
    ppermute x1, waiting for transfers between devices, shards(): lax.ppermute(own(out_w.reshape(-1, width), 0, piece), ('tm', 'stream'), r...  5.99 us
  transfers between devices with their start and end apart: 25, of which 12 were waited for; matrix products, arithmetic and copies ran while one was open for 3% of the time, Pallas kernels for 12%

profile of v3, /device:TPU:32, one launch (start us, length us, event | category | flops | bytes accessed | tf_op | source)
XLA Modules:
  0.0 172.2 jit_solution(12114496797715060617)
XLA Ops:
  1.2 1.8 %shard_map.104 = (bf16[16,24,640]{2,1,0:T(8,128)(2,1)}, bf16[24,384]{1,0:T(8,128)(2,1)}) custom-call(s32[2]{0:T(128)} %pad_add_fusion.at, bf16[24,3328]{1,0:T(8,128)(2,1)} %in_w.1), custom_call_target="tpu_custom_call" | custom-call | flops 100000000 | bytes 669696 | tf_op jit(solution)/shard_map/pallas_call | solution.py:38
  3.0 9.7 %all-to-all-start = ((bf16[16,24,640]{2,1,0:T(8,128)(2,1)}), bf16[16,24,640]{2,1,0:T(8,128)(2,1)S(1)}, u32[]{:S(2)}, u32[]{:S(2)}) async-start(bf16[16,24,640]{2,1,0:T(8,128)(2,1)} %get-tuple-element.46), calls=%async_computation | async-start | bytes 983040 | tf_op jit(solution)/shard_map/all_to_all | solution.py:387
  12.8 6.4 %collective-permute-start.9 = (bf16[24,384]{1,0:T(8,128)(2,1)S(1)}, bf16[24,384]{1,0:T(8,128)(2,1)S(1)}, u32[]{:S(2)}, u32[]{:S(2)}) collective-permute-start(bf16[24,384]{1,0:T(8,128)(2,1)S(1)} %constant_dynamic-slice_fusion), channel_id=1, source_target_pairs={{0,0},{1,4},{2,8},{3,12},{4,16},{5,20},{6,24},{7,28},{8,32},{9,36}... | collective-permute-start | bytes 55304 | tf_op jit(solution)/shard_map/ppermute | solution.py:418
  19.2 6.0 %collective-permute-done.9 = bf16[24,384]{1,0:T(8,128)(2,1)S(1)} collective-permute-done((bf16[24,384]{1,0:T(8,128)(2,1)S(1)}, bf16[24,384]{1,0:T(8,128)(2,1)S(1)}, u32[]{:S(2)}, u32[]{:S(2)}) %collective-permute-start.9) | collective-permute-done | bytes 18464 | tf_op jit(solution)/shard_map/ppermute | solution.py:418
  25.2 2.7 %all-to-all-done.same = bf16[16,24,640]{2,1,0:T(8,128)(2,1)S(1)} async-done(((bf16[16,24,640]{2,1,0:T(8,128)(2,1)}), bf16[16,24,640]{2,1,0:T(8,128)(2,1)S(1)}, u32[]{:S(2)}, u32[]{:S(2)}) %all-to-all-start) | async-done | bytes 491552 | tf_op jit(solution)/shard_map/all_to_all | solution.py:387
  28.8 6.5 %all-to-all-start.1 = ((bf16[16,24,768]{2,1,0:T(8,128)(2,1)}), bf16[16,24,768]{2,1,0:T(8,128)(2,1)S(1)}, u32[]{:S(2)}, u32[]{:S(2)}) async-start(bf16[16,24,768]{2,1,0:T(8,128)(2,1)} %broadcast_in_dim.35), calls=%async_computation.1 | async-start | bytes 1179648 | tf_op jit(solution)/shard_map/all_to_all | solution.py:387
  35.4 16.4 %all-to-all-done.1.same = bf16[16,24,768]{2,1,0:T(8,128)(2,1)S(1)} async-done(((bf16[16,24,768]{2,1,0:T(8,128)(2,1)}), bf16[16,24,768]{2,1,0:T(8,128)(2,1)S(1)}, u32[]{:S(2)}, u32[]{:S(2)}) %all-to-all-start.1) | async-done | bytes 589856 | tf_op jit(solution)/shard_map/all_to_all | solution.py:387
  53.7 2.0 %shard_map.103 = (bf16[8,768]{1,0:T(8,128)(2,1)}, bf16[136,768]{1,0:T(8,128)(2,1)}, bf16[136,768]{1,0:T(8,128)(2,1)}, bf16[136,768]{1,0:T(8,128)(2,1)}) custom-call(s32[2]{0:T(128)} %pad_add_fusion.at, f32[24,128]{1,0:T(8,128)} %bitcast.21, bf16[128,768]{1,0:T(8,128)(2,1)} %bitcast.11, bf16[8,768]{1,0:T(8,128)(2,1)} %copy-done.25), custom_call_target="tpu_custom_call" | custom-call | flops 100000000 | bytes 860160 | tf_op jit(solution)/shard_map/pallas_call | solution.py:38
  55.7 1.3 collective-permute-start.1
  57.0 8.3 %collective-permute-start.2 = (bf16[136,768]{1,0:T(8,128)(2,1)}, bf16[136,768]{1,0:T(8,128)(2,1)S(1)}, u32[]{:S(2)}, u32[]{:S(2)}) collective-permute-start(bf16[136,768]{1,0:T(8,128)(2,1)} %get-tuple-element.44), channel_id=1, source_target_pairs={{0,64},{32,96},{64,0},{96,32},{128,192},{160,224},{192,128},{224,1... | collective-permute-start | bytes 626696 | tf_op jit(solution)/shard_map/ppermute | solution.py:378
  67.4 1.8 %collective-permute-done.1.recv1.tok1 = bf16[136,768]{1,0:T(8,128)(2,1)S(1)} collective-permute-done((bf16[136,768]{1,0:T(8,128)(2,1)}, bf16[136,768]{1,0:T(8,128)(2,1)S(1)}, u32[]{:S(2)}, u32[]{:S(2)}) %collective-permute-start.1) | collective-permute-done | bytes 208928 | tf_op jit(solution)/shard_map/ppermute | solution.py:378
  69.5 6.5 %collective-permute-done.2.recv2.tok2 = bf16[136,768]{1,0:T(8,128)(2,1)S(1)} collective-permute-done((bf16[136,768]{1,0:T(8,128)(2,1)}, bf16[136,768]{1,0:T(8,128)(2,1)S(1)}, u32[]{:S(2)}, u32[]{:S(2)}) %collective-permute-start.2) | collective-permute-done | bytes 208928 | tf_op jit(solution)/shard_map/ppermute | solution.py:378
  76.1 2.0 %collective-permute-start.8 = (bf16[128,768]{1,0:T(8,128)(2,1)S(1)}, bf16[128,768]{1,0:T(8,128)(2,1)S(1)}, u32[]{:S(2)}, u32[]{:S(2)}) collective-permute-start(bf16[128,768]{1,0:T(8,128)(2,1)S(1)} %bitcast.18), channel_id=1, source_target_pairs={{0,96},{32,0},{64,32},{96,64},{128,224},{160,128},{192,160},{224,1... | collective-permute-start | bytes 589832 | tf_op jit(solution)/shard_map/ppermute | solution.py:378
  78.7 5.9 %shard_map.105 = (bf16[768,640]{1,0:T(8,128)(2,1)}, f32[512,384]{1,0:T(8,128)}, f32[4,8,128]{2,1,0:T(8,128)}, bf16[512,640]{1,0:T(8,128)(2,1)}, bf16[512,640]{1,...) custom-call(s32[2]{0:T(128)} %pad_add_fusion.at, bf16[128,768]{1,0:T(8,128)(2,1)} %bitcast.12, ...), custom_call_target="tpu_custom_call" | custom-call | flops 100000000 | bytes 5416960 | tf_op jit(solution)/shard_map/pallas_call | solution.py:38
  84.6 6.8 %collective-permute-start.5 = (bf16[128,384]{1,0:T(8,128)(2,1)}, bf16[128,384]{1,0:T(8,128)(2,1)S(1)}, u32[]{:S(2)}, u32[]{:S(2)}) collective-permute-start(bf16[128,384]{1,0:T(8,128)(2,1)} %get-tuple-element.50), channel_id=1, source_target_pairs={{0,128},{32,160},{64,192},{96,224},{1,129},{33,161},{65,193},{97,2... | collective-permute-start | bytes 294920 | tf_op jit(solution)/shard_map/ppermute | solution.py:445
  91.4 3.2 %shard_map.106.y_in = f32[512,384]{1,0:T(8,128)} custom-call(bf16[512,640]{1,0:T(8,128)(2,1)} %get-tuple-element.47.conv, f32[512,384]{1,0:T(8,128)} %get-tuple-element.48.cum, f32[4,8,128]{2,1,0:T(8,128)} %get-tuple-element.51.cum_t, f32[1,384]{1,0:T(1,128)} %broadcast_in_dim_reshape.3.dskip), custom_call_target="tpu_custom_call" | custom-call | flops 100000000 | bytes 2246144 | tf_op jit(solution)/shard_map/pallas_call | solution.py:38
  95.7 6.6 %shard_map.107 = (f32[512,384]{1,0:T(8,128)}, bf16[4,128,384]{2,1,0:T(8,128)(2,1)}, bf16[512,384]{1,0:T(8,128)(2,1)}, bf16[512,384]{1,0:T(8,128)(2,1)}, bf16[4,1...) custom-call(s32[2]{0:T(128)} %pad_add_fusion.at, bf16[512,640]{1,0:T(8,128)(2,1)} %get-tuple-element.47.conv, ...), custom_call_target="tpu_custom_call" | custom-call | flops 100000000 | bytes 8857088 | tf_op jit(solution)/shard_map/pallas_call | solution.py:38
  103.2 2.1 %collective-permute-start.12 = (f32[2,512]{1,0:T(2,128)}, f32[2,512]{1,0:T(2,128)S(1)}, u32[]{:S(2)}, u32[]{:S(2)}) collective-permute-start(f32[2,512]{1,0:T(2,128)} %get-tuple-element.57.stats0), channel_id=1, source_target_pairs={{0,64},{32,96},{64,0},{96,32},{128,192},{160,224},{192,128},{224,1... | collective-permute-start | bytes 12296 | tf_op jit(solution)/shard_map/ppermute | solution.py:378
  105.3 2.5 %collective-permute-start.13 = (f32[2,512]{1,0:T(2,128)}, f32[2,512]{1,0:T(2,128)S(1)}, u32[]{:S(2)}, u32[]{:S(2)}) collective-permute-start(f32[2,512]{1,0:T(2,128)} %get-tuple-element.57.stats0), channel_id=1, source_target_pairs={{0,96},{32,0},{64,32},{96,64},{128,224},{160,128},{192,160},{224,1... | collective-permute-start | bytes 12296 | tf_op jit(solution)/shard_map/ppermute | solution.py:378
  109.9 5.5 %shard_map.108 = (f32[4,128,128]{2,1,0:T(8,128)}, bf16[512,384]{1,0:T(8,128)(2,1)}, bf16[512,384]{1,0:T(8,128)(2,1)}, bf16[4,128,384]{2,1,0:T(8,128)(2,1)}, bf16...) custom-call(s32[2]{0:T(128)} %pad_add_fusion.at, f32[512,384]{1,0:T(8,128)} %get-tuple-element.54.y, ...), custom_call_target="tpu_custom_call" | custom-call | flops 100000000 | bytes 7128576 | tf_op jit(solution)/shard_map/pallas_call | solution.py:38
  115.6 4.8 %all-to-all-start.2 = ((bf16[4,128,768]{2,1,0:T(8,128)(2,1)}), bf16[4,128,768]{2,1,0:T(8,128)(2,1)S(1)}, u32[]{:S(2)}, u32[]{:S(2)}) async-start(bf16[4,128,768]{2,1,0:T(8,128)(2,1)} %get-tuple-element.64), calls=%async_computation.2 | async-start | bytes 1572864 | tf_op jit(solution)/shard_map/all_to_all | solution.py:381
  120.4 2.8 %collective-permute-start.17 = (bf16[192,384]{1,0:T(8,128)(2,1)S(1)}, bf16[192,384]{1,0:T(8,128)(2,1)S(1)}, u32[]{:S(2)}, u32[]{:S(2)}) collective-permute-start(bf16[192,384]{1,0:T(8,128)(2,1)S(1)} %slice.28), channel_id=1, source_target_pairs={{0,128},{32,160},{64,192},{96,224},{128,0},{160,32},{192,64},{224,... | collective-permute-start | bytes 442376 | tf_op jit(solution)/shard_map/ppermute | solution.py:473
  123.3 4.7 %collective-permute-done.17 = bf16[192,384]{1,0:T(8,128)(2,1)S(1)} collective-permute-done((bf16[192,384]{1,0:T(8,128)(2,1)S(1)}, bf16[192,384]{1,0:T(8,128)(2,1)S(1)}, u32[]{:S(2)}, u32[]{:S(2)}) %collective-permute-start.17) | collective-permute-done | bytes 147488 | tf_op jit(solution)/shard_map/ppermute | solution.py:473
  128.7 4.5 %all-to-all-done.2.parts = bf16[4,128,768]{2,1,0:T(8,128)(2,1)S(1)} async-done(((bf16[4,128,768]{2,1,0:T(8,128)(2,1)}), bf16[4,128,768]{2,1,0:T(8,128)(2,1)S(1)}, u32[]{:S(2)}, u32[]{:S(2)}) %all-to-all-start.2) | async-done | bytes 786464 | tf_op jit(solution)/shard_map/all_to_all | solution.py:381
  133.3 4.7 %all-to-all-start.3 = ((bf16[16,12,384]{2,1,0:T(8,128)(2,1)}), bf16[16,12,384]{2,1,0:T(8,128)(2,1)S(1)}, u32[]{:S(2)}, u32[]{:S(2)}) async-start(bf16[16,12,384]{2,1,0:T(8,128)(2,1)} %reshape.93), calls=%async_computation.3 | async-start | bytes 393216 | tf_op jit(solution)/shard_map/all_to_all | solution.py:481
  139.3 5.0 %shard_map.109 = (bf16[512,384]{1,0:T(8,128)(2,1)}, bf16[512,256]{1,0:T(8,128)(2,1)}, f32[8,640]{1,0:T(8,128)}) custom-call(bf16[512,640]{1,0:T(8,128)(2,1)} %get-tuple-element.47.conv, f32[512,384]{1,0:T(8,128)} %get-tuple-element.48.cum, f32[4,8,128]{2,1,0:T(8,128)} %get-tuple-element.51.cum_t, f32[1,384]{1,0:T(1,128)} %broadcast_in_dim_reshape.3.dskip, ...), custom_call_target="tpu_custom_call" | custom-call | flops 100000000 | bytes 3970560 | tf_op jit(solution)/shard_map/pallas_call | solution.py:38
  144.3 1.5 collective-permute-start.15
  146.9 4.3 %shard_map.110 = (bf16[512,640]{1,0:T(8,128)(2,1)}, bf16[128,768]{1,0:T(8,128)(2,1)}) custom-call(s32[2]{0:T(128)} %pad_add_fusion.at, bf16[512,640]{1,0:T(8,128)(2,1)} %get-tuple-element.47.conv, f32[512,384]{1,0:T(8,128)} %get-tuple-element.48.cum, bf16[4,128,384]{2,1,0:T(8,128)(2,1)} %get-tuple-element.53.full, ...), custom_call_target="tpu_custom_call" | custom-call | flops 100000000 | bytes 5931008 | tf_op jit(solution)/shard_map/pallas_call | solution.py:38
  152.3 5.4 %shard_map.111 = (bf16[128,768]{1,0:T(8,128)(2,1)}, bf16[136,768]{1,0:T(8,128)(2,1)}, bf16[136,768]{1,0:T(8,128)(2,1)}, bf16[136,768]{1,0:T(8,128)(2,1)}, f32[8,384]{1,0:T(8,128)}) custom-call(s32[2]{0:T(128)} %pad_add_fusion.at, bf16[512,640]{1,0:T(8,128)(2,1)} %get-tuple-element.67.gp, f32[8,640]{1,0:T(8,128)} %copy-done.19, ...), custom_call_target="tpu_custom_call" | custom-call | flops 100000000 | bytes 3635200 | tf_op jit(solution)/shard_map/pallas_call | solution.py:38
  158.3 2.1 %collective-permute-start.19 = (bf16[136,768]{1,0:T(8,128)(2,1)}, bf16[136,768]{1,0:T(8,128)(2,1)S(1)}, u32[]{:S(2)}, u32[]{:S(2)}) collective-permute-start(bf16[136,768]{1,0:T(8,128)(2,1)} %get-tuple-element.77), channel_id=1, source_target_pairs={{0,64},{32,96},{64,0},{96,32},{128,192},{160,224},{192,128},{224,1... | collective-permute-start | bytes 626696 | tf_op jit(solution)/shard_map/ppermute | solution.py:378
  161.0 7.6 %collective-permute-done.18.got1 = bf16[136,768]{1,0:T(8,128)(2,1)S(1)} collective-permute-done((bf16[136,768]{1,0:T(8,128)(2,1)}, bf16[136,768]{1,0:T(8,128)(2,1)S(1)}, u32[]{:S(2)}, u32[]{:S(2)}) %collective-permute-start.18) | collective-permute-done | bytes 208928 | tf_op jit(solution)/shard_map/ppermute | solution.py:378
  170.8 1.3 shard_map.112
  (105 shorter events, 18.6 us)
Async XLA Ops:
  3.0 22.2 %copy-start.20 = (bf16[24,384]{1,0:T(8,128)(2,1)S(1)}, bf16[24,384]{1,0:T(8,128)(2,1)}, u32[]{:S(2)}) copy-start(bf16[24,384]{1,0:T(8,128)(2,1)} %get-tuple-element.52) | copy-start | bytes 55300
  3.0 24.9 %all-to-all-start = ((bf16[16,24,640]{2,1,0:T(8,128)(2,1)}), bf16[16,24,640]{2,1,0:T(8,128)(2,1)S(1)}, u32[]{:S(2)}, u32[]{:S(2)}) async-start(bf16[16,24,640]{2,1,0:T(8,128)(2,1)} %get-tuple-element.46), calls=%async_computation | async-start | bytes 983040 | tf_op jit(solution)/shard_map/all_to_all | solution.py:387
  12.8 12.4 %collective-permute-start.9 = (bf16[24,384]{1,0:T(8,128)(2,1)S(1)}, bf16[24,384]{1,0:T(8,128)(2,1)S(1)}, u32[]{:S(2)}, u32[]{:S(2)}) collective-permute-start(bf16[24,384]{1,0:T(8,128)(2,1)S(1)} %constant_dynamic-slice_fusion), channel_id=1, source_target_pairs={{0,0},{1,4},{2,8},{3,12},{4,16},{5,20},{6,24},{7,28},{8,32},{9,36}... | collective-permute-start | bytes 55304 | tf_op jit(solution)/shard_map/ppermute | solution.py:418
  25.2 40.2 %copy-start.26 = (f32[24]{0:T(128)S(1)}, f32[24]{0:T(128)}, u32[]{:S(2)}) copy-start(f32[24]{0:T(128)} %param.14) | copy-start | bytes 292
  25.2 42.2 %slice-start = ((f32[4,1792]{1,0:T(4,128)}), f32[4,1536]{1,0:T(4,128)S(1)}, s32[]{:S(2)}) async-start(f32[4,1792]{1,0:T(4,128)} %param.13), calls=%async_computation.4 | async-start | bytes 49152 | tf_op jit(solution)/shard_map/slice | solution.py:423
  25.2 44.0 %copy-start.9 = (bf16[1,128,768]{2,1,0:T(8,128)(2,1)S(1)}, bf16[1,128,768]{2,1,0:T(8,128)(2,1)}, u32[]{:S(2)}) copy-start(bf16[1,128,768]{2,1,0:T(8,128)(2,1)} %param.9) | copy-start | bytes 589828
  25.2 52.9 %slice-start.1 = ((f32[4,1792]{1,0:T(4,128)}), f32[4,256]{1,0:T(4,128)S(1)}, s32[]{:S(2)}) async-start(f32[4,1792]{1,0:T(4,128)} %param.13), calls=%async_computation.5 | async-start | bytes 8192 | tf_op jit(solution)/shard_map/slice | solution.py:423
  27.9 50.8 %copy-start.5 = (bf16[16,24,640]{2,1,0:T(8,128)(2,1)}, bf16[16,24,640]{2,1,0:T(8,128)(2,1)S(1)}, u32[]{:S(2)}) copy-start(bf16[16,24,640]{2,1,0:T(8,128)(2,1)S(1)} %all-to-all-done.same) | copy-start | bytes 1474564
  28.8 22.9 %all-to-all-start.1 = ((bf16[16,24,768]{2,1,0:T(8,128)(2,1)}), bf16[16,24,768]{2,1,0:T(8,128)(2,1)S(1)}, u32[]{:S(2)}, u32[]{:S(2)}) async-start(bf16[16,24,768]{2,1,0:T(8,128)(2,1)} %broadcast_in_dim.35), calls=%async_computation.1 | async-start | bytes 1179648 | tf_op jit(solution)/shard_map/all_to_all | solution.py:387
  35.3 43.4 %collective-permute-start.4 = (bf16[16,24,640]{2,1,0:T(8,128)(2,1)S(1)}, bf16[16,24,640]{2,1,0:T(8,128)(2,1)}, u32[]{:S(2)}, u32[]{:S(2)}) collective-permute-start(bf16[16,24,640]{2,1,0:T(8,128)(2,1)S(1)} %all-to-all-done.same), channel_id=1, source_target_pairs={{0,1},{1,0},{2,3},{3,2},{4,5},{5,4},{6,7},{7,6},{8,9},{9,8},{10,11... | collective-permute-start | bytes 1474568 | tf_op jit(solution)/shard_map/ppermute | solution.py:388
  51.7 32.9 %copy-start.4 = (bf16[16,24,768]{2,1,0:T(8,128)(2,1)}, bf16[16,24,768]{2,1,0:T(8,128)(2,1)S(1)}, u32[]{:S(2)}) copy-start(bf16[16,24,768]{2,1,0:T(8,128)(2,1)S(1)} %all-to-all-done.1.same) | copy-start | bytes 1769476
  51.7 43.0 %collective-permute-start.10 = (bf16[16,24,768]{2,1,0:T(8,128)(2,1)S(1)}, bf16[16,24,768]{2,1,0:T(8,128)(2,1)S(1)}, u32[]{:S(2)}, u32[]{:S(2)}) collective-permute-start(bf16[16,24,768]{2,1,0:T(8,128)(2,1)S(1)} %all-to-all-done.1.same), channel_id=1, source_target_pairs={{0,1},{1,0},{2,3},{3,2},{4,5},{5,4},{6,7},{7,6},{8,9},{9,8},{10,11... | collective-permute-start | bytes 1769480 | tf_op jit(solution)/shard_map/ppermute | solution.py:388
  52.4 0.7 collective-permute-start
  55.7 13.5 %collective-permute-start.1 = (bf16[136,768]{1,0:T(8,128)(2,1)}, bf16[136,768]{1,0:T(8,128)(2,1)S(1)}, u32[]{:S(2)}, u32[]{:S(2)}) collective-permute-start(bf16[136,768]{1,0:T(8,128)(2,1)} %get-tuple-element.43), channel_id=1, source_target_pairs={{0,32},{32,64},{64,96},{96,0},{128,160},{160,192},{192,224},{224,1... | collective-permute-start | bytes 626696 | tf_op jit(solution)/shard_map/ppermute | solution.py:378
  57.0 19.0 %collective-permute-start.2 = (bf16[136,768]{1,0:T(8,128)(2,1)}, bf16[136,768]{1,0:T(8,128)(2,1)S(1)}, u32[]{:S(2)}, u32[]{:S(2)}) collective-permute-start(bf16[136,768]{1,0:T(8,128)(2,1)} %get-tuple-element.44), channel_id=1, source_target_pairs={{0,64},{32,96},{64,0},{96,32},{128,192},{160,224},{192,128},{224,1... | collective-permute-start | bytes 626696 | tf_op jit(solution)/shard_map/ppermute | solution.py:378
  65.3 10.7 %collective-permute-start.3 = (bf16[136,768]{1,0:T(8,128)(2,1)}, bf16[136,768]{1,0:T(8,128)(2,1)S(1)}, u32[]{:S(2)}, u32[]{:S(2)}) collective-permute-start(bf16[136,768]{1,0:T(8,128)(2,1)} %get-tuple-element.45), channel_id=1, source_target_pairs={{0,96},{32,0},{64,32},{96,64},{128,224},{160,128},{192,160},{224,1... | collective-permute-start | bytes 626696 | tf_op jit(solution)/shard_map/ppermute | solution.py:378
  69.2 25.4 %collective-permute-start.6 = (bf16[128,768]{1,0:T(8,128)(2,1)S(1)}, bf16[128,768]{1,0:T(8,128)(2,1)S(1)}, u32[]{:S(2)}, u32[]{:S(2)}) collective-permute-start(bf16[128,768]{1,0:T(8,128)(2,1)S(1)} %bitcast.16), channel_id=1, source_target_pairs={{0,32},{32,64},{64,96},{96,0},{128,160},{160,192},{192,224},{224,1... | collective-permute-start | bytes 589832 | tf_op jit(solution)/shard_map/ppermute | solution.py:378
  76.0 18.6 %collective-permute-start.7 = (bf16[128,768]{1,0:T(8,128)(2,1)S(1)}, bf16[128,768]{1,0:T(8,128)(2,1)S(1)}, u32[]{:S(2)}, u32[]{:S(2)}) collective-permute-start(bf16[128,768]{1,0:T(8,128)(2,1)S(1)} %bitcast.17), channel_id=1, source_target_pairs={{0,64},{32,96},{64,0},{96,32},{128,192},{160,224},{192,128},{224,1... | collective-permute-start | bytes 589832 | tf_op jit(solution)/shard_map/ppermute | solution.py:378
  76.1 18.6 %collective-permute-start.8 = (bf16[128,768]{1,0:T(8,128)(2,1)S(1)}, bf16[128,768]{1,0:T(8,128)(2,1)S(1)}, u32[]{:S(2)}, u32[]{:S(2)}) collective-permute-start(bf16[128,768]{1,0:T(8,128)(2,1)S(1)} %bitcast.18), channel_id=1, source_target_pairs={{0,96},{32,0},{64,32},{96,64},{128,224},{160,128},{192,160},{224,1... | collective-permute-start | bytes 589832 | tf_op jit(solution)/shard_map/ppermute | solution.py:378
  84.6 10.0 %collective-permute-start.5 = (bf16[128,384]{1,0:T(8,128)(2,1)}, bf16[128,384]{1,0:T(8,128)(2,1)S(1)}, u32[]{:S(2)}, u32[]{:S(2)}) collective-permute-start(bf16[128,384]{1,0:T(8,128)(2,1)} %get-tuple-element.50), channel_id=1, source_target_pairs={{0,128},{32,160},{64,192},{96,224},{1,129},{33,161},{65,193},{97,2... | collective-permute-start | bytes 294920 | tf_op jit(solution)/shard_map/ppermute | solution.py:445
  102.3 6.8 %collective-permute-start.11 = (f32[2,512]{1,0:T(2,128)}, f32[2,512]{1,0:T(2,128)S(1)}, u32[]{:S(2)}, u32[]{:S(2)}) collective-permute-start(f32[2,512]{1,0:T(2,128)} %get-tuple-element.57.stats0), channel_id=1, source_target_pairs={{0,32},{32,64},{64,96},{96,0},{128,160},{160,192},{192,224},{224,1... | collective-permute-start | bytes 12296 | tf_op jit(solution)/shard_map/ppermute | solution.py:378
  103.2 5.9 %collective-permute-start.12 = (f32[2,512]{1,0:T(2,128)}, f32[2,512]{1,0:T(2,128)S(1)}, u32[]{:S(2)}, u32[]{:S(2)}) collective-permute-start(f32[2,512]{1,0:T(2,128)} %get-tuple-element.57.stats0), channel_id=1, source_target_pairs={{0,64},{32,96},{64,0},{96,32},{128,192},{160,224},{192,128},{224,1... | collective-permute-start | bytes 12296 | tf_op jit(solution)/shard_map/ppermute | solution.py:378
  105.3 4.1 %collective-permute-start.13 = (f32[2,512]{1,0:T(2,128)}, f32[2,512]{1,0:T(2,128)S(1)}, u32[]{:S(2)}, u32[]{:S(2)}) collective-permute-start(f32[2,512]{1,0:T(2,128)} %get-tuple-element.57.stats0), channel_id=1, source_target_pairs={{0,96},{32,0},{64,32},{96,64},{128,224},{160,128},{192,160},{224,1... | collective-permute-start | bytes 12296 | tf_op jit(solution)/shard_map/ppermute | solution.py:378
  115.5 4.9 %collective-permute-start.16 = (bf16[384,384]{1,0:T(8,128)(2,1)}, bf16[384,384]{1,0:T(8,128)(2,1)S(1)}, u32[]{:S(2)}, u32[]{:S(2)}) collective-permute-start(bf16[384,384]{1,0:T(8,128)(2,1)} %get-tuple-element.73), channel_id=1, source_target_pairs={{0,1},{1,0},{2,3},{3,2},{4,5},{5,4},{6,7},{7,6},{8,9},{9,8},{10,11... | collective-permute-start | bytes 884744 | tf_op jit(solution)/shard_map/ppermute | solution.py:470
  115.6 17.7 %all-to-all-start.2 = ((bf16[4,128,768]{2,1,0:T(8,128)(2,1)}), bf16[4,128,768]{2,1,0:T(8,128)(2,1)S(1)}, u32[]{:S(2)}, u32[]{:S(2)}) async-start(bf16[4,128,768]{2,1,0:T(8,128)(2,1)} %get-tuple-element.64), calls=%async_computation.2 | async-start | bytes 1572864 | tf_op jit(solution)/shard_map/all_to_all | solution.py:381
  120.4 7.5 %collective-permute-start.17 = (bf16[192,384]{1,0:T(8,128)(2,1)S(1)}, bf16[192,384]{1,0:T(8,128)(2,1)S(1)}, u32[]{:S(2)}, u32[]{:S(2)}) collective-permute-start(bf16[192,384]{1,0:T(8,128)(2,1)S(1)} %slice.28), channel_id=1, source_target_pairs={{0,128},{32,160},{64,192},{96,224},{128,0},{160,32},{192,64},{224,... | collective-permute-start | bytes 442376 | tf_op jit(solution)/shard_map/ppermute | solution.py:473
  133.3 18.4 %all-to-all-start.3 = ((bf16[16,12,384]{2,1,0:T(8,128)(2,1)}), bf16[16,12,384]{2,1,0:T(8,128)(2,1)S(1)}, u32[]{:S(2)}, u32[]{:S(2)}) async-start(bf16[16,12,384]{2,1,0:T(8,128)(2,1)} %reshape.93), calls=%async_computation.3 | async-start | bytes 393216 | tf_op jit(solution)/shard_map/all_to_all | solution.py:481
  138.0 8.3 %collective-permute-start.14 = (bf16[128,384]{1,0:T(8,128)(2,1)S(1)}, bf16[128,384]{1,0:T(8,128)(2,1)S(1)}, u32[]{:S(2)}, u32[]{:S(2)}) collective-permute-start(bf16[128,384]{1,0:T(8,128)(2,1)S(1)} %copy-done.24), channel_id=1, source_target_pairs={{128,0},{160,32},{192,64},{224,96},{129,1},{161,33},{193,65},{225,... | collective-permute-start | bytes 294920 | tf_op jit(solution)/shard_map/ppermute | solution.py:469
  144.3 7.4 %collective-permute-start.15 = (f32[8,640]{1,0:T(8,128)}, f32[8,640]{1,0:T(8,128)S(1)}, u32[]{:S(2)}, u32[]{:S(2)}) collective-permute-start(f32[8,640]{1,0:T(8,128)} %get-tuple-element.68), channel_id=1, source_target_pairs={{128,0},{160,32},{192,64},{224,96},{129,1},{161,33},{193,65},{225,... | collective-permute-start | bytes 61448 | tf_op jit(solution)/shard_map/ppermute | solution.py:479
  157.7 10.9 %collective-permute-start.18 = (bf16[136,768]{1,0:T(8,128)(2,1)}, bf16[136,768]{1,0:T(8,128)(2,1)S(1)}, u32[]{:S(2)}, u32[]{:S(2)}) collective-permute-start(bf16[136,768]{1,0:T(8,128)(2,1)} %get-tuple-element.76), channel_id=1, source_target_pairs={{0,32},{32,64},{64,96},{96,0},{128,160},{160,192},{192,224},{224,1... | collective-permute-start | bytes 626696 | tf_op jit(solution)/shard_map/ppermute | solution.py:378
  158.3 10.3 %collective-permute-start.19 = (bf16[136,768]{1,0:T(8,128)(2,1)}, bf16[136,768]{1,0:T(8,128)(2,1)S(1)}, u32[]{:S(2)}, u32[]{:S(2)}) collective-permute-start(bf16[136,768]{1,0:T(8,128)(2,1)} %get-tuple-element.77), channel_id=1, source_target_pairs={{0,64},{32,96},{64,0},{96,32},{128,192},{160,224},{192,128},{224,1... | collective-permute-start | bytes 626696 | tf_op jit(solution)/shard_map/ppermute | solution.py:378
  160.3 8.9 %collective-permute-start.20 = (bf16[136,768]{1,0:T(8,128)(2,1)}, bf16[136,768]{1,0:T(8,128)(2,1)S(1)}, u32[]{:S(2)}, u32[]{:S(2)}) collective-permute-start(bf16[136,768]{1,0:T(8,128)(2,1)} %get-tuple-element.78), channel_id=1, source_target_pairs={{0,96},{32,0},{64,32},{96,64},{128,224},{160,128},{192,160},{224,1... | collective-permute-start | bytes 626696 | tf_op jit(solution)/shard_map/ppermute | solution.py:378
  (22 other events, 87.3 us)

commit v4 on v3

--- a/solution.py
+++ b/solution.py
@@ -32,14 +32,14 @@
 
 
 def kernel_call(body, outs, *args, scalars=None, scratch=(), flops=10**8, limit=None):
-    spec = pl.BlockSpec(memory_space=pltpu.VMEM)
+    near = pl.BlockSpec(memory_space=pltpu.VMEM)
     size = sum(a.size * a.dtype.itemsize for a in list(args) + list(outs))
     first = [] if scalars is None else [scalars]
     return pl.pallas_call(
         body,
         out_shape=outs,
-        in_specs=[pl.BlockSpec(memory_space=pltpu.SMEM)] * len(first) + [spec] * len(args),
-        out_specs=[spec] * len(outs),
+        in_specs=[pl.BlockSpec(memory_space=pltpu.SMEM)] * len(first) + [near] * len(args),
+        out_specs=[near] * len(outs),
         scratch_shapes=list(scratch),
         compiler_params=pltpu.CompilerParams(vmem_limit_bytes=limit),
         cost_estimate=pl.CostEstimate(flops=flops, bytes_accessed=size, transcendentals=0),
@@ -120,7 +120,7 @@
 
 
 def project(at, tokens, aux, recv1, recv2, recv3, same, other, conv_w,
-            w_mix, cum, cum_t, pre, conv, states, last, mix):
+            w_mix, cum, cum_t, pre, conv, states, last, pre0, mix):
     width = last.shape[1]
     chunks = XS
     block = CHUNK
@@ -160,6 +160,7 @@
         faded = jnp.exp(end - cum[r, :]) * conv[r, :width].astype(f32)
         state = jnp.exp(end) * state + dot(conv[r, width : width + 128], faded, TN)
     last[...] = state.astype(bf16)
+    pre0[...] = pre[: pre0.shape[0], :]
 
 
 def inside(conv, cum, cum_t, dskip, y):
@@ -182,7 +183,7 @@
 
 def gated(at, conv, cum, states, entering, y_in, tok0, tok1, tok2, tok3, cot0, cot1, cot2, cot3,
           same, other, norm_w,
-          y, full, gate, dn, part, stats, w_gate, raw, w_out):
+          y, full, gate, dn, part, stats, w_gate, full0, raw, w_out):
     width = y.shape[1]
     chunks = y.shape[0] // CHUNK
     assemble(at, same, other, w_gate, slice(0, width))
@@ -201,6 +202,8 @@
         r = rows_of(c)
         state = states[c].astype(f32) + carried
         full[c] = state.astype(bf16)
+        if c == 0:
+            full0[...] = state.astype(bf16)
         carried = jnp.exp(cum[(c + 1) * CHUNK - 1 : (c + 1) * CHUNK, :]) * carried
         value = y_in[r, :].astype(f32) + jnp.exp(cum[r, :]) * dot(conv[r, width + 128 : width + 256], state)
         y[r, :] = value
@@ -216,7 +219,7 @@
 
 def normed_part(inner, at, y, gate, dn, stats0, stats1, stats2, stats3, conv, cum, norm_w,
                 cot0, cot1, cot2, cot3, perm,
-                factors, dgate, dy, ends, first, keep, give, low, cot):
+                factors, dgate, dy, ends, first, keep, give, ends0, low, cot):
     width = y.shape[1]
     chunks = y.shape[0] // CHUNK
     adjoint = jnp.zeros(first.shape, f32)
@@ -237,6 +240,8 @@
         dy[r, :] = dvalue.astype(bf16)
         dgate[r, :] = (dg * value * q * (1.0 + z * (1.0 - q))).astype(bf16)
         ends[c] = adjoint.astype(bf16)
+        if c == 0:
+            ends0[...] = adjoint.astype(bf16)
         end = cum[(c + 1) * CHUNK - 1 : (c + 1) * CHUNK, :]
         adjoint = jnp.exp(end) * adjoint + dot(
             conv[r, width + 128 : width + 256], jnp.exp(cum[r, :]) * dvalue, TN
@@ -249,7 +254,7 @@
     keep[...] = dot(perm[: keep.shape[0], :], summed).astype(bf16)
 
 
-def inside_back(conv, cum, cum_t, dskip, dy, full, ends, pre, dx, dbc, head):
+def inside_back(conv, cum, cum_t, dskip, dy, full0, ends0, pre, dx, dbc, head):
     width = dy.shape[1]
     left = halves()
     for c in range(dy.shape[0] // CHUNK):
@@ -270,7 +275,7 @@
             dscores = dscores + fa * dot(da, x, NT) + fb * dot(db, x, NT)
         dbc[r, :128] = dot(dscores, cv, TN).astype(dbc.dtype)
         dbc[r, 128:] = dot(dscores, b).astype(dbc.dtype)
-    first = conv_rows(conv, cum, full[0], ends[0], dy, dx, dbc, pre, 0, 16)
+    first = conv_rows(conv, cum, full0[...], ends0[...], dy, dx, dbc, pre, 0, 16)
     for lanes, value in first:
         head[:, lanes] = value[:8]
 
@@ -408,15 +413,15 @@
     for r in range(1, XS):
         recv.append(along_x(sends[r - 1], r))
         cots.append(along_x(cotangent[0], r))
-    piece = 2 * out_w.shape[0] // XS
+    piece = out_w.shape[0] // XS
     routes = []
     for t in range(tm):
         for s in range(stream):
             group, place_ = divmod(s, stream // XS)
             target = (t // XS * XS + group, XS * place_ + t % XS)
             routes.append((t * stream + s, target[0] * stream + target[1]))
-    out_piece = lax.ppermute(own(out_w.reshape(-1, width), 0, piece), ("tm", "stream"), routes)
-    wide2 = jnp.concatenate([gate_w, out_piece], axis=1)
+    out_piece = lax.ppermute(own(out_w, 0, piece), ("tm", "stream"), routes)
+    wide2 = jnp.concatenate([gate_w, out_piece.reshape(short, width)], axis=1)
     wide2 = jnp.broadcast_to(wide2[None], (half,) + wide2.shape)
     same2, other2 = gather_weights(wide2)
 
@@ -433,22 +438,22 @@
     perm = (source[:, None] == index[None, :]).astype(bf16)
 
     chunks = rows // CHUNK
-    w_mix, cum, cum_t, pre, conv, states, last = kernel_call(
+    w_mix, cum, cum_t, pre, conv, states, last, pre0 = kernel_call(
         project,
         [out((model, mixed), bf16), out((rows, width), f32), out((chunks, 8, CHUNK), f32),
          out((rows, mixed), bf16), out((rows, mixed), bf16), out((chunks, state, width), bf16),
-         out((state, width), bf16)],
+         out((state, width), bf16), out((16, mixed), bf16)],
         tokens[0], aux, *recv, same1, other1, taps,
         scalars=at,
         scratch=[pltpu.VMEM((rows + 8, mixed), f32)],
     )
     entering = lax.ppermute(last, "tm", up)
     (y_in,) = kernel_call(inside, [out((rows, width), f32)], conv, cum, cum_t, skip)
-    y, full, gate, dn, part, stats, w_gate = kernel_call(
+    y, full, gate, dn, part, stats, w_gate, full0 = kernel_call(
         gated,
         [out((rows, width), f32), out(states.shape, bf16), out((rows, width), bf16),
          out((rows, width), bf16), out((XS, block, model), bf16), out((2, rows), f32),
-         out((model, width), bf16)],
+         out((model, width), bf16), out((state, width), bf16)],
         conv, cum, states, entering, y_in, tokens[0], *recv, *cots, same2, other2, gain,
         scalars=at,
         scratch=[pltpu.VMEM((width // LANES, model, LANES), f32), pltpu.VMEM((width, model), bf16)],
@@ -457,11 +462,11 @@
     for r in range(1, XS):
         others.append(along_x(stats, r))
     parts = swap_x(part)
-    factors, dgate, dy, ends, first, keep, give = kernel_call(
+    factors, dgate, dy, ends, first, keep, give, ends0 = kernel_call(
         functools.partial(normed_part, inner),
         [out((chunks, CHUNK, LANES), f32), out((rows, width), bf16), out((rows, width), bf16),
          out(states.shape, bf16), out((state, width), bf16), out((model // 2, width), bf16),
-         out((model // 2, width), bf16)],
+         out((model // 2, width), bf16), out((state, width), bf16)],
         y, gate, dn, stats, *others, conv, cum, gain, *cots, perm,
         scalars=at,
         scratch=[pltpu.VMEM((rows, width), bf16), pltpu.VMEM((rows, model), bf16)],
@@ -474,7 +479,7 @@
     dx, dbc, head = kernel_call(
         inside_back,
         [out((rows, width), bf16), out((rows, 2 * state), bf16), out((8, mixed), f32)],
-        conv, cum, cum_t, skip, dy, full, ends, pre,
+        conv, cum, cum_t, skip, dy, full0, ends0, pre0,
     )
     after = lax.ppermute(head, "tm", down)
     pair = (pair[:quarter] + crossed.astype(f32)).astype(bf16)

time: 175 us -> 175 us (level)
    unnamed x54 -> x52, local copies, waits for them, and re-layouts: 5.21 us -> 5.17 us
  transfers between devices with their start and end apart: 25 -> 25, of which waited for: 12 -> 11; matrix products, arithmetic and copies ran while one was open for 3% -> 4% of each run, Pallas kernels for 12% -> 12%
where the time goes in v4:
time: 175 us; the launch traced here: 173 us
  starting transfers between devices  67.1 us (38%)
  waiting for transfers between devices  51.2 us (29%)
  Pallas kernels  40.6 us (23%)
  local copies, waits for them, and re-layouts  9.74 us (6%)
  other arithmetic  3.27 us (2%)
    pallas_call x10, Pallas kernels, kernel_call(): pl.pallas_call(body, out_shape=outs, in_specs=[pl.BlockSpec(memory_space=...  40.6 us
    ppermute x12, starting transfers between devices, along_x(): return lax.ppermute(array, 'tm', pairs)  21 us
    all_to_all x2, waiting for transfers between devices, gather_weights(): same = lax.all_to_all(wide, 'stream', 0, 0, axis_index_groups=cores)  18 us
    all_to_all x2, starting transfers between devices, gather_weights(): same = lax.all_to_all(wide, 'stream', 0, 0, axis_index_groups=cores)  17.1 us
    ppermute x12, waiting for transfers between devices, along_x(): return lax.ppermute(array, 'tm', pairs)  16.8 us
    ppermute x1, starting transfers between devices, shards(): entering = lax.ppermute(last, 'tm', up)  6.76 us
    ppermute x1, starting transfers between devices, shards(): out_piece = lax.ppermute(own(out_w, 0, piece), ('tm', 'stream'), routes)  6.38 us
    ppermute x1, waiting for transfers between devices, shards(): out_piece = lax.ppermute(own(out_w, 0, piece), ('tm', 'stream'), routes)  6.29 us
  transfers between devices with their start and end apart: 25, of which 11 were waited for; matrix products, arithmetic and copies ran while one was open for 4% of the time, Pallas kernels for 12%

profile of v4, /device:TPU:32, one launch (start us, length us, event | category | flops | bytes accessed | tf_op | source)
XLA Modules:
  0.0 172.9 jit_solution(7176307298638282502)
XLA Ops:
  1.2 1.8 %shard_map.104 = (bf16[16,24,640]{2,1,0:T(8,128)(2,1)}, bf16[24,384]{1,0:T(8,128)(2,1)}) custom-call(s32[2]{0:T(128)} %pad_add_fusion.at, bf16[24,3328]{1,0:T(8,128)(2,1)} %in_w.1), custom_call_target="tpu_custom_call" | custom-call | flops 100000000 | bytes 669696 | tf_op jit(solution)/shard_map/pallas_call | solution.py:38
  3.0 9.6 %all-to-all-start = ((bf16[16,24,640]{2,1,0:T(8,128)(2,1)}), bf16[16,24,640]{2,1,0:T(8,128)(2,1)S(1)}, u32[]{:S(2)}, u32[]{:S(2)}) async-start(bf16[16,24,640]{2,1,0:T(8,128)(2,1)} %get-tuple-element.49), calls=%async_computation | async-start | bytes 983040 | tf_op jit(solution)/shard_map/all_to_all | solution.py:392
  12.6 6.4 %collective-permute-start.9 = (bf16[12,768]{1,0:T(8,128)(2,1)S(1)}, bf16[12,768]{1,0:T(8,128)(2,1)S(1)}, u32[]{:S(2)}, u32[]{:S(2)}) collective-permute-start(bf16[12,768]{1,0:T(8,128)(2,1)S(1)} %constant_dynamic-slice_fusion), channel_id=1, source_target_pairs={{0,0},{1,4},{2,8},{3,12},{4,16},{5,20},{6,24},{7,28},{8,32},{9,36}... | collective-permute-start | bytes 55304 | tf_op jit(solution)/shard_map/ppermute | solution.py:423
  19.0 6.3 %collective-permute-done.9 = bf16[12,768]{1,0:T(8,128)(2,1)S(1)} collective-permute-done((bf16[12,768]{1,0:T(8,128)(2,1)S(1)}, bf16[12,768]{1,0:T(8,128)(2,1)S(1)}, u32[]{:S(2)}, u32[]{:S(2)}) %collective-permute-start.9) | collective-permute-done | bytes 18464 | tf_op jit(solution)/shard_map/ppermute | solution.py:423
  26.0 1.7 all-to-all-done.same
  28.6 7.5 %all-to-all-start.1 = ((bf16[16,24,768]{2,1,0:T(8,128)(2,1)}), bf16[16,24,768]{2,1,0:T(8,128)(2,1)S(1)}, u32[]{:S(2)}, u32[]{:S(2)}) async-start(bf16[16,24,768]{2,1,0:T(8,128)(2,1)} %broadcast_in_dim.35), calls=%async_computation.1 | async-start | bytes 1179648 | tf_op jit(solution)/shard_map/all_to_all | solution.py:392
  36.1 16.4 %all-to-all-done.1.same = bf16[16,24,768]{2,1,0:T(8,128)(2,1)S(1)} async-done(((bf16[16,24,768]{2,1,0:T(8,128)(2,1)}), bf16[16,24,768]{2,1,0:T(8,128)(2,1)S(1)}, u32[]{:S(2)}, u32[]{:S(2)}) %all-to-all-start.1) | async-done | bytes 589856 | tf_op jit(solution)/shard_map/all_to_all | solution.py:392
  54.5 2.0 %shard_map.103 = (bf16[8,768]{1,0:T(8,128)(2,1)}, bf16[136,768]{1,0:T(8,128)(2,1)}, bf16[136,768]{1,0:T(8,128)(2,1)}, bf16[136,768]{1,0:T(8,128)(2,1)}) custom-call(s32[2]{0:T(128)} %pad_add_fusion.at, f32[24,128]{1,0:T(8,128)} %bitcast.21, bf16[128,768]{1,0:T(8,128)(2,1)} %bitcast.11, bf16[8,768]{1,0:T(8,128)(2,1)} %copy-done.24), custom_call_target="tpu_custom_call" | custom-call | flops 100000000 | bytes 860160 | tf_op jit(solution)/shard_map/pallas_call | solution.py:38
  56.5 1.3 collective-permute-start.1
  57.8 8.3 %collective-permute-start.2 = (bf16[136,768]{1,0:T(8,128)(2,1)}, bf16[136,768]{1,0:T(8,128)(2,1)S(1)}, u32[]{:S(2)}, u32[]{:S(2)}) collective-permute-start(bf16[136,768]{1,0:T(8,128)(2,1)} %get-tuple-element.47), channel_id=1, source_target_pairs={{0,64},{32,96},{64,0},{96,32},{128,192},{160,224},{192,128},{224,1... | collective-permute-start | bytes 626696 | tf_op jit(solution)/shard_map/ppermute | solution.py:383
  68.3 1.7 collective-permute-done.1.recv1.tok1
  70.4 6.4 %collective-permute-done.2.recv2.tok2 = bf16[136,768]{1,0:T(8,128)(2,1)S(1)} collective-permute-done((bf16[136,768]{1,0:T(8,128)(2,1)}, bf16[136,768]{1,0:T(8,128)(2,1)S(1)}, u32[]{:S(2)}, u32[]{:S(2)}) %collective-permute-start.2) | collective-permute-done | bytes 208928 | tf_op jit(solution)/shard_map/ppermute | solution.py:383
  76.8 2.0 %collective-permute-start.8 = (bf16[128,768]{1,0:T(8,128)(2,1)S(1)}, bf16[128,768]{1,0:T(8,128)(2,1)S(1)}, u32[]{:S(2)}, u32[]{:S(2)}) collective-permute-start(bf16[128,768]{1,0:T(8,128)(2,1)S(1)} %bitcast.18), channel_id=1, source_target_pairs={{0,96},{32,0},{64,32},{96,64},{128,224},{160,128},{192,160},{224,1... | collective-permute-start | bytes 589832 | tf_op jit(solution)/shard_map/ppermute | solution.py:383
  79.5 5.9 %shard_map.105 = (bf16[768,640]{1,0:T(8,128)(2,1)}, f32[512,384]{1,0:T(8,128)}, f32[4,8,128]{2,1,0:T(8,128)}, bf16[512,640]{1,0:T(8,128)(2,1)}, bf16[512,640]{1,...) custom-call(s32[2]{0:T(128)} %pad_add_fusion.at, ...), custom_call_target="tpu_custom_call" | custom-call | flops 100000000 | bytes 5437440 | tf_op jit(solution)/shard_map/pallas_call | solution.py:38
  85.5 6.8 %collective-permute-start.5 = (bf16[128,384]{1,0:T(8,128)(2,1)}, bf16[128,384]{1,0:T(8,128)(2,1)S(1)}, u32[]{:S(2)}, u32[]{:S(2)}) collective-permute-start(bf16[128,384]{1,0:T(8,128)(2,1)} %get-tuple-element.53), channel_id=1, source_target_pairs={{0,128},{32,160},{64,192},{96,224},{1,129},{33,161},{65,193},{97,2... | collective-permute-start | bytes 294920 | tf_op jit(solution)/shard_map/ppermute | solution.py:450
  92.3 3.1 %shard_map.106.y_in = f32[512,384]{1,0:T(8,128)} custom-call(bf16[512,640]{1,0:T(8,128)(2,1)} %get-tuple-element.50.conv, f32[512,384]{1,0:T(8,128)} %get-tuple-element.51.cum, f32[4,8,128]{2,1,0:T(8,128)} %get-tuple-element.54.cum_t, f32[1,384]{1,0:T(1,128)} %broadcast_in_dim_reshape.3.dskip), custom_call_target="tpu_custom_call" | custom-call | flops 100000000 | bytes 2246144 | tf_op jit(solution)/shard_map/pallas_call | solution.py:38
  96.4 6.6 %shard_map.107 = (f32[512,384]{1,0:T(8,128)}, bf16[4,128,384]{2,1,0:T(8,128)(2,1)}, bf16[512,384]{1,0:T(8,128)(2,1)}, bf16[512,384]{1,0:T(8,128)(2,1)}, bf16[4,1...) custom-call(s32[2]{0:T(128)} %pad_add_fusion.at, ...), custom_call_target="tpu_custom_call" | custom-call | flops 100000000 | bytes 8955392 | tf_op jit(solution)/shard_map/pallas_call | solution.py:38
  104.0 2.1 %collective-permute-start.12 = (f32[2,512]{1,0:T(2,128)}, f32[2,512]{1,0:T(2,128)S(1)}, u32[]{:S(2)}, u32[]{:S(2)}) collective-permute-start(f32[2,512]{1,0:T(2,128)} %get-tuple-element.60.stats0), channel_id=1, source_target_pairs={{0,64},{32,96},{64,0},{96,32},{128,192},{160,224},{192,128},{224,1... | collective-permute-start | bytes 12296 | tf_op jit(solution)/shard_map/ppermute | solution.py:383
  106.1 2.5 %collective-permute-start.13 = (f32[2,512]{1,0:T(2,128)}, f32[2,512]{1,0:T(2,128)S(1)}, u32[]{:S(2)}, u32[]{:S(2)}) collective-permute-start(f32[2,512]{1,0:T(2,128)} %get-tuple-element.60.stats0), channel_id=1, source_target_pairs={{0,96},{32,0},{64,32},{96,64},{128,224},{160,128},{192,160},{224,1... | collective-permute-start | bytes 12296 | tf_op jit(solution)/shard_map/ppermute | solution.py:383
  110.8 5.5 %shard_map.108 = (f32[4,128,128]{2,1,0:T(8,128)}, bf16[512,384]{1,0:T(8,128)(2,1)}, bf16[512,384]{1,0:T(8,128)(2,1)}, bf16[4,128,384]{2,1,0:T(8,128)(2,1)}, bf16...) custom-call(s32[2]{0:T(128)} %pad_add_fusion.at, ...), custom_call_target="tpu_custom_call" | custom-call | flops 100000000 | bytes 7226880 | tf_op jit(solution)/shard_map/pallas_call | solution.py:38
  116.4 4.8 %all-to-all-start.2 = ((bf16[4,128,768]{2,1,0:T(8,128)(2,1)}), bf16[4,128,768]{2,1,0:T(8,128)(2,1)S(1)}, u32[]{:S(2)}, u32[]{:S(2)}) async-start(bf16[4,128,768]{2,1,0:T(8,128)(2,1)} %get-tuple-element.70), calls=%async_computation.2 | async-start | bytes 1572864 | tf_op jit(solution)/shard_map/all_to_all | solution.py:386
  121.3 2.9 %collective-permute-start.17 = (bf16[192,384]{1,0:T(8,128)(2,1)S(1)}, bf16[192,384]{1,0:T(8,128)(2,1)S(1)}, u32[]{:S(2)}, u32[]{:S(2)}) collective-permute-start(bf16[192,384]{1,0:T(8,128)(2,1)S(1)} %slice.28), channel_id=1, source_target_pairs={{0,128},{32,160},{64,192},{96,224},{128,0},{160,32},{192,64},{224,... | collective-permute-start | bytes 442376 | tf_op jit(solution)/shard_map/ppermute | solution.py:478
  124.1 4.7 %collective-permute-done.17 = bf16[192,384]{1,0:T(8,128)(2,1)S(1)} collective-permute-done((bf16[192,384]{1,0:T(8,128)(2,1)S(1)}, bf16[192,384]{1,0:T(8,128)(2,1)S(1)}, u32[]{:S(2)}, u32[]{:S(2)}) %collective-permute-start.17) | collective-permute-done | bytes 147488 | tf_op jit(solution)/shard_map/ppermute | solution.py:478
  129.6 4.5 %all-to-all-done.2.parts = bf16[4,128,768]{2,1,0:T(8,128)(2,1)S(1)} async-done(((bf16[4,128,768]{2,1,0:T(8,128)(2,1)}), bf16[4,128,768]{2,1,0:T(8,128)(2,1)S(1)}, u32[]{:S(2)}, u32[]{:S(2)}) %all-to-all-start.2) | async-done | bytes 786464 | tf_op jit(solution)/shard_map/all_to_all | solution.py:386
  134.1 4.7 %all-to-all-start.3 = ((bf16[16,12,384]{2,1,0:T(8,128)(2,1)}), bf16[16,12,384]{2,1,0:T(8,128)(2,1)S(1)}, u32[]{:S(2)}, u32[]{:S(2)}) async-start(bf16[16,12,384]{2,1,0:T(8,128)(2,1)} %reshape.93), calls=%async_computation.3 | async-start | bytes 393216 | tf_op jit(solution)/shard_map/all_to_all | solution.py:486
  140.1 4.6 %shard_map.109 = (bf16[512,384]{1,0:T(8,128)(2,1)}, bf16[512,256]{1,0:T(8,128)(2,1)}, f32[8,640]{1,0:T(8,128)}) custom-call(bf16[512,640]{1,0:T(8,128)(2,1)} %get-tuple-element.50.conv, f32[512,384]{1,0:T(8,128)} %get-tuple-element.51.cum, f32[4,8,128]{2,1,0:T(8,128)} %get-tuple-element.54.cum_t, f32[1,384]{1,0:T(1,128)} %broadcast_in_dim_reshape.3.dskip, ...), custom_call_target="tpu_custom_call" | custom-call | flops 100000000 | bytes 2745856 | tf_op jit(solution)/shard_map/pallas_call | solution.py:38
  144.7 1.5 collective-permute-start.15
  147.7 4.3 %shard_map.110 = (bf16[512,640]{1,0:T(8,128)(2,1)}, bf16[128,768]{1,0:T(8,128)(2,1)}) custom-call(s32[2]{0:T(128)} %pad_add_fusion.at, bf16[512,640]{1,0:T(8,128)(2,1)} %get-tuple-element.50.conv, f32[512,384]{1,0:T(8,128)} %get-tuple-element.51.cum, bf16[4,128,384]{2,1,0:T(8,128)(2,1)} %get-tuple-element.56.full, ...), custom_call_target="tpu_custom_call" | custom-call | flops 100000000 | bytes 5931008 | tf_op jit(solution)/shard_map/pallas_call | solution.py:38
  152.8 5.3 %shard_map.111 = (bf16[128,768]{1,0:T(8,128)(2,1)}, bf16[136,768]{1,0:T(8,128)(2,1)}, bf16[136,768]{1,0:T(8,128)(2,1)}, bf16[136,768]{1,0:T(8,128)(2,1)}, f32[8,384]{1,0:T(8,128)}) custom-call(s32[2]{0:T(128)} %pad_add_fusion.at, bf16[512,640]{1,0:T(8,128)(2,1)} %get-tuple-element.73.gp, f32[8,640]{1,0:T(8,128)} %copy-done.19, ...), custom_call_target="tpu_custom_call" | custom-call | flops 100000000 | bytes 3635200 | tf_op jit(solution)/shard_map/pallas_call | solution.py:38
  158.7 2.1 %collective-permute-start.19 = (bf16[136,768]{1,0:T(8,128)(2,1)}, bf16[136,768]{1,0:T(8,128)(2,1)S(1)}, u32[]{:S(2)}, u32[]{:S(2)}) collective-permute-start(bf16[136,768]{1,0:T(8,128)(2,1)} %get-tuple-element.83), channel_id=1, source_target_pairs={{0,64},{32,96},{64,0},{96,32},{128,192},{160,224},{192,128},{224,1... | collective-permute-start | bytes 626696 | tf_op jit(solution)/shard_map/ppermute | solution.py:383
  161.5 7.8 %collective-permute-done.18.got1 = bf16[136,768]{1,0:T(8,128)(2,1)S(1)} collective-permute-done((bf16[136,768]{1,0:T(8,128)(2,1)}, bf16[136,768]{1,0:T(8,128)(2,1)S(1)}, u32[]{:S(2)}, u32[]{:S(2)}) %collective-permute-start.18) | collective-permute-done | bytes 208928 | tf_op jit(solution)/shard_map/ppermute | solution.py:383
  171.5 1.3 shard_map.112
  (103 shorter events, 19.5 us)
Async XLA Ops:
  3.0 24.7 %all-to-all-start = ((bf16[16,24,640]{2,1,0:T(8,128)(2,1)}), bf16[16,24,640]{2,1,0:T(8,128)(2,1)S(1)}, u32[]{:S(2)}, u32[]{:S(2)}) async-start(bf16[16,24,640]{2,1,0:T(8,128)(2,1)} %get-tuple-element.49), calls=%async_computation | async-start | bytes 983040 | tf_op jit(solution)/shard_map/all_to_all | solution.py:392
  12.6 12.7 %collective-permute-start.9 = (bf16[12,768]{1,0:T(8,128)(2,1)S(1)}, bf16[12,768]{1,0:T(8,128)(2,1)S(1)}, u32[]{:S(2)}, u32[]{:S(2)}) collective-permute-start(bf16[12,768]{1,0:T(8,128)(2,1)S(1)} %constant_dynamic-slice_fusion), channel_id=1, source_target_pairs={{0,0},{1,4},{2,8},{3,12},{4,16},{5,20},{6,24},{7,28},{8,32},{9,36}... | collective-permute-start | bytes 55304 | tf_op jit(solution)/shard_map/ppermute | solution.py:423
  25.3 40.8 %copy-start.25 = (f32[24]{0:T(128)S(1)}, f32[24]{0:T(128)}, u32[]{:S(2)}) copy-start(f32[24]{0:T(128)} %param.14) | copy-start | bytes 292
  26.0 42.3 %slice-start = ((f32[4,1792]{1,0:T(4,128)}), f32[4,1536]{1,0:T(4,128)S(1)}, s32[]{:S(2)}) async-start(f32[4,1792]{1,0:T(4,128)} %param.13), calls=%async_computation.4 | async-start | bytes 49152 | tf_op jit(solution)/shard_map/slice | solution.py:428
  26.0 43.9 %copy-start.10 = (bf16[1,128,768]{2,1,0:T(8,128)(2,1)S(1)}, bf16[1,128,768]{2,1,0:T(8,128)(2,1)}, u32[]{:S(2)}) copy-start(bf16[1,128,768]{2,1,0:T(8,128)(2,1)} %param.9) | copy-start | bytes 589828
  26.0 52.8 %slice-start.1 = ((f32[4,1792]{1,0:T(4,128)}), f32[4,256]{1,0:T(4,128)S(1)}, s32[]{:S(2)}) async-start(f32[4,1792]{1,0:T(4,128)} %param.13), calls=%async_computation.5 | async-start | bytes 8192 | tf_op jit(solution)/shard_map/slice | solution.py:428
  27.7 51.8 %copy-start.6 = (bf16[16,24,640]{2,1,0:T(8,128)(2,1)}, bf16[16,24,640]{2,1,0:T(8,128)(2,1)S(1)}, u32[]{:S(2)}) copy-start(bf16[16,24,640]{2,1,0:T(8,128)(2,1)S(1)} %all-to-all-done.same) | copy-start | bytes 1474564
  28.6 23.8 %all-to-all-start.1 = ((bf16[16,24,768]{2,1,0:T(8,128)(2,1)}), bf16[16,24,768]{2,1,0:T(8,128)(2,1)S(1)}, u32[]{:S(2)}, u32[]{:S(2)}) async-start(bf16[16,24,768]{2,1,0:T(8,128)(2,1)} %broadcast_in_dim.35), calls=%async_computation.1 | async-start | bytes 1179648 | tf_op jit(solution)/shard_map/all_to_all | solution.py:392
  36.1 43.4 %collective-permute-start.4 = (bf16[16,24,640]{2,1,0:T(8,128)(2,1)S(1)}, bf16[16,24,640]{2,1,0:T(8,128)(2,1)}, u32[]{:S(2)}, u32[]{:S(2)}) collective-permute-start(bf16[16,24,640]{2,1,0:T(8,128)(2,1)S(1)} %all-to-all-done.same), channel_id=1, source_target_pairs={{0,1},{1,0},{2,3},{3,2},{4,5},{5,4},{6,7},{7,6},{8,9},{9,8},{10,11... | collective-permute-start | bytes 1474568 | tf_op jit(solution)/shard_map/ppermute | solution.py:393
  52.5 33.0 %copy-start.5 = (bf16[16,24,768]{2,1,0:T(8,128)(2,1)}, bf16[16,24,768]{2,1,0:T(8,128)(2,1)S(1)}, u32[]{:S(2)}) copy-start(bf16[16,24,768]{2,1,0:T(8,128)(2,1)S(1)} %all-to-all-done.1.same) | copy-start | bytes 1769476
  52.5 43.0 %collective-permute-start.10 = (bf16[16,24,768]{2,1,0:T(8,128)(2,1)S(1)}, bf16[16,24,768]{2,1,0:T(8,128)(2,1)S(1)}, u32[]{:S(2)}, u32[]{:S(2)}) collective-permute-start(bf16[16,24,768]{2,1,0:T(8,128)(2,1)S(1)} %all-to-all-done.1.same), channel_id=1, source_target_pairs={{0,1},{1,0},{2,3},{3,2},{4,5},{5,4},{6,7},{7,6},{8,9},{9,8},{10,11... | collective-permute-start | bytes 1769480 | tf_op jit(solution)/shard_map/ppermute | solution.py:393
  53.2 0.7 collective-permute-start
  56.5 13.5 %collective-permute-start.1 = (bf16[136,768]{1,0:T(8,128)(2,1)}, bf16[136,768]{1,0:T(8,128)(2,1)S(1)}, u32[]{:S(2)}, u32[]{:S(2)}) collective-permute-start(bf16[136,768]{1,0:T(8,128)(2,1)} %get-tuple-element.46), channel_id=1, source_target_pairs={{0,32},{32,64},{64,96},{96,0},{128,160},{160,192},{192,224},{224,1... | collective-permute-start | bytes 626696 | tf_op jit(solution)/shard_map/ppermute | solution.py:383
  57.8 19.0 %collective-permute-start.2 = (bf16[136,768]{1,0:T(8,128)(2,1)}, bf16[136,768]{1,0:T(8,128)(2,1)S(1)}, u32[]{:S(2)}, u32[]{:S(2)}) collective-permute-start(bf16[136,768]{1,0:T(8,128)(2,1)} %get-tuple-element.47), channel_id=1, source_target_pairs={{0,64},{32,96},{64,0},{96,32},{128,192},{160,224},{192,128},{224,1... | collective-permute-start | bytes 626696 | tf_op jit(solution)/shard_map/ppermute | solution.py:383
  66.1 10.7 %collective-permute-start.3 = (bf16[136,768]{1,0:T(8,128)(2,1)}, bf16[136,768]{1,0:T(8,128)(2,1)S(1)}, u32[]{:S(2)}, u32[]{:S(2)}) collective-permute-start(bf16[136,768]{1,0:T(8,128)(2,1)} %get-tuple-element.48), channel_id=1, source_target_pairs={{0,96},{32,0},{64,32},{96,64},{128,224},{160,128},{192,160},{224,1... | collective-permute-start | bytes 626696 | tf_op jit(solution)/shard_map/ppermute | solution.py:383
  70.0 25.4 %collective-permute-start.6 = (bf16[128,768]{1,0:T(8,128)(2,1)S(1)}, bf16[128,768]{1,0:T(8,128)(2,1)S(1)}, u32[]{:S(2)}, u32[]{:S(2)}) collective-permute-start(bf16[128,768]{1,0:T(8,128)(2,1)S(1)} %bitcast.16), channel_id=1, source_target_pairs={{0,32},{32,64},{64,96},{96,0},{128,160},{160,192},{192,224},{224,1... | collective-permute-start | bytes 589832 | tf_op jit(solution)/shard_map/ppermute | solution.py:383
  76.8 18.6 %collective-permute-start.7 = (bf16[128,768]{1,0:T(8,128)(2,1)S(1)}, bf16[128,768]{1,0:T(8,128)(2,1)S(1)}, u32[]{:S(2)}, u32[]{:S(2)}) collective-permute-start(bf16[128,768]{1,0:T(8,128)(2,1)S(1)} %bitcast.17), channel_id=1, source_target_pairs={{0,64},{32,96},{64,0},{96,32},{128,192},{160,224},{192,128},{224,1... | collective-permute-start | bytes 589832 | tf_op jit(solution)/shard_map/ppermute | solution.py:383
  76.8 18.6 %collective-permute-start.8 = (bf16[128,768]{1,0:T(8,128)(2,1)S(1)}, bf16[128,768]{1,0:T(8,128)(2,1)S(1)}, u32[]{:S(2)}, u32[]{:S(2)}) collective-permute-start(bf16[128,768]{1,0:T(8,128)(2,1)S(1)} %bitcast.18), channel_id=1, source_target_pairs={{0,96},{32,0},{64,32},{96,64},{128,224},{160,128},{192,160},{224,1... | collective-permute-start | bytes 589832 | tf_op jit(solution)/shard_map/ppermute | solution.py:383
  85.5 10.0 %collective-permute-start.5 = (bf16[128,384]{1,0:T(8,128)(2,1)}, bf16[128,384]{1,0:T(8,128)(2,1)S(1)}, u32[]{:S(2)}, u32[]{:S(2)}) collective-permute-start(bf16[128,384]{1,0:T(8,128)(2,1)} %get-tuple-element.53), channel_id=1, source_target_pairs={{0,128},{32,160},{64,192},{96,224},{1,129},{33,161},{65,193},{97,2... | collective-permute-start | bytes 294920 | tf_op jit(solution)/shard_map/ppermute | solution.py:450
  103.1 6.8 %collective-permute-start.11 = (f32[2,512]{1,0:T(2,128)}, f32[2,512]{1,0:T(2,128)S(1)}, u32[]{:S(2)}, u32[]{:S(2)}) collective-permute-start(f32[2,512]{1,0:T(2,128)} %get-tuple-element.60.stats0), channel_id=1, source_target_pairs={{0,32},{32,64},{64,96},{96,0},{128,160},{160,192},{192,224},{224,1... | collective-permute-start | bytes 12296 | tf_op jit(solution)/shard_map/ppermute | solution.py:383
  104.0 5.9 %collective-permute-start.12 = (f32[2,512]{1,0:T(2,128)}, f32[2,512]{1,0:T(2,128)S(1)}, u32[]{:S(2)}, u32[]{:S(2)}) collective-permute-start(f32[2,512]{1,0:T(2,128)} %get-tuple-element.60.stats0), channel_id=1, source_target_pairs={{0,64},{32,96},{64,0},{96,32},{128,192},{160,224},{192,128},{224,1... | collective-permute-start | bytes 12296 | tf_op jit(solution)/shard_map/ppermute | solution.py:383
  106.1 4.1 %collective-permute-start.13 = (f32[2,512]{1,0:T(2,128)}, f32[2,512]{1,0:T(2,128)S(1)}, u32[]{:S(2)}, u32[]{:S(2)}) collective-permute-start(f32[2,512]{1,0:T(2,128)} %get-tuple-element.60.stats0), channel_id=1, source_target_pairs={{0,96},{32,0},{64,32},{96,64},{128,224},{160,128},{192,160},{224,1... | collective-permute-start | bytes 12296 | tf_op jit(solution)/shard_map/ppermute | solution.py:383
  116.3 4.9 %collective-permute-start.16 = (bf16[384,384]{1,0:T(8,128)(2,1)}, bf16[384,384]{1,0:T(8,128)(2,1)S(1)}, u32[]{:S(2)}, u32[]{:S(2)}) collective-permute-start(bf16[384,384]{1,0:T(8,128)(2,1)} %get-tuple-element.79), channel_id=1, source_target_pairs={{0,1},{1,0},{2,3},{3,2},{4,5},{5,4},{6,7},{7,6},{8,9},{9,8},{10,11... | collective-permute-start | bytes 884744 | tf_op jit(solution)/shard_map/ppermute | solution.py:475
  116.4 17.7 %all-to-all-start.2 = ((bf16[4,128,768]{2,1,0:T(8,128)(2,1)}), bf16[4,128,768]{2,1,0:T(8,128)(2,1)S(1)}, u32[]{:S(2)}, u32[]{:S(2)}) async-start(bf16[4,128,768]{2,1,0:T(8,128)(2,1)} %get-tuple-element.70), calls=%async_computation.2 | async-start | bytes 1572864 | tf_op jit(solution)/shard_map/all_to_all | solution.py:386
  121.2 17.6 %copy-start.23 = (bf16[128,384]{1,0:T(8,128)(2,1)S(1)}, bf16[128,384]{1,0:T(8,128)(2,1)}, u32[]{:S(2)}) copy-start(bf16[128,384]{1,0:T(8,128)(2,1)} %get-tuple-element.62) | copy-start | bytes 294916
  121.3 7.5 %collective-permute-start.17 = (bf16[192,384]{1,0:T(8,128)(2,1)S(1)}, bf16[192,384]{1,0:T(8,128)(2,1)S(1)}, u32[]{:S(2)}, u32[]{:S(2)}) collective-permute-start(bf16[192,384]{1,0:T(8,128)(2,1)S(1)} %slice.28), channel_id=1, source_target_pairs={{0,128},{32,160},{64,192},{96,224},{128,0},{160,32},{192,64},{224,... | collective-permute-start | bytes 442376 | tf_op jit(solution)/shard_map/ppermute | solution.py:478
  134.1 18.0 %all-to-all-start.3 = ((bf16[16,12,384]{2,1,0:T(8,128)(2,1)}), bf16[16,12,384]{2,1,0:T(8,128)(2,1)S(1)}, u32[]{:S(2)}, u32[]{:S(2)}) async-start(bf16[16,12,384]{2,1,0:T(8,128)(2,1)} %reshape.93), calls=%async_computation.3 | async-start | bytes 393216 | tf_op jit(solution)/shard_map/all_to_all | solution.py:486
  138.8 8.3 %collective-permute-start.14 = (bf16[128,384]{1,0:T(8,128)(2,1)S(1)}, bf16[128,384]{1,0:T(8,128)(2,1)S(1)}, u32[]{:S(2)}, u32[]{:S(2)}) collective-permute-start(bf16[128,384]{1,0:T(8,128)(2,1)S(1)} %copy-done.23), channel_id=1, source_target_pairs={{128,0},{160,32},{192,64},{224,96},{129,1},{161,33},{193,65},{225,... | collective-permute-start | bytes 294920 | tf_op jit(solution)/shard_map/ppermute | solution.py:474
  144.7 7.4 %collective-permute-start.15 = (f32[8,640]{1,0:T(8,128)}, f32[8,640]{1,0:T(8,128)S(1)}, u32[]{:S(2)}, u32[]{:S(2)}) collective-permute-start(f32[8,640]{1,0:T(8,128)} %get-tuple-element.74), channel_id=1, source_target_pairs={{128,0},{160,32},{192,64},{224,96},{129,1},{161,33},{193,65},{225,... | collective-permute-start | bytes 61448 | tf_op jit(solution)/shard_map/ppermute | solution.py:484
  158.1 11.1 %collective-permute-start.18 = (bf16[136,768]{1,0:T(8,128)(2,1)}, bf16[136,768]{1,0:T(8,128)(2,1)S(1)}, u32[]{:S(2)}, u32[]{:S(2)}) collective-permute-start(bf16[136,768]{1,0:T(8,128)(2,1)} %get-tuple-element.82), channel_id=1, source_target_pairs={{0,32},{32,64},{64,96},{96,0},{128,160},{160,192},{192,224},{224,1... | collective-permute-start | bytes 626696 | tf_op jit(solution)/shard_map/ppermute | solution.py:383
  158.7 10.6 %collective-permute-start.19 = (bf16[136,768]{1,0:T(8,128)(2,1)}, bf16[136,768]{1,0:T(8,128)(2,1)S(1)}, u32[]{:S(2)}, u32[]{:S(2)}) collective-permute-start(bf16[136,768]{1,0:T(8,128)(2,1)} %get-tuple-element.83), channel_id=1, source_target_pairs={{0,64},{32,96},{64,0},{96,32},{128,192},{160,224},{192,128},{224,1... | collective-permute-start | bytes 626696 | tf_op jit(solution)/shard_map/ppermute | solution.py:383
  160.8 9.1 %collective-permute-start.20 = (bf16[136,768]{1,0:T(8,128)(2,1)}, bf16[136,768]{1,0:T(8,128)(2,1)S(1)}, u32[]{:S(2)}, u32[]{:S(2)}) collective-permute-start(bf16[136,768]{1,0:T(8,128)(2,1)} %get-tuple-element.84), channel_id=1, source_target_pairs={{0,96},{32,0},{64,32},{96,64},{128,224},{160,128},{192,160},{224,1... | collective-permute-start | bytes 626696 | tf_op jit(solution)/shard_map/ppermute | solution.py:383
  (21 other events, 69.3 us)
